TPU v7x, 256 devices: a whole 4x4x8 slice. The times are simulated.
256 devices in a mesh: rows: 32 (over z_lo, x, core), sub: 8 (over y, z_hi).
Axes of the slice: x: 4, y: 4, z: 8 (z_hi: 2, z_lo: 4; z = z_hi * 4 + z_lo), core: 2. Of those that a mesh axis runs over, the one named last changes fastest.
Arguments:
- embeddings: bfloat16 [16384, 1024], P('rows', 'sub'), may hold values from -40 to 40
- rotation: bfloat16 [1024, 1024], P(None, 'sub'), may hold values from -0.1875 to 0.1875
- codebooks: float32 [64, 16, 256], P('sub'), may hold values from -6 to 6
Outputs:
- new_codebooks: float32 [64, 16, 256], P('sub')
- new_rotation: float32 [1024, 1024], P('rows', 'sub')
All inputs are finite; a program needn't handle non-finite values.
Results may differ from a plain program's by a relative error of at most 0.006.
The roundings to bfloat16 on the way count: a program that leaves them out, or rounds other values in their place, can miss the bound.
Values may be sent and summed in bfloat16 or wider, within the bound.
No kernel may reach another device: no remote copies, remote signals or barrier semaphores. Data moves between devices by JAX's collectives and lax.ppermute only.
A program may use at most 64 MiB of HBM per device.

v0:
```python
import jax
import jax.numpy as jnp
from jax import lax
from jax.sharding import PartitionSpec as P

SUB_DIM = 16
ITERS = 2
POLAR_ITER_COUNT = 2


softness_level = 4.0
prior_weight = 8.0
quintic_one = 3.4445
quintic_three = -4.775
quintic_five = 2.0315


def complete_feature_rows(embeddings):
    return lax.all_gather(embeddings, "sub", axis=1, tiled=True)


def subspace_pass(pieces, centroid_tables):
    books_low = centroid_tables.astype(jnp.bfloat16)

    def per_subspace(inputs):
        features, assignment_probs, codes_low = inputs
        cross_products = lax.dot_general(
            codes_low, features, (((0,), (0,)), ((), ())), preferred_element_type=jnp.float32
        )
        centroid_logits = (
            2.0 * cross_products - jnp.sum(assignment_probs * assignment_probs, axis=0)[:, None]
        ) / softness_level
        centroid_logits = centroid_logits - jnp.max(centroid_logits, axis=0, keepdims=True)
        exponent = jnp.exp(centroid_logits)
        weights = (exponent / jnp.sum(exponent, axis=0, keepdims=True)).astype(jnp.bfloat16)
        counts = jnp.sum(weights, axis=1, dtype=jnp.float32)
        totals = lax.dot_general(
            features, weights, (((1,), (1,)), ((), ())), preferred_element_type=jnp.float32
        )
        return (counts, totals, weights)

    return lax.map(per_subspace, (pieces, centroid_tables, books_low))


def per_device(embeddings, rotation, codebooks):
    row_count = embeddings.shape[0]
    width_own = rotation.shape[1]
    local_subs = codebooks.shape[0]
    full_x = complete_feature_rows(embeddings)
    rotated = lax.dot_general(
        rotation, full_x, (((0,), (1,)), ((), ())), preferred_element_type=jnp.float32
    ).astype(jnp.bfloat16)
    pieces = rotated.reshape(local_subs, SUB_DIM, row_count)
    books_now = codebooks
    weights = None
    for repeat in range(ITERS):
        counts, totals, weights = subspace_pass(pieces, books_now)
        totals, counts = lax.psum((totals, counts), "rows")
        books_now = (totals + prior_weight * books_now) / (counts[:, None, :] + prior_weight)
    books_low = books_now.astype(jnp.bfloat16)
    rebuilt = jnp.einsum("mdk,mkr->mdr", books_low, weights, preferred_element_type=jnp.float32)
    rebuilt = rebuilt.reshape(width_own, row_count).astype(jnp.bfloat16)
    row_share = full_x.shape[1] // lax.axis_size("rows")
    partial_value = lax.dot_general(
        full_x, rebuilt, (((0,), (1,)), ((), ())), preferred_element_type=jnp.float32
    )
    summed = lax.psum(partial_value, "rows")
    own_cross = lax.dynamic_slice_in_dim(summed, lax.axis_index("rows") * row_share, row_share, 0)
    frob_norm = jnp.sqrt(lax.psum(jnp.sum(own_cross * own_cross), ("rows", "sub")) + 1e-06)
    polar_now = own_cross / frob_norm
    for polar_rotation_step in range(POLAR_ITER_COUNT):
        columns = lax.all_gather(polar_now, "rows", axis=0, tiled=True)
        gram_part = lax.dot_general(
            polar_now,
            columns,
            (((1,), (1,)), ((), ())),
            precision=lax.Precision.HIGHEST,
            preferred_element_type=jnp.float32,
        )
        gram_rows = lax.psum(gram_part, "sub")
        image = jnp.dot(
            gram_rows, columns, precision=lax.Precision.HIGHEST, preferred_element_type=jnp.float32
        )
        image_cols = lax.all_gather(image, "rows", axis=0, tiled=True)
        second = jnp.dot(
            gram_rows,
            image_cols,
            precision=lax.Precision.HIGHEST,
            preferred_element_type=jnp.float32,
        )
        polar_now = quintic_one * polar_now + quintic_three * image + quintic_five * second
    return (books_now, polar_now)


def solution(mesh):
    return jax.shard_map(
        per_device,
        mesh=mesh,
        in_specs=(P("rows", "sub"), P(None, "sub"), P("sub", None, None)),
        out_specs=(P("sub", None, None), P("rows", "sub")),
        check_vma=False,
    )
```

profile of v0, /device:TPU:1, one launch (start us, length us, event | category | flops | bytes accessed | tf_op | source)
XLA Modules:
  0.0 1482.6 jit_solution(5863832114635413068)
XLA Ops:
  8.9 65.7 %all-gather.2.cloned.1.call-done = bf16[512,1024]{1,0:T(8,128)(2,1)} async-done(((bf16[512,128]{1,0:T(8,128)(2,1)}), bf16[512,1024]{1,0:T(8,128)(2,1)}) %all-gather.2.cloned.1.call-update) | async-done | bytes 1048592 | tf_op jit(solution)/shard_map/all_gather | solution.py:19
  74.6 1.7 convolution_convert_fusion.1
  76.4 12.3 while.26
  88.7 69.8 %psum.57 = f32[8,256]{1,0:T(8,128)S(1)} all-reduce(f32[8,256]{1,0:T(8,128)S(1)} %get-tuple-element.75), channel_id=1, replica_groups=mesh['rows'=32,'sub'=8] {'rows'}, use_global_device_ids=true, to_apply=%region_7.8 | all-reduce | flops 2048 | bytes 16384 | tf_op jit(solution)/shard_map/psum | solution.py:58
  158.6 247.6 %all-reduce.6.cloned.1.call-done = f32[8,16,256]{2,1,0:T(8,128)} async-done(((f32[8,16,256]{2,1,0:T(8,128)}), f32[8,16,256]{2,1,0:T(8,128)}) %all-reduce.6.cloned.1.call-update) | async-done | bytes 131088 | tf_op jit(solution)/shard_map/psum | solution.py:58
  407.8 11.8 while.27
  419.6 70.0 %psum.59 = f32[8,256]{1,0:T(8,128)S(1)} all-reduce(f32[8,256]{1,0:T(8,128)S(1)} %get-tuple-element.77), channel_id=1, replica_groups=mesh['rows'=32,'sub'=8] {'rows'}, use_global_device_ids=true, to_apply=%region_15.16 | all-reduce | flops 2048 | bytes 16384 | tf_op jit(solution)/shard_map/psum | solution.py:58
  489.7 252.1 %all-reduce.8.cloned.1.call-done = f32[8,16,256]{2,1,0:T(8,128)} async-done(((f32[8,16,256]{2,1,0:T(8,128)}), f32[8,16,256]{2,1,0:T(8,128)}) %all-reduce.8.cloned.1.call-update) | async-done | bytes 131088 | tf_op jit(solution)/shard_map/psum | solution.py:58
  743.4 1.4 convolution_bitcast_fusion.2
  744.8 275.9 %all-reduce.10.cloned.1.call-done = f32[1024,128]{1,0:T(8,128)} async-done(((f32[1024,128]{1,0:T(8,128)}), f32[1024,128]{1,0:T(8,128)}) %all-reduce.10.cloned.1.call-update) | async-done | bytes 524304 | tf_op jit(solution)/shard_map/psum | solution.py:67
  1020.8 1.3 multiply_reduce_fusion.2
  1022.1 78.1 %psum.61 = f32[]{:T(128)} all-reduce(f32[]{:T(128)} %multiply_reduce_fusion.2), channel_id=1, replica_groups=mesh['rows'=32,'sub'=8] {'rows','sub'}, use_global_device_ids=true, to_apply=%region_18.19 | all-reduce | flops 1 | bytes 8 | tf_op jit(solution)/shard_map/psum | solution.py:69
  1101.6 39.9 %all_gather.16 = f32[1024,128]{1,0:T(8,128)S(1)} all-gather(f32[32,128]{1,0:T(8,128)S(1)} %dynamic-slice_divide_fusion), channel_id=1, replica_groups=mesh['rows'=32,'sub'=8] {'rows'}, dimensions={0}, use_global_device_ids=true | all-gather | bytes 540672 | tf_op jit(solution)/shard_map/all_gather | solution.py:72
  1141.5 1.3 fusion.30
  1142.8 95.5 %all-reduce.12.cloned.1.call-done = f32[32,1024]{1,0:T(8,128)} async-done(((f32[32,1024]{1,0:T(8,128)}), f32[32,1024]{1,0:T(8,128)}) %all-reduce.12.cloned.1.call-update) | async-done | bytes 131088 | tf_op jit(solution)/shard_map/psum | solution.py:80
  1238.3 1.3 fusion.31
  1239.6 47.8 %all_gather.17 = f32[1024,128]{1,0:T(8,128)S(1)} all-gather(f32[32,128]{1,0:T(8,128)S(1)} %fusion.31), channel_id=1, replica_groups=mesh['rows'=32,'sub'=8] {'rows'}, dimensions={0}, use_global_device_ids=true | all-gather | bytes 540672 | tf_op jit(solution)/shard_map/all_gather | solution.py:84
  1287.5 1.3 fusion.25
  1288.8 39.3 %all_gather.18 = f32[1024,128]{1,0:T(8,128)S(1)} all-gather(f32[32,128]{1,0:T(8,128)S(1)} %fusion.25), channel_id=1, replica_groups=mesh['rows'=32,'sub'=8] {'rows'}, dimensions={0}, use_global_device_ids=true | all-gather | bytes 540672 | tf_op jit(solution)/shard_map/all_gather | solution.py:72
  1328.1 1.3 fusion.32
  1329.3 95.4 %all-reduce.14.cloned.1.call-done = f32[32,1024]{1,0:T(8,128)} async-done(((f32[32,1024]{1,0:T(8,128)}), f32[32,1024]{1,0:T(8,128)}) %all-reduce.14.cloned.1.call-update) | async-done | bytes 131088 | tf_op jit(solution)/shard_map/psum | solution.py:80
  1424.7 1.3 fusion.33
  1426.0 47.8 %all_gather.19 = f32[1024,128]{1,0:T(8,128)S(1)} all-gather(f32[32,128]{1,0:T(8,128)S(1)} %fusion.33), channel_id=1, replica_groups=mesh['rows'=32,'sub'=8] {'rows'}, dimensions={0}, use_global_device_ids=true | all-gather | bytes 540672 | tf_op jit(solution)/shard_map/all_gather | solution.py:84
  1473.9 1.9 fusion.24
  (136 shorter events, 29.5 us)
Async XLA Ops:
  7.2 67.5 %copy-start = (bf16[1024,128]{1,0:T(8,128)(2,1)S(1)}, bf16[1024,128]{1,0:T(8,128)(2,1)}, u32[]{:S(2)}) copy-start(bf16[1024,128]{1,0:T(8,128)(2,1)} %param.8) | copy-start | bytes 786436
  7.2 67.5 %all-gather.2.cloned.1.call-start = ((), (), s32[]{:S(2)}) async-start(), calls=%async_computation | async-start | bytes 1179648 | tf_op jit(solution)/shard_map/all_gather | solution.py:19
  7.9 398.2 %all-reduce.6.cloned.1.call-start = ((), (), s32[]{:S(2)}) async-start(), calls=%async_computation.1 | async-start | bytes 262144 | tf_op jit(solution)/shard_map/psum | solution.py:58
  88.7 69.8 %copy-start.3 = (f32[8,16,256]{2,1,0:T(8,128)}, f32[8,16,256]{2,1,0:T(8,128)S(1)}, u32[]{:S(2)}) copy-start(f32[8,16,256]{2,1,0:T(8,128)S(1)} %get-tuple-element.74) | copy-start | bytes 393220
  158.5 583.3 %all-reduce.8.cloned.1.call-start = ((), (), s32[]{:S(2)}) async-start(), calls=%async_computation.2 | async-start | bytes 262144 | tf_op jit(solution)/shard_map/psum | solution.py:58
  419.6 323.8 %copy-start.1 = (bf16[512,1024]{1,0:T(8,128)(2,1)S(1)}, bf16[512,1024]{1,0:T(8,128)(2,1)}, u32[]{:S(2)}) copy-start(bf16[512,1024]{1,0:T(8,128)(2,1)} %all-gather.2.cloned.1.call-done) | copy-start | bytes 3145732
  489.7 531.1 %all-reduce.10.cloned.1.call-start = ((), (), s32[]{:S(2)}) async-start(), calls=%async_computation.3 | async-start | bytes 1048576 | tf_op jit(solution)/shard_map/psum | solution.py:67
  742.7 0.7 copy-start.2
  744.8 493.5 %all-reduce.12.cloned.1.call-start = ((), (), s32[]{:S(2)}) async-start(), calls=%async_computation.4 | async-start | bytes 262144 | tf_op jit(solution)/shard_map/psum | solution.py:80
  1142.8 282.0 %all-reduce.14.cloned.1.call-start = ((), (), s32[]{:S(2)}) async-start(), calls=%async_computation.5 | async-start | bytes 262144 | tf_op jit(solution)/shard_map/psum | solution.py:80
Sparse Core Ops, SparseCore 0:
  10.5 64.1 all-gather.1
  158.6 247.4 all-reduce.5
  489.8 251.9 all-reduce.7
  744.9 275.8 all-reduce.9
  1142.9 95.3 all-reduce.11
  1329.5 95.2 all-reduce.13
where the time goes:
time: 1480 us
  waiting for transfers between devices  1030 us (70%)
  blocking collectives  393 us (27%)
  matrix products  23.6 us (2%)
  other arithmetic  15.8 us (1%)
  between operations  15 us (1%)
    psum x2, waiting for transfers between devices, per_device(): totals, counts = lax.psum((totals, counts), 'rows')  500 us
    psum x1, waiting for transfers between devices, per_device(): summed = lax.psum(partial_value, 'rows')  276 us
    psum x2, waiting for transfers between devices, per_device(): gram_rows = lax.psum(gram_part, 'sub')  191 us
    psum x2, blocking collectives, per_device(): totals, counts = lax.psum((totals, counts), 'rows')  140 us
    all_gather x2, blocking collectives, per_device(): image_cols = lax.all_gather(image, 'rows', axis=0, tiled=True)  95.7 us
    all_gather x2, blocking collectives, per_device(): columns = lax.all_gather(polar_now, 'rows', axis=0, tiled=True)  79.2 us
    psum x1, blocking collectives, per_device(): lax.psum(jnp.sum(own_cross * own_cross), ('rows', 'sub')) + 1e-06  78.1 us
    all_gather x1, waiting for transfers between devices, complete_feature_rows(): return lax.all_gather(embeddings, 'sub', axis=1, tiled=True)  65.7 us
  transfers between devices with their start and end apart: 6, of which 6 were waited for; matrix products, arithmetic and copies ran while one was open for 0% of the time, Pallas kernels for 0%

commit v1 on v0

v1 whole, which is shorter than its diff:
```python
import jax
import jax.numpy as jnp
from jax import lax
from jax.experimental import pallas as pl
from jax.experimental.pallas import tpu as pltpu
from jax.sharding import PartitionSpec as P

SUB_DIM = 16
CODES = 256
SOFTNESS = 4.0
PRIOR = 8.0
Q1, Q3, Q5 = 3.4445, -4.775, 2.0315

ROW_DEVS = 32
SUB_DEVS = 8
CHIPS = [[8 * z + 2 * x + c for z in range(4) for x in range(4)] for c in range(2)]

f32 = jnp.float32
bf16 = jnp.bfloat16
VMEM_LIMIT = 48 * 1024 * 1024


def call(kernel, out_shape, n_scalars, n_arrays, scratch=()):
    return pl.pallas_call(
        kernel,
        out_shape=out_shape,
        in_specs=[pl.BlockSpec(memory_space=pltpu.SMEM)] * n_scalars
        + [pl.BlockSpec(memory_space=pltpu.VMEM)] * n_arrays,
        scratch_shapes=list(scratch),
        compiler_params=pltpu.CompilerParams(vmem_limit_bytes=VMEM_LIMIT),
    )


def shape(dims, dtype):
    return jax.ShapeDtypeStruct(dims, dtype)


def dot(a, b, dims=((1,), (0,)), precision=None):
    return lax.dot_general(a, b, (dims, ((), ())), precision=precision, preferred_element_type=f32)


def permute_rows(x, to):
    return lax.ppermute(x, "rows", [(i, to(i)) for i in range(ROW_DEVS)])


def other_core(x):
    return permute_rows(x, lambda i: i ^ 1)


def gather_by_exchange(x, axis, count, groups=None):
    copies = jnp.broadcast_to(x[None], (count,) + x.shape)
    return lax.all_to_all(copies, axis, 0, 0, tiled=True, axis_index_groups=groups)


def rotate_kernel(core_ref, e_ref, r_ref, keep_ref, send_ref):
    full = jnp.concatenate([e_ref[s] for s in range(SUB_DEVS)], axis=1)
    rot = dot(full, r_ref[...]).T.astype(bf16)
    half = rot.shape[0] // 2
    first = core_ref[0] == 0
    keep_ref[...] = jnp.where(first, rot[:half], rot[half:])
    send_ref[...] = jnp.where(first, rot[half:], rot[:half])


def assign(book, feats):
    sq = 0.25 * jnp.sum(book * book, axis=0, keepdims=True)
    sq_a = sq.astype(bf16).astype(f32)
    sq_b = (sq - sq_a).astype(bf16).astype(f32)
    sq_c = (sq - sq_a) - sq_b
    low = book.astype(bf16).astype(f32)
    pad = jnp.zeros((SUB_DIM - 3, book.shape[1]), f32)
    lhs = jnp.concatenate([0.5 * low, -sq_a, -sq_b, -sq_c, pad], axis=0).T.astype(bf16)
    rhs = jnp.concatenate([feats, jnp.ones_like(feats)], axis=0)
    logits = dot(lhs, rhs)
    e = jnp.exp(logits - jnp.max(logits, axis=0, keepdims=True))
    w = (e * (1.0 / jnp.sum(e, axis=0, keepdims=True))).astype(bf16)
    stats = dot(rhs, w, ((1,), (1,)))
    return w, stats


def write_stats(stats_ref, m, n_sub, stats):
    stats_ref[SUB_DIM * m : SUB_DIM * (m + 1)] = stats[:SUB_DIM]
    stats_ref[SUB_DIM * n_sub + m : SUB_DIM * n_sub + m + 1] = stats[SUB_DIM : SUB_DIM + 1]


def first_kernel(core_ref, keep_ref, recv_ref, book_ref, stats_ref):
    n_sub = keep_ref.shape[0] // SUB_DIM
    feats = jnp.concatenate([keep_ref[...], recv_ref[...]], axis=1)
    stats_ref[...] = jnp.zeros_like(stats_ref)
    for m in range(n_sub):
        _, stats = assign(book_ref[core_ref[0] * n_sub + m], feats[SUB_DIM * m : SUB_DIM * (m + 1)])
        write_stats(stats_ref, m, n_sub, stats)


def new_book(a, b, c, d, m, n_sub, book):
    rows = slice(SUB_DIM * m, SUB_DIM * (m + 1))
    row = slice(SUB_DIM * n_sub + m, SUB_DIM * n_sub + m + 1)
    totals = (a[rows] + b[rows]) + (c[rows] + d[rows])
    counts = (a[row] + b[row]) + (c[row] + d[row])
    return (totals + PRIOR * book) / (counts + PRIOR)


def second_kernel(core_ref, keep_ref, recv_ref, book_ref, a, b, c, d, book_out, w_ref, stats_ref):
    n_sub = keep_ref.shape[0] // SUB_DIM
    feats = jnp.concatenate([keep_ref[...], recv_ref[...]], axis=1)
    stats_ref[...] = jnp.zeros_like(stats_ref)
    for m in range(n_sub):
        book = new_book(a, b, c, d, m, n_sub, book_ref[core_ref[0] * n_sub + m])
        book_out[m] = book
        w, stats = assign(book, feats[SUB_DIM * m : SUB_DIM * (m + 1)])
        w_ref[m] = w
        write_stats(stats_ref, m, n_sub, stats)


def cross_kernel(a, b, c, d, book_ref, w_ref, own_ref, oth_ref, book_out, cross_ref):
    n_sub = w_ref.shape[0]
    parts = []
    for m in range(n_sub):
        book = new_book(a, b, c, d, m, n_sub, book_ref[m])
        book_out[m] = book
        parts.append(dot(book.astype(bf16), w_ref[m]).astype(bf16))
    rebuilt = jnp.concatenate(parts, axis=0)
    n = own_ref.shape[1]
    for p in range(SUB_DEVS // 2):
        mine = jnp.concatenate([own_ref[2 * p], own_ref[2 * p + 1]], axis=1)
        other = jnp.concatenate([oth_ref[2 * p], oth_ref[2 * p + 1]], axis=1)
        part = dot(rebuilt[:, :n], mine) + dot(rebuilt[:, n:], other)
        h, q = divmod(p, 2)
        for t in range(part.shape[0] // 8):
            cross_ref[2 * t + h, :, 256 * q : 256 * (q + 1)] = part[8 * t : 8 * (t + 1)]


def sum_kernel(x_ref, out_ref):
    total = x_ref[0]
    for i in range(1, x_ref.shape[0]):
        total = total + x_ref[i]
    for i in range(out_ref.shape[0]):
        out_ref[i] = total


def columns_kernel(x_ref, v_ref, low_ref):
    for t in range(x_ref.shape[0] // 2):
        v_ref[8 * t : 8 * (t + 1)] = jnp.concatenate([x_ref[2 * t], x_ref[2 * t + 1]], axis=1)
    low = v_ref[...].astype(bf16)
    for i in range(SUB_DEVS):
        low_ref[i] = low


def polar_kernel(core_ref, base_ref, own_ref, oth_ref, vown_ref, voth_ref, out_ref, hi_ref, lo_ref):
    width = vown_ref.shape[1]
    gram = jnp.zeros((width, width), f32)
    for ref in (own_ref, oth_ref):
        cols = ref[...].reshape(-1, width)
        gram = gram + dot(cols, cols, ((0,), (0,)))
    eye = lax.broadcasted_iota(jnp.int32, (128, 128), 0) == lax.broadcasted_iota(jnp.int32, (128, 128), 1)
    diag = jnp.zeros((128, 128), f32)
    for i in range(0, width, 128):
        diag = diag + jnp.where(eye, gram[i : i + 128, i : i + 128], 0.0)
    square = jnp.sum(jnp.sum(diag, axis=0, keepdims=True), axis=1, keepdims=True) + 1e-06
    gram = gram * (1.0 / square)
    hi = gram.astype(bf16)
    hi_ref[...] = hi
    lo_ref[...] = (gram - hi.astype(f32)).astype(bf16)

    def times_gram(v):
        v_hi = v.astype(bf16)
        v_lo = (v - v_hi.astype(f32)).astype(bf16)
        n = v.shape[0]
        both = dot(jnp.concatenate([v_hi, v_lo], axis=0), hi_ref[...])
        return both[:n] + (both[n:] + dot(v_hi, lo_ref[...]))

    def quintic(v):
        image = times_gram(v)
        return Q1 * v + Q3 * image + Q5 * times_gram(image)

    def times_next_gram(v):
        return quintic(times_gram(quintic(v)))

    polar = jnp.concatenate([vown_ref[...], voth_ref[...]], axis=0) * (1.0 / jnp.sqrt(square))
    polar = quintic(polar)
    image = times_next_gram(polar)
    second = times_next_gram(image)
    polar = Q1 * polar + Q3 * image + Q5 * second
    n = out_ref.shape[0]
    pick = lax.broadcasted_iota(jnp.int32, (n, width), 1) == lax.broadcasted_iota(jnp.int32, (n, width), 0) + base_ref[0]
    out = dot(pick.astype(f32), polar, ((1,), (1,)), lax.Precision.HIGHEST)
    out_ref[...] = jnp.where(core_ref[0] == 0, out, pltpu.roll(out, out.shape[1] // 2, 1))


def sum_over_chips(stats):
    x = [permute_rows(stats, lambda i, d=d: i ^ (2 * d)) for d in (1, 2, 3)]
    stats = (stats + x[0]) + (x[1] + x[2])
    z = [permute_rows(stats, lambda i, d=d: i ^ (8 * d)) for d in (1, 2, 3)]
    return stats, z[0], z[1], z[2]


def per_device(embeddings, rotation, codebooks):
    n, _ = embeddings.shape
    width = rotation.shape[0]
    subs, _, codes = codebooks.shape
    n_sub = subs // 2
    half = n_sub * SUB_DIM
    row_index = lax.axis_index("rows")
    core = (row_index % 2).astype(jnp.int32)
    core_arr = core.reshape(1)
    base = (row_index * (width // ROW_DEVS)).astype(jnp.int32).reshape(1)

    e_own = gather_by_exchange(embeddings, "sub", SUB_DEVS)
    keep, send = call(rotate_kernel, (shape((half, n), bf16),) * 2, 1, 2)(core_arr, e_own, rotation)
    recv = other_core(send)
    e_oth = other_core(e_own)

    stats_shape = shape((half + 8, codes), f32)
    stats = call(first_kernel, stats_shape, 1, 3)(core_arr, keep, recv, codebooks)
    sums = sum_over_chips(stats)
    book, weights, stats = call(
        second_kernel,
        (shape((n_sub, SUB_DIM, codes), f32), shape((n_sub, codes, 2 * n), bf16), stats_shape),
        1,
        7,
    )(core_arr, keep, recv, codebooks, *sums)
    sums = sum_over_chips(stats)
    book, cross = call(
        cross_kernel,
        (shape((n_sub, SUB_DIM, codes), f32), shape((16, 8, width // 2), f32)),
        0,
        8,
    )(*sums, book, weights, e_own, e_oth)

    cross = lax.all_to_all(cross, "rows", 0, 0, tiled=True, axis_index_groups=CHIPS)
    copies = call(sum_kernel, shape(cross.shape, f32), 0, 1)(cross)
    cols = lax.all_to_all(copies, "rows", 0, 0, tiled=True, axis_index_groups=CHIPS)
    v_own, low = call(
        columns_kernel, (shape((half, width), f32), shape((SUB_DEVS, half, width), bf16)), 0, 1
    )(cols)
    v_oth = other_core(v_own)
    book_oth = other_core(book)
    c_own = lax.all_to_all(low, "sub", 0, 0, tiled=True)
    c_oth = other_core(c_own)
    new_rotation = call(
        polar_kernel,
        shape((width // ROW_DEVS, 2 * half), f32),
        2,
        4,
        (pltpu.VMEM((width, width), bf16), pltpu.VMEM((width, width), bf16)),
    )(core_arr, base, c_own, c_oth, v_own, v_oth)
    first = core == 0
    books = jnp.concatenate([jnp.where(first, book, book_oth), jnp.where(first, book_oth, book)], axis=0)
    return (books, new_rotation)


def solution(mesh):
    return jax.shard_map(
        per_device,
        mesh=mesh,
        in_specs=(P("rows", "sub"), P(None, "sub"), P("sub", None, None)),
        out_specs=(P("sub", None, None), P("rows", "sub")),
        check_vma=False,
    )
```

time: 1480 us -> 157 us (0.11)
  waiting for transfers between devices: 1030 us -> 19.3 us
  blocking collectives: 393 us -> 75.2 us
  starting transfers between devices: 0.24 us -> 37.8 us
  matrix products: 23.6 us -> 0 us
  Pallas kernels: 0 us -> 19.7 us
  other arithmetic: 15.8 us -> 0.72 us
    psum x5 -> x0, waiting for transfers between devices: 966 us -> none  [the longest x2 500 us: per_device(): totals, counts = lax.psum((totals, counts), 'rows')]
    psum x3 -> x0, blocking collectives: 218 us -> none  [the longest x2 140 us: per_device(): totals, counts = lax.psum((totals, counts), 'rows')]
    all_gather x4 -> x0, blocking collectives: 175 us -> none  [the longest x2 95.7 us: per_device(): image_cols = lax.all_gather(image, 'rows', axis=0, tiled=True)]
    all_to_all x0 -> x4, blocking collectives: none -> 75.2 us  [the longest x1 32.4 us: gather_by_exchange(): lax.all_to_all(copies, axis, 0, 0, tiled=True, axis_index_groups=groups)]
    all_gather x1 -> x0, waiting for transfers between devices: 65.7 us -> none  [complete_feature_rows(): return lax.all_gather(embeddings, 'sub', axis=1, tiled=True)]
    ppermute x0 -> x17, starting transfers between devices: none -> 37.8 us  [permute_rows(): return lax.ppermute(x, 'rows', [(i, to(i)) for i in range(ROW_DEVS)])]
    dot_general x41 -> x0, matrix products: 23.6 us -> none  [the longest x16 7.59 us: per_subspace(): lax.dot_general(features, weights, (((1,), (1,)), ((), ())), preferred_el...]
    pallas_call x0 -> x7, Pallas kernels: none -> 19.7 us  [the longest x1 14.6 us: per_device(): call(polar_kernel, shape((width // ROW_DEVS, 2 * half), f32), 2, 4, (pltp...]
  transfers between devices with their start and end apart: 6 -> 17, of which waited for: 6 -> 10; matrix products, arithmetic and copies ran while one was open for 0% -> 0% of each run, Pallas kernels for 0% -> 3%
where the time goes in v1:
time: 157 us; the launch traced here: 155 us
  blocking collectives  75.2 us (48%)
  starting transfers between devices  37.8 us (24%)
  Pallas kernels  19.7 us (13%)
  waiting for transfers between devices  19.3 us (12%)
    ppermute x17, starting transfers between devices, permute_rows(): return lax.ppermute(x, 'rows', [(i, to(i)) for i in range(ROW_DEVS)])  37.8 us
    all_to_all x1, blocking collectives, gather_by_exchange(): lax.all_to_all(copies, axis, 0, 0, tiled=True, axis_index_groups=groups)  32.4 us
    ppermute x17, waiting for transfers between devices, permute_rows(): return lax.ppermute(x, 'rows', [(i, to(i)) for i in range(ROW_DEVS)])  19.3 us
    all_to_all x1, blocking collectives, per_device(): c_own = lax.all_to_all(low, 'sub', 0, 0, tiled=True)  19.2 us
    pallas_call x1, Pallas kernels, per_device(): call(polar_kernel, shape((width // ROW_DEVS, 2 * half), f32), 2, 4, (pltp...  14.6 us
    all_to_all x1, blocking collectives, per_device(): lax.all_to_all(cross, 'rows', 0, 0, tiled=True, axis_index_groups=CHIPS)  12.2 us
    all_to_all x1, blocking collectives, per_device(): lax.all_to_all(copies, 'rows', 0, 0, tiled=True, axis_index_groups=CHIPS)  11.4 us
  transfers between devices with their start and end apart: 17, of which 10 were waited for; matrix products, arithmetic and copies ran while one was open for 0% of the time, Pallas kernels for 3%

profile of v1, /device:TPU:1, one launch (start us, length us, event | category | flops | bytes accessed | tf_op | source)
XLA Modules:
  0.0 154.5 jit_solution(12114009633196839123)
XLA Ops:
  1.7 32.4 %all_to_all.20.e_ref.own_ref = bf16[8,512,128]{2,1,0:T(8,128)(2,1)S(1)} all-to-all(bf16[8,512,128]{2,1,0:T(8,128)(2,1)S(1)} %broadcast_in_dim.2), channel_id=1, replica_groups=mesh['rows'=32,'sub'=8] {'sub'}, dimensions={0} | all-to-all | bytes 2097152 | tf_op jit(solution)/shard_map/all_to_all | solution.py:52
  34.1 2.0 %collective-permute-start.13 = (bf16[8,512,128]{2,1,0:T(8,128)(2,1)S(1)}, bf16[8,512,128]{2,1,0:T(8,128)(2,1)S(1)}, u32[]{:S(2)}, u32[]{:S(2)}) collective-permute-start(bf16[8,512,128]{2,1,0:T(8,128)(2,1)S(1)} %all_to_all.20.e_ref.own_ref), channel_id=1, source_target_pairs={{0,8},{8,0},{16,24},{24,16},{32,40},{40,32},{48,56},{56,48},{64,72... | collective-permute-start | bytes 3145736 | tf_op jit(solution)/shard_map/ppermute | solution.py:43
  36.7 1.8 %collective-permute-done.recv_ref = bf16[64,512]{1,0:T(8,128)(2,1)S(1)} collective-permute-done((bf16[64,512]{1,0:T(8,128)(2,1)S(1)}, bf16[64,512]{1,0:T(8,128)(2,1)S(1)}, u32[]{:S(2)}, u32[]{:S(2)}) %collective-permute-start) | collective-permute-done | bytes 65568 | tf_op jit(solution)/shard_map/ppermute | solution.py:43
  38.5 1.7 %shard_map.51 = f32[72,256]{1,0:T(8,128)S(1)} custom-call(s32[1]{0:T(128)} %bitcast.core_ref, bf16[64,512]{1,0:T(8,128)(2,1)S(1)} %get-tuple-element.11.keep_ref, bf16[64,512]{1,0:T(8,128)(2,1)S(1)} %collective-permute-done.recv_ref, f32[8,16,256]{2,1,0:T(8,128)S(1)} %copy-done), custom_call_target="tpu_custom_call" | custom-call | tf_op jit(solution)/shard_map/pallas_call | solution.py:213
  41.5 2.5 %collective-permute-start.2 = (f32[72,256]{1,0:T(8,128)S(1)}, f32[72,256]{1,0:T(8,128)S(1)}, u32[]{:S(2)}, u32[]{:S(2)}) collective-permute-start(f32[72,256]{1,0:T(8,128)S(1)} %shard_map.51), channel_id=1, source_target_pairs={{0,32},{8,40},{16,48},{24,56},{32,0},{40,8},{48,16},{56,24},{64,96... | collective-permute-start | bytes 221192 | tf_op jit(solution)/shard_map/ppermute | solution.py:43
  44.1 3.1 %collective-permute-done.2 = f32[72,256]{1,0:T(8,128)S(1)} collective-permute-done((f32[72,256]{1,0:T(8,128)S(1)}, f32[72,256]{1,0:T(8,128)S(1)}, u32[]{:S(2)}, u32[]{:S(2)}) %collective-permute-start.2) | collective-permute-done | bytes 73760 | tf_op jit(solution)/shard_map/ppermute | solution.py:43
  47.2 1.6 %collective-permute-done.3 = f32[72,256]{1,0:T(8,128)S(1)} collective-permute-done((f32[72,256]{1,0:T(8,128)S(1)}, f32[72,256]{1,0:T(8,128)S(1)}, u32[]{:S(2)}, u32[]{:S(2)}) %collective-permute-start.3) | collective-permute-done | bytes 73760 | tf_op jit(solution)/shard_map/ppermute | solution.py:43
  48.8 9.7 %collective-permute-start.4 = (f32[72,256]{1,0:T(8,128)S(1)}, f32[72,256]{1,0:T(8,128)S(1)}, u32[]{:S(2)}, u32[]{:S(2)}) collective-permute-start(f32[72,256]{1,0:T(8,128)S(1)} %add_add_fusion.1.a), channel_id=1, source_target_pairs={{0,64},{8,72},{16,80},{24,88},{32,96},{40,104},{48,112},{56,120},{... | collective-permute-start | bytes 221192 | tf_op jit(solution)/shard_map/ppermute | solution.py:43
  59.1 1.6 %collective-permute-start.6 = (f32[72,256]{1,0:T(8,128)S(1)}, f32[72,256]{1,0:T(8,128)S(1)}, u32[]{:S(2)}, u32[]{:S(2)}) collective-permute-start(f32[72,256]{1,0:T(8,128)S(1)} %add_add_fusion.1.a), channel_id=1, source_target_pairs={{0,192},{8,200},{16,208},{24,216},{32,224},{40,232},{48,240},{56,2... | collective-permute-start | bytes 221192 | tf_op jit(solution)/shard_map/ppermute | solution.py:43
  60.7 2.8 %collective-permute-done.5.c = f32[72,256]{1,0:T(8,128)S(1)} collective-permute-done((f32[72,256]{1,0:T(8,128)S(1)}, f32[72,256]{1,0:T(8,128)S(1)}, u32[]{:S(2)}, u32[]{:S(2)}) %collective-permute-start.5) | collective-permute-done | bytes 73760 | tf_op jit(solution)/shard_map/ppermute | solution.py:43
  63.6 1.4 collective-permute-done.6.d
  65.0 1.9 %shard_map.52 = (f32[4,16,256]{2,1,0:T(8,128)S(1)}, bf16[4,256,1024]{2,1,0:T(8,128)(2,1)S(1)}, f32[72,256]{1,0:T(8,128)S(1)}) custom-call(s32[1]{0:T(128)} %bitcast.core_ref, bf16[64,512]{1,0:T(8,128)(2,1)S(1)} %get-tuple-element.11.keep_ref, bf16[64,512]{1,0:T(8,128)(2,1)S(1)} %collective-permute-done.recv_ref, f32[8,16,256]{2,1,0:T(8,128)S(1)} %copy-done, ...), custom_call_target="tpu_custom_call" | custom-call | tf_op jit(solution)/shard_map/pallas_call | solution.py:215
  66.9 2.5 %collective-permute-start.8 = (f32[72,256]{1,0:T(8,128)S(1)}, f32[72,256]{1,0:T(8,128)S(1)}, u32[]{:S(2)}, u32[]{:S(2)}) collective-permute-start(f32[72,256]{1,0:T(8,128)S(1)} %get-tuple-element.13), channel_id=1, source_target_pairs={{0,32},{8,40},{16,48},{24,56},{32,0},{40,8},{48,16},{56,24},{64,96... | collective-permute-start | bytes 221192 | tf_op jit(solution)/shard_map/ppermute | solution.py:43
  69.4 1.4 collective-permute-start.9
  71.9 1.9 %collective-permute-done.9 = f32[72,256]{1,0:T(8,128)S(1)} collective-permute-done((f32[72,256]{1,0:T(8,128)S(1)}, f32[72,256]{1,0:T(8,128)S(1)}, u32[]{:S(2)}, u32[]{:S(2)}) %collective-permute-start.9) | collective-permute-done | bytes 73760 | tf_op jit(solution)/shard_map/ppermute | solution.py:43
  73.9 3.7 %collective-permute-start.10 = (f32[72,256]{1,0:T(8,128)S(1)}, f32[72,256]{1,0:T(8,128)S(1)}, u32[]{:S(2)}, u32[]{:S(2)}) collective-permute-start(f32[72,256]{1,0:T(8,128)S(1)} %add_add_fusion.a), channel_id=1, source_target_pairs={{0,64},{8,72},{16,80},{24,88},{32,96},{40,104},{48,112},{56,120},{... | collective-permute-start | bytes 221192 | tf_op jit(solution)/shard_map/ppermute | solution.py:43
  78.1 1.6 %collective-permute-start.12 = (f32[72,256]{1,0:T(8,128)S(1)}, f32[72,256]{1,0:T(8,128)S(1)}, u32[]{:S(2)}, u32[]{:S(2)}) collective-permute-start(f32[72,256]{1,0:T(8,128)S(1)} %add_add_fusion.a), channel_id=1, source_target_pairs={{0,192},{8,200},{16,208},{24,216},{32,224},{40,232},{48,240},{56,2... | collective-permute-start | bytes 221192 | tf_op jit(solution)/shard_map/ppermute | solution.py:43
  79.7 2.8 %collective-permute-done.11.c = f32[72,256]{1,0:T(8,128)S(1)} collective-permute-done((f32[72,256]{1,0:T(8,128)S(1)}, f32[72,256]{1,0:T(8,128)S(1)}, u32[]{:S(2)}, u32[]{:S(2)}) %collective-permute-start.11) | collective-permute-done | bytes 73760 | tf_op jit(solution)/shard_map/ppermute | solution.py:43
  84.2 12.2 %all_to_all.21.x_ref = f32[16,8,512]{2,1,0:T(8,128)S(1)} all-to-all(f32[16,8,512]{2,1,0:T(8,128)S(1)} %get-tuple-element.17), channel_id=1, replica_groups={{0,16,32,48,64,80,96,112,128,144,160,176,192,208,224,240},{8,24,40,56,7..., dimensions={0} | all-to-all | bytes 524288 | tf_op jit(solution)/shard_map/all_to_all | solution.py:229
  96.4 11.4 %all_to_all.22.x_ref = f32[16,8,512]{2,1,0:T(8,128)S(1)} all-to-all(f32[16,8,512]{2,1,0:T(8,128)S(1)} %shard_map.54), channel_id=1, replica_groups={{0,16,32,48,64,80,96,112,128,144,160,176,192,208,224,240},{8,24,40,56,7..., dimensions={0} | all-to-all | bytes 524288 | tf_op jit(solution)/shard_map/all_to_all | solution.py:231
  107.9 19.2 %all_to_all.23.own_ref = bf16[8,64,1024]{2,1,0:T(8,128)(2,1)S(1)} all-to-all(bf16[8,64,1024]{2,1,0:T(8,128)(2,1)S(1)} %get-tuple-element.18), channel_id=1, replica_groups=mesh['rows'=32,'sub'=8] {'sub'}, dimensions={0} | all-to-all | bytes 2097152 | tf_op jit(solution)/shard_map/all_to_all | solution.py:237
  127.1 9.7 %collective-permute-start.15 = (bf16[8,64,1024]{2,1,0:T(8,128)(2,1)S(1)}, bf16[8,64,1024]{2,1,0:T(8,128)(2,1)S(1)}, u32[]{:S(2)}, u32[]{:S(2)}) collective-permute-start(bf16[8,64,1024]{2,1,0:T(8,128)(2,1)S(1)} %all_to_all.23.own_ref), channel_id=1, source_target_pairs={{0,8},{8,0},{16,24},{24,16},{32,40},{40,32},{48,56},{56,48},{64,72... | collective-permute-start | bytes 3145736 | tf_op jit(solution)/shard_map/ppermute | solution.py:43
  137.4 1.9 %collective-permute-done.14 = f32[4,16,256]{2,1,0:T(8,128)S(1)} collective-permute-done((f32[4,16,256]{2,1,0:T(8,128)S(1)}, f32[4,16,256]{2,1,0:T(8,128)S(1)}, u32[]{:S(2)}, u32[]{:S(2)}) %collective-permute-start.14) | collective-permute-done | bytes 65568 | tf_op jit(solution)/shard_map/ppermute | solution.py:43
  139.9 14.6 %shard_map.56 = f32[32,128]{1,0:T(8,128)} custom-call(s32[1]{0:T(128)} %bitcast.core_ref, s32[1]{0:T(128)} %bitcast.1.base_ref, bf16[8,64,1024]{2,1,0:T(8,128)(2,1)S(1)} %all_to_all.23.own_ref, bf16[8,64,1024]{2,1,0:T(8,128)(2,1)S(1)} %collective-permute-done.15.oth_ref, f32[64,1024]{1,0:T(8,128)S(1)} %get-tuple-element.19.vown_ref, ...), custom_call_target="tpu_custom_call" | custom-call | tf_op jit(solution)/shard_map/pallas_call | solution.py:239
  (30 shorter events, 8.5 us)
Async XLA Ops:
  0.6 35.5 %copy-start.1 = (bf16[1024,128]{1,0:T(8,128)(2,1)S(1)}, bf16[1024,128]{1,0:T(8,128)(2,1)}, u32[]{:S(2)}) copy-start(bf16[1024,128]{1,0:T(8,128)(2,1)} %r_ref.1) | copy-start | bytes 786436
  0.6 37.8 %copy-start = (f32[8,16,256]{2,1,0:T(8,128)S(1)}, f32[8,16,256]{2,1,0:T(8,128)}, u32[]{:S(2)}) copy-start(f32[8,16,256]{2,1,0:T(8,128)} %book_ref.3) | copy-start | bytes 393220
  34.1 49.3 %collective-permute-start.13 = (bf16[8,512,128]{2,1,0:T(8,128)(2,1)S(1)}, bf16[8,512,128]{2,1,0:T(8,128)(2,1)S(1)}, u32[]{:S(2)}, u32[]{:S(2)}) collective-permute-start(bf16[8,512,128]{2,1,0:T(8,128)(2,1)S(1)} %all_to_all.20.e_ref.own_ref), channel_id=1, source_target_pairs={{0,8},{8,0},{16,24},{24,16},{32,40},{40,32},{48,56},{56,48},{64,72... | collective-permute-start | bytes 3145736 | tf_op jit(solution)/shard_map/ppermute | solution.py:43
  36.6 1.9 %collective-permute-start = (bf16[64,512]{1,0:T(8,128)(2,1)S(1)}, bf16[64,512]{1,0:T(8,128)(2,1)S(1)}, u32[]{:S(2)}, u32[]{:S(2)}) collective-permute-start(bf16[64,512]{1,0:T(8,128)(2,1)S(1)} %get-tuple-element.12), channel_id=1, source_target_pairs={{0,8},{8,0},{16,24},{24,16},{32,40},{40,32},{48,56},{56,48},{64,72... | collective-permute-start | bytes 196616 | tf_op jit(solution)/shard_map/ppermute | solution.py:43
  40.2 3.9 %collective-permute-start.1 = (f32[72,256]{1,0:T(8,128)S(1)}, f32[72,256]{1,0:T(8,128)S(1)}, u32[]{:S(2)}, u32[]{:S(2)}) collective-permute-start(f32[72,256]{1,0:T(8,128)S(1)} %shard_map.51), channel_id=1, source_target_pairs={{0,16},{8,24},{16,0},{24,8},{32,48},{40,56},{48,32},{56,40},{64,80... | collective-permute-start | bytes 221192 | tf_op jit(solution)/shard_map/ppermute | solution.py:43
  41.5 5.8 %collective-permute-start.2 = (f32[72,256]{1,0:T(8,128)S(1)}, f32[72,256]{1,0:T(8,128)S(1)}, u32[]{:S(2)}, u32[]{:S(2)}) collective-permute-start(f32[72,256]{1,0:T(8,128)S(1)} %shard_map.51), channel_id=1, source_target_pairs={{0,32},{8,40},{16,48},{24,56},{32,0},{40,8},{48,16},{56,24},{64,96... | collective-permute-start | bytes 221192 | tf_op jit(solution)/shard_map/ppermute | solution.py:43
  43.9 4.9 %collective-permute-start.3 = (f32[72,256]{1,0:T(8,128)S(1)}, f32[72,256]{1,0:T(8,128)S(1)}, u32[]{:S(2)}, u32[]{:S(2)}) collective-permute-start(f32[72,256]{1,0:T(8,128)S(1)} %shard_map.51), channel_id=1, source_target_pairs={{0,48},{8,56},{16,32},{24,40},{32,16},{40,24},{48,0},{56,8},{64,11... | collective-permute-start | bytes 221192 | tf_op jit(solution)/shard_map/ppermute | solution.py:43
  48.8 11.9 %collective-permute-start.4 = (f32[72,256]{1,0:T(8,128)S(1)}, f32[72,256]{1,0:T(8,128)S(1)}, u32[]{:S(2)}, u32[]{:S(2)}) collective-permute-start(f32[72,256]{1,0:T(8,128)S(1)} %add_add_fusion.1.a), channel_id=1, source_target_pairs={{0,64},{8,72},{16,80},{24,88},{32,96},{40,104},{48,112},{56,120},{... | collective-permute-start | bytes 221192 | tf_op jit(solution)/shard_map/ppermute | solution.py:43
  58.6 5.0 %collective-permute-start.5 = (f32[72,256]{1,0:T(8,128)S(1)}, f32[72,256]{1,0:T(8,128)S(1)}, u32[]{:S(2)}, u32[]{:S(2)}) collective-permute-start(f32[72,256]{1,0:T(8,128)S(1)} %add_add_fusion.1.a), channel_id=1, source_target_pairs={{0,128},{8,136},{16,144},{24,152},{32,160},{40,168},{48,176},{56,1... | collective-permute-start | bytes 221192 | tf_op jit(solution)/shard_map/ppermute | solution.py:43
  59.1 5.9 %collective-permute-start.6 = (f32[72,256]{1,0:T(8,128)S(1)}, f32[72,256]{1,0:T(8,128)S(1)}, u32[]{:S(2)}, u32[]{:S(2)}) collective-permute-start(f32[72,256]{1,0:T(8,128)S(1)} %add_add_fusion.1.a), channel_id=1, source_target_pairs={{0,192},{8,200},{16,208},{24,216},{32,224},{40,232},{48,240},{56,2... | collective-permute-start | bytes 221192 | tf_op jit(solution)/shard_map/ppermute | solution.py:43
  66.9 3.9 %collective-permute-start.7 = (f32[72,256]{1,0:T(8,128)S(1)}, f32[72,256]{1,0:T(8,128)S(1)}, u32[]{:S(2)}, u32[]{:S(2)}) collective-permute-start(f32[72,256]{1,0:T(8,128)S(1)} %get-tuple-element.13), channel_id=1, source_target_pairs={{0,16},{8,24},{16,0},{24,8},{32,48},{40,56},{48,32},{56,40},{64,80... | collective-permute-start | bytes 221192 | tf_op jit(solution)/shard_map/ppermute | solution.py:43
  66.9 5.0 %collective-permute-start.8 = (f32[72,256]{1,0:T(8,128)S(1)}, f32[72,256]{1,0:T(8,128)S(1)}, u32[]{:S(2)}, u32[]{:S(2)}) collective-permute-start(f32[72,256]{1,0:T(8,128)S(1)} %get-tuple-element.13), channel_id=1, source_target_pairs={{0,32},{8,40},{16,48},{24,56},{32,0},{40,8},{48,16},{56,24},{64,96... | collective-permute-start | bytes 221192 | tf_op jit(solution)/shard_map/ppermute | solution.py:43
  69.4 4.4 %collective-permute-start.9 = (f32[72,256]{1,0:T(8,128)S(1)}, f32[72,256]{1,0:T(8,128)S(1)}, u32[]{:S(2)}, u32[]{:S(2)}) collective-permute-start(f32[72,256]{1,0:T(8,128)S(1)} %get-tuple-element.13), channel_id=1, source_target_pairs={{0,48},{8,56},{16,32},{24,40},{32,16},{40,24},{48,0},{56,8},{64,11... | collective-permute-start | bytes 221192 | tf_op jit(solution)/shard_map/ppermute | solution.py:43
  73.9 5.8 %collective-permute-start.10 = (f32[72,256]{1,0:T(8,128)S(1)}, f32[72,256]{1,0:T(8,128)S(1)}, u32[]{:S(2)}, u32[]{:S(2)}) collective-permute-start(f32[72,256]{1,0:T(8,128)S(1)} %add_add_fusion.a), channel_id=1, source_target_pairs={{0,64},{8,72},{16,80},{24,88},{32,96},{40,104},{48,112},{56,120},{... | collective-permute-start | bytes 221192 | tf_op jit(solution)/shard_map/ppermute | solution.py:43
  77.5 5.0 %collective-permute-start.11 = (f32[72,256]{1,0:T(8,128)S(1)}, f32[72,256]{1,0:T(8,128)S(1)}, u32[]{:S(2)}, u32[]{:S(2)}) collective-permute-start(f32[72,256]{1,0:T(8,128)S(1)} %add_add_fusion.a), channel_id=1, source_target_pairs={{0,128},{8,136},{16,144},{24,152},{32,160},{40,168},{48,176},{56,1... | collective-permute-start | bytes 221192 | tf_op jit(solution)/shard_map/ppermute | solution.py:43
  78.1 5.2 %collective-permute-start.12 = (f32[72,256]{1,0:T(8,128)S(1)}, f32[72,256]{1,0:T(8,128)S(1)}, u32[]{:S(2)}, u32[]{:S(2)}) collective-permute-start(f32[72,256]{1,0:T(8,128)S(1)} %add_add_fusion.a), channel_id=1, source_target_pairs={{0,192},{8,200},{16,208},{24,216},{32,224},{40,232},{48,240},{56,2... | collective-permute-start | bytes 221192 | tf_op jit(solution)/shard_map/ppermute | solution.py:43
  127.1 12.8 %collective-permute-start.15 = (bf16[8,64,1024]{2,1,0:T(8,128)(2,1)S(1)}, bf16[8,64,1024]{2,1,0:T(8,128)(2,1)S(1)}, u32[]{:S(2)}, u32[]{:S(2)}) collective-permute-start(bf16[8,64,1024]{2,1,0:T(8,128)(2,1)S(1)} %all_to_all.23.own_ref), channel_id=1, source_target_pairs={{0,8},{8,0},{16,24},{24,16},{32,40},{40,32},{48,56},{56,48},{64,72... | collective-permute-start | bytes 3145736 | tf_op jit(solution)/shard_map/ppermute | solution.py:43
  136.8 2.4 %collective-permute-start.14 = (f32[4,16,256]{2,1,0:T(8,128)S(1)}, f32[4,16,256]{2,1,0:T(8,128)S(1)}, u32[]{:S(2)}, u32[]{:S(2)}) collective-permute-start(f32[4,16,256]{2,1,0:T(8,128)S(1)} %get-tuple-element.16), channel_id=1, source_target_pairs={{0,8},{8,0},{16,24},{24,16},{32,40},{40,32},{48,56},{56,48},{64,72... | collective-permute-start | bytes 196616 | tf_op jit(solution)/shard_map/ppermute | solution.py:43
  136.8 3.1 %collective-permute-start.16 = (f32[64,1024]{1,0:T(8,128)S(1)}, f32[64,1024]{1,0:T(8,128)S(1)}, u32[]{:S(2)}, u32[]{:S(2)}) collective-permute-start(f32[64,1024]{1,0:T(8,128)S(1)} %get-tuple-element.19.vown_ref), channel_id=1, source_target_pairs={{0,8},{8,0},{16,24},{24,16},{32,40},{40,32},{48,56},{56,48},{64,72... | collective-permute-start | bytes 786440 | tf_op jit(solution)/shard_map/ppermute | solution.py:43

commit v2 on v1

v2 whole, which is shorter than its diff:
```python
import jax
import jax.numpy as jnp
from jax import lax
from jax.experimental import pallas as pl
from jax.experimental.pallas import tpu as pltpu
from jax.sharding import PartitionSpec as P

SUB_DIM = 16
CODES = 256
SOFTNESS = 4.0
PRIOR = 8.0
Q1, Q3, Q5 = 3.4445, -4.775, 2.0315

ROW_DEVS = 32
SUB_DEVS = 8
CHIPS = [[8 * z + 2 * x + c for z in range(4) for x in range(4)] for c in range(2)]

f32 = jnp.float32
bf16 = jnp.bfloat16
VMEM_LIMIT = 48 * 1024 * 1024


def call(kernel, out_shape, n_scalars, n_arrays, scratch=()):
    return pl.pallas_call(
        kernel,
        out_shape=out_shape,
        in_specs=[pl.BlockSpec(memory_space=pltpu.SMEM)] * n_scalars
        + [pl.BlockSpec(memory_space=pltpu.VMEM)] * n_arrays,
        scratch_shapes=list(scratch),
        compiler_params=pltpu.CompilerParams(vmem_limit_bytes=VMEM_LIMIT),
    )


def shape(dims, dtype):
    return jax.ShapeDtypeStruct(dims, dtype)


def dot(a, b, dims=((1,), (0,)), precision=None):
    return lax.dot_general(a, b, (dims, ((), ())), precision=precision, preferred_element_type=f32)


def permute_rows(x, to):
    return lax.ppermute(x, "rows", [(i, to(i)) for i in range(ROW_DEVS)])


def other_core(x):
    return permute_rows(x, lambda i: i ^ 1)


def load_kernel(sub_ref, r_ref, e_ref, book_ref, r_out, e_out, book_out):
    n = e_ref.shape[1]
    for k in range(SUB_DEVS):
        r_out[n * k : n * (k + 1)] = r_ref[pl.ds(pl.multiple_of((sub_ref[0] ^ k) * n, n), n)]
    e_out[...] = e_ref[...]
    book_out[...] = book_ref[...]


def rotate_kernel(place_ref, *refs):
    e_refs, r_ref, keep_ref, send_ref, feats_ref, rot_ref = refs[:SUB_DEVS], *refs[SUB_DEVS:]
    n = e_refs[0].shape[1]
    for k in range(SUB_DEVS):
        feats_ref[:, n * k : n * (k + 1)] = e_refs[k][...]
    rot = dot(feats_ref[...], r_ref[...]).T.astype(bf16)
    for m in range(rot_ref.shape[0]):
        rot_ref[m] = rot[SUB_DIM * m : SUB_DIM * (m + 1)]
    core, x = place_ref[0], place_ref[1]
    for d in range(4):
        keep_ref[d] = rot_ref[4 * core + (x ^ d)]
        send_ref[d] = rot_ref[4 * (1 - core) + (x ^ d)]


def join_kernel(keep_ref, recv_ref, *outs):
    n = keep_ref.shape[2]
    for d, out in enumerate(outs):
        out[:, :n] = keep_ref[d + 1]
        out[:, n:] = recv_ref[d + 1]


def assign(book, feats):
    sq = 0.25 * jnp.sum(book * book, axis=0, keepdims=True)
    sq_a = sq.astype(bf16).astype(f32)
    sq_b = (sq - sq_a).astype(bf16).astype(f32)
    sq_c = (sq - sq_a) - sq_b
    low = book.astype(bf16).astype(f32)
    pad = jnp.zeros((SUB_DIM - 3, book.shape[1]), f32)
    lhs = jnp.concatenate([0.5 * low, -sq_a, -sq_b, -sq_c, pad], axis=0).T.astype(bf16)
    rhs = jnp.concatenate([feats, jnp.ones_like(feats)], axis=0)
    logits = dot(lhs, rhs)
    e = jnp.exp(logits - jnp.max(logits, axis=0, keepdims=True))
    w = (e * (1.0 / jnp.sum(e, axis=0, keepdims=True))).astype(bf16)
    stats = dot(rhs, w, ((1,), (1,)))
    return w, stats


def assign_all(book, f_refs, stats_ref, w_ref=None):
    keep_ref, recv_ref = f_refs[:2]
    total = None
    for d in range(4):
        feats = f_refs[d + 1][...] if d else jnp.concatenate([keep_ref[0], recv_ref[0]], axis=1)
        w, stats = assign(book, feats)
        total = stats if total is None else total + stats
        if w_ref is not None:
            w_ref[d] = w
    stats_ref[...] = total[: stats_ref.shape[0]]


def first_kernel(place_ref, k, r, f1, f2, f3, book_ref, stats_ref):
    assign_all(book_ref[4 * place_ref[0] + place_ref[1]], (k, r, f1, f2, f3), stats_ref)


def new_book(a, b, c, d, book):
    stats = (a[...] + b[...]) + (c[...] + d[...])
    return (stats[:SUB_DIM] + PRIOR * book) / (stats[SUB_DIM : SUB_DIM + 1] + PRIOR)


def second_kernel(place_ref, k, r, f1, f2, f3, book_ref, a, b, c, d, book_out, w_ref, stats_ref):
    book = new_book(a, b, c, d, book_ref[4 * place_ref[0] + place_ref[1]])
    book_out[...] = book
    assign_all(book, (k, r, f1, f2, f3), stats_ref, w_ref)


def rebuild_kernel(a, b, c, d, book_ref, w_ref, book_out, *outs):
    book = new_book(a, b, c, d, book_ref[...])
    n = book_out.shape[2]
    for q in range(book_out.shape[0]):
        for h in range(2):
            book_out[q, 4 * h : 4 * (h + 1)] = book[4 * q : 4 * (q + 1), n * h : n * (h + 1)]
    low = book.astype(bf16)
    for i, out in enumerate(outs):
        out[...] = dot(low, w_ref[i]).astype(bf16)


def cross_kernel(place_ref, x0, x1, x2, x3, own_ref, oth_ref, out_ref, rebuilt_ref):
    for d, x in enumerate((x0, x1, x2, x3)):
        at = pl.multiple_of((place_ref[1] ^ d) * SUB_DIM, SUB_DIM)
        rebuilt_ref[pl.ds(at, SUB_DIM)] = x[...]
    n = own_ref.shape[0]
    width = out_ref.shape[2]
    for h in range(2):
        at = slice(width * h, width * (h + 1))
        part = dot(rebuilt_ref[:, :n], own_ref[:, at]) + dot(rebuilt_ref[:, n:], oth_ref[:, at])
        for t in range(part.shape[0] // 8):
            out_ref[2 * t + h] = part[8 * t : 8 * (t + 1)]


def sum_kernel(z_ref, x_ref, book_ref, out_ref):
    total = x_ref[0]
    for i in range(1, x_ref.shape[0]):
        total = total + x_ref[i]
    both = jnp.concatenate([total, book_ref[z_ref[0]]], axis=1)
    for i in range(out_ref.shape[0]):
        out_ref[i] = both


def columns_kernel(sub_ref, x_ref, v_ref, low_ref):
    n = low_ref.shape[1] // SUB_DEVS
    rows = low_ref.shape[0]
    for k in range(SUB_DEVS):
        at = pl.ds(pl.multiple_of((sub_ref[0] ^ k) * n, n), n)
        h, q = divmod(k, SUB_DEVS // 2)
        block = jnp.concatenate([x_ref[2 * t + h, :, n * q : n * (q + 1)] for t in range(rows // 8)], axis=0)
        v_ref[:rows, at] = block
        low_ref[:, at] = block.astype(bf16)
    for i in range(x_ref.shape[0]):
        u, v = divmod(i, SUB_DEVS)
        v_ref[rows + 8 * u : rows + 8 * (u + 1), n * v : n * (v + 1)] = x_ref[i, :, n * 4 :]


def polar_kernel(place_ref, c0, c1, c2, c3, vown_ref, voth_ref, out_ref, book_out, hi_ref, lo_ref, all_ref, block_ref):
    width = vown_ref.shape[1]
    rows = c0.shape[1]
    core = place_ref[0]
    n = book_out.shape[2] // 2
    for ref, at in ((vown_ref, core), (voth_ref, 1 - core)):
        for i in range(16):
            z, x = divmod(i, 4)
            u, v = divmod(i, SUB_DEVS)
            part = ref[rows + 8 * u : rows + 8 * (u + 1), n * v : n * (v + 1)]
            for h in range(2):
                book_out[4 * at + x, 4 * z : 4 * (z + 1), n * h : n * (h + 1)] = part[4 * h : 4 * (h + 1)]
    cols = jnp.concatenate([c[...].reshape(-1, width) for c in (c0, c1, c2, c3)], axis=0)
    gram = dot(cols, cols, ((0,), (0,)))
    eye = lax.broadcasted_iota(jnp.int32, (n, n), 0) == lax.broadcasted_iota(jnp.int32, (n, n), 1)
    diag = jnp.zeros((n, n), f32)
    for i in range(0, width, n):
        diag = diag + jnp.where(eye, gram[i : i + n, i : i + n], 0.0)
    square = jnp.sum(jnp.sum(diag, axis=0, keepdims=True), axis=1, keepdims=True) + 1e-06
    gram = gram * (1.0 / square)
    hi = gram.astype(bf16)
    hi_ref[...] = hi
    lo_ref[...] = (gram - hi.astype(f32)).astype(bf16)

    def times_gram(v):
        v_hi = v.astype(bf16)
        v_lo = (v - v_hi.astype(f32)).astype(bf16)
        n = v.shape[0]
        both = dot(jnp.concatenate([v_hi, v_lo], axis=0), hi_ref[...])
        return both[:n] + (both[n:] + dot(v_hi, lo_ref[...]))

    def quintic(v):
        image = times_gram(v)
        return Q1 * v + Q3 * image + Q5 * times_gram(image)

    def times_next_gram(v):
        return quintic(times_gram(quintic(v)))

    polar = jnp.concatenate([vown_ref[:rows], voth_ref[:rows]], axis=0) * (1.0 / jnp.sqrt(square))
    polar = quintic(polar)
    image = times_next_gram(polar)
    second = times_next_gram(image)
    all_ref[...] = Q1 * polar + Q3 * image + Q5 * second
    n_out = out_ref.shape[0]
    block, at = place_ref[2] // (n // n_out), place_ref[2] % (n // n_out)
    block_ref[...] = all_ref[:, pl.ds(pl.multiple_of(block * n, n), n)].T
    out = block_ref[pl.ds(pl.multiple_of(at * n_out, n_out), n_out)]
    out_ref[...] = jnp.where(core == 0, out, pltpu.roll(out, rows, 1))


def over_sub(x, k):
    return lax.ppermute(x, "sub", [(i, i ^ k) for i in range(SUB_DEVS)])


def over_y(x):
    return [over_sub(x, 2 * d) for d in (1, 2, 3)]


def mirror_z(x):
    pairs = []
    for z in range(4):
        for j in range(8):
            for s in range(SUB_DEVS):
                pairs.append(((8 * z + j) * SUB_DEVS + s, (8 * (3 - z) + j) * SUB_DEVS + (s ^ 1)))
    return lax.ppermute(x, ("rows", "sub"), pairs)


def over_z(x):
    return [x] + [permute_rows(x, lambda i, d=d: i ^ (8 * d)) for d in (1, 2, 3)]


def over_x(xs):
    return [permute_rows(x, lambda i, d=d: i ^ (2 * d)) for d, x in zip((1, 2, 3), xs)]


def exchange(x, groups):
    return lax.all_to_all(x, "rows", 0, 0, tiled=True, axis_index_groups=groups)


def per_device(embeddings, rotation, codebooks):
    n, n_feat = embeddings.shape
    width = rotation.shape[0]
    subs, _, codes = codebooks.shape
    half = subs * SUB_DIM // 2
    row_index = lax.axis_index("rows").astype(jnp.int32)
    place = jnp.stack([row_index % 2, (row_index // 2) % 4, row_index])
    z = (row_index // 8).reshape(1)
    sub = lax.axis_index("sub").astype(jnp.int32).reshape(1)

    z_block = over_sub(embeddings, 1)
    own_y = over_y(embeddings)
    other_y = over_y(z_block)
    mats, mine, books = call(
        load_kernel, tuple(shape(v.shape, v.dtype) for v in (rotation, embeddings, codebooks)), 1, 3
    )(sub, rotation, embeddings, codebooks)
    blocks = [mine, z_block]
    for a, b in zip(own_y, other_y):
        blocks += [a, b]
    part = shape((4, SUB_DIM, n), bf16)
    keep, send, e_own = call(
        rotate_kernel,
        (part, part, shape((n, width), bf16)),
        1,
        SUB_DEVS + 1,
        (pltpu.VMEM((subs, SUB_DIM, n), bf16),),
    )(place, *blocks, mats)
    recv = other_core(send)
    e_own, recv = lax.optimization_barrier((e_own, recv))
    e_oth = other_core(e_own)
    piece = shape((SUB_DIM, 2 * n), bf16)
    feats = (keep, recv, *over_x(call(join_kernel, (piece,) * 3, 0, 2)(keep, recv)))

    stats_shape = shape((SUB_DIM + 8, codes), f32)
    stats = call(first_kernel, stats_shape, 1, 6)(place, *feats, books)
    book, weights, stats = call(
        second_kernel, (shape((SUB_DIM, codes), f32), shape((4, codes, 2 * n), bf16), stats_shape), 1, 10
    )(place, *feats, books, *over_z(stats))
    book, *rebuilt = call(rebuild_kernel, (shape((4, 8, codes // 2), f32),) + (piece,) * 4, 0, 6)(
        *over_z(stats), book, weights
    )
    cross = call(
        cross_kernel, shape((16, 8, width // 2), f32), 1, 6, (pltpu.VMEM((half, 2 * n), bf16),)
    )(place, rebuilt[0], *over_x(rebuilt[1:]), e_own, e_oth)

    cross = exchange(cross, CHIPS)
    copies = call(sum_kernel, shape((16, 8, width // 2 + codes // 2), f32), 1, 2)(z, cross, book)
    cols = exchange(copies, CHIPS)
    v_own, low = call(
        columns_kernel, (shape((half + SUB_DIM, width), f32), shape((half, width), bf16)), 1, 1
    )(sub, cols)
    v_oth = other_core(v_own)
    z_low = mirror_z(low)
    c_own = jnp.stack([low] + over_y(low))
    c_oth = other_core(c_own)
    z_own = jnp.stack([z_low] + over_y(z_low))
    z_oth = other_core(z_own)
    new_rotation, new_codebooks = call(
        polar_kernel,
        (shape((width // ROW_DEVS, 2 * half), f32), shape(codebooks.shape, f32)),
        1,
        6,
        (
            pltpu.VMEM((width, width), bf16),
            pltpu.VMEM((width, width), bf16),
            pltpu.VMEM((2 * half, width), f32),
            pltpu.VMEM((128, 2 * half), f32),
        ),
    )(place, c_own, c_oth, z_own, z_oth, v_own, v_oth)
    return (new_codebooks, new_rotation)


def solution(mesh):
    return jax.shard_map(
        per_device,
        mesh=mesh,
        in_specs=(P("rows", "sub"), P(None, "sub"), P("sub", None, None)),
        out_specs=(P("sub", None, None), P("rows", "sub")),
        check_vma=False,
    )
```

time: 157 us -> 133 us (0.85); the launches traced: 155 us -> 132 us
  blocking collectives: 75.2 us -> 12 us
  starting transfers between devices: 37.8 us -> 62 us
  waiting for transfers between devices: 19.3 us -> 32.4 us
  Pallas kernels: 19.7 us -> 22.3 us
  local copies, waits for them, and re-layouts: 1.1 us -> 2.76 us
    all_to_all x4 -> x1, blocking collectives: 75.2 us -> 12 us  [exchange(): return lax.all_to_all(x, 'rows', 0, 0, tiled=True, axis_index_groups=groups)]
    ppermute x0 -> x14, starting transfers between devices: none -> 23 us  [the longest x13 20.6 us: over_sub(): return lax.ppermute(x, 'sub', [(i, i ^ k) for i in range(SUB_DEVS)])]
    ppermute x0 -> x14, waiting for transfers between devices: none -> 9.44 us  [the longest x13 8.59 us: over_sub(): return lax.ppermute(x, 'sub', [(i, i ^ k) for i in range(SUB_DEVS)])]
    all_to_all x0 -> x1, waiting for transfers between devices: none -> 8.82 us  [exchange(): return lax.all_to_all(x, 'rows', 0, 0, tiled=True, axis_index_groups=groups)]
    ppermute x17, waiting for transfers between devices: 19.3 us -> 14.1 us  [permute_rows(): return lax.ppermute(x, 'rows', [(i, to(i)) for i in range(ROW_DEVS)])]
    all_to_all x0 -> x1, starting transfers between devices: none -> 5.02 us  [exchange(): return lax.all_to_all(x, 'rows', 0, 0, tiled=True, axis_index_groups=groups)]
    ppermute x17, starting transfers between devices: 37.8 us -> 33.9 us  [permute_rows(): return lax.ppermute(x, 'rows', [(i, to(i)) for i in range(ROW_DEVS)])]
    unnamed x4 -> x6, local copies, waits for them, and re-layouts: 0.01 us -> 2.76 us
  transfers between devices with their start and end apart: 17 -> 32, of which waited for: 10 -> 16; matrix products, arithmetic and copies ran while one was open for 0% -> 0% of each run, Pallas kernels for 3% -> 4%
where the time goes in v2:
time: 133 us; the launch traced here: 132 us
  starting transfers between devices  62 us (47%)
  waiting for transfers between devices  32.4 us (24%)
  Pallas kernels  22.3 us (17%)
  blocking collectives  12 us (9%)
  local copies, waits for them, and re-layouts  2.76 us (2%)
    ppermute x17, starting transfers between devices, permute_rows(): return lax.ppermute(x, 'rows', [(i, to(i)) for i in range(ROW_DEVS)])  33.9 us
    ppermute x13, starting transfers between devices, over_sub(): return lax.ppermute(x, 'sub', [(i, i ^ k) for i in range(SUB_DEVS)])  20.6 us
    ppermute x17, waiting for transfers between devices, permute_rows(): return lax.ppermute(x, 'rows', [(i, to(i)) for i in range(ROW_DEVS)])  14.1 us
    pallas_call x1, Pallas kernels, per_device(): call(polar_kernel, (shape((width // ROW_DEVS, 2 * half), f32), shape(code...  14.1 us
    all_to_all x1, blocking collectives, exchange(): return lax.all_to_all(x, 'rows', 0, 0, tiled=True, axis_index_groups=groups)  12 us
    all_to_all x1, waiting for transfers between devices, exchange(): return lax.all_to_all(x, 'rows', 0, 0, tiled=True, axis_index_groups=groups)  8.82 us
    ppermute x13, waiting for transfers between devices, over_sub(): return lax.ppermute(x, 'sub', [(i, i ^ k) for i in range(SUB_DEVS)])  8.59 us
    all_to_all x1, starting transfers between devices, exchange(): return lax.all_to_all(x, 'rows', 0, 0, tiled=True, axis_index_groups=groups)  5.02 us
  transfers between devices with their start and end apart: 32, of which 16 were waited for; matrix products, arithmetic and copies ran while one was open for 0% of the time, Pallas kernels for 4%

profile of v2, /device:TPU:1, one launch (start us, length us, event | category | flops | bytes accessed | tf_op | source)
XLA Modules:
  0.0 132.3 jit_solution(5063471562717785725)
XLA Ops:
  0.6 7.8 %collective-permute-start = (bf16[512,128]{1,0:T(8,128)(2,1)}, bf16[512,128]{1,0:T(8,128)(2,1)S(1)}, u32[]{:S(2)}, u32[]{:S(2)}) collective-permute-start(bf16[512,128]{1,0:T(8,128)(2,1)} %e_ref.1), channel_id=1, source_target_pairs={{0,1},{1,0},{2,3},{3,2},{4,5},{5,4},{6,7},{7,6},{8,9},{9,8},{10,11... | collective-permute-start | bytes 393224 | tf_op jit(solution)/shard_map/ppermute | solution.py:220
  9.8 2.6 %collective-permute-start.3 = (bf16[512,128]{1,0:T(8,128)(2,1)}, bf16[512,128]{1,0:T(8,128)(2,1)S(1)}, u32[]{:S(2)}, u32[]{:S(2)}) collective-permute-start(bf16[512,128]{1,0:T(8,128)(2,1)} %e_ref.1), channel_id=1, source_target_pairs={{0,4},{1,5},{2,6},{3,7},{4,0},{5,1},{6,2},{7,3},{8,12},{9,13},{10,... | collective-permute-start | bytes 393224 | tf_op jit(solution)/shard_map/ppermute | solution.py:220
  13.2 3.1 %collective-permute-start.4 = (bf16[512,128]{1,0:T(8,128)(2,1)S(1)}, bf16[512,128]{1,0:T(8,128)(2,1)S(1)}, u32[]{:S(2)}, u32[]{:S(2)}) collective-permute-start(bf16[512,128]{1,0:T(8,128)(2,1)S(1)} %collective-permute-done.refs_1_), channel_id=1, source_target_pairs={{0,4},{1,5},{2,6},{3,7},{4,0},{5,1},{6,2},{7,3},{8,12},{9,13},{10,... | collective-permute-start | bytes 393224 | tf_op jit(solution)/shard_map/ppermute | solution.py:220
  19.8 3.5 %collective-permute-done.4.refs_5_ = bf16[512,128]{1,0:T(8,128)(2,1)S(1)} collective-permute-done((bf16[512,128]{1,0:T(8,128)(2,1)S(1)}, bf16[512,128]{1,0:T(8,128)(2,1)S(1)}, u32[]{:S(2)}, u32[]{:S(2)}) %collective-permute-start.4) | collective-permute-done | bytes 131104 | tf_op jit(solution)/shard_map/ppermute | solution.py:220
  23.3 2.9 %collective-permute-done.6.refs_7_ = bf16[512,128]{1,0:T(8,128)(2,1)S(1)} collective-permute-done((bf16[512,128]{1,0:T(8,128)(2,1)S(1)}, bf16[512,128]{1,0:T(8,128)(2,1)S(1)}, u32[]{:S(2)}, u32[]{:S(2)}) %collective-permute-start.6) | collective-permute-done | bytes 131104 | tf_op jit(solution)/shard_map/ppermute | solution.py:220
  31.2 2.4 %collective-permute-start.9 = (bf16[16,1024]{1,0:T(8,128)(2,1)S(1)}, bf16[16,1024]{1,0:T(8,128)(2,1)S(1)}, u32[]{:S(2)}, u32[]{:S(2)}) collective-permute-start(bf16[16,1024]{1,0:T(8,128)(2,1)S(1)} %get-tuple-element.32), channel_id=1, source_target_pairs={{0,32},{8,40},{16,48},{24,56},{32,0},{40,8},{48,16},{56,24},{64,96... | collective-permute-start | bytes 98312 | tf_op jit(solution)/shard_map/ppermute | solution.py:43
  33.9 1.9 %collective-permute-done.9.f2 = bf16[16,1024]{1,0:T(8,128)(2,1)S(1)} collective-permute-done((bf16[16,1024]{1,0:T(8,128)(2,1)S(1)}, bf16[16,1024]{1,0:T(8,128)(2,1)S(1)}, u32[]{:S(2)}, u32[]{:S(2)}) %collective-permute-start.9) | collective-permute-done | bytes 32800 | tf_op jit(solution)/shard_map/ppermute | solution.py:43
  35.7 1.9 %collective-permute-done.10.f3 = bf16[16,1024]{1,0:T(8,128)(2,1)S(1)} collective-permute-done((bf16[16,1024]{1,0:T(8,128)(2,1)S(1)}, bf16[16,1024]{1,0:T(8,128)(2,1)S(1)}, u32[]{:S(2)}, u32[]{:S(2)}) %collective-permute-start.10) | collective-permute-done | bytes 32800 | tf_op jit(solution)/shard_map/ppermute | solution.py:43
  37.6 2.4 %shard_map.53.a = f32[24,256]{1,0:T(8,128)S(1)} custom-call(s32[3]{0:T(128)S(1)} %pad_add_fusion.place_ref, bf16[4,16,512]{2,1,0:T(8,128)(2,1)S(1)} %get-tuple-element.27.keep_ref.k, bf16[4,16,512]{2,1,0:T(8,128)(2,1)S(1)} %collective-permute-done.7.recv_ref.r, bf16[16,1024]{1,0:T(8,128)(2,1)S(1)} %collective-permute-done.8.f1, ...), custom_call_target="tpu_custom_call" | custom-call | tf_op jit(solution)/shard_map/pallas_call | solution.py:282
  44.4 2.3 %collective-permute-done.13.d = f32[24,256]{1,0:T(8,128)S(1)} collective-permute-done((f32[24,256]{1,0:T(8,128)S(1)}, f32[24,256]{1,0:T(8,128)S(1)}, u32[]{:S(2)}, u32[]{:S(2)}) %collective-permute-start.13) | collective-permute-done | bytes 24608 | tf_op jit(solution)/shard_map/ppermute | solution.py:43
  46.6 2.5 %shard_map.54 = (f32[16,256]{1,0:T(8,128)S(1)}, bf16[4,256,1024]{2,1,0:T(8,128)(2,1)S(1)}, f32[24,256]{1,0:T(8,128)S(1)}) custom-call(s32[3]{0:T(128)S(1)} %pad_add_fusion.place_ref, bf16[4,16,512]{2,1,0:T(8,128)(2,1)S(1)} %get-tuple-element.27.keep_ref.k, bf16[4,16,512]{2,1,0:T(8,128)(2,1)S(1)} %collective-permute-done.7.recv_ref.r, ...), custom_call_target="tpu_custom_call" | custom-call | tf_op jit(solution)/shard_map/pallas_call | solution.py:283
  49.2 1.7 %collective-permute-start.15 = (f32[24,256]{1,0:T(8,128)S(1)}, f32[24,256]{1,0:T(8,128)S(1)}, u32[]{:S(2)}, u32[]{:S(2)}) collective-permute-start(f32[24,256]{1,0:T(8,128)S(1)} %get-tuple-element.35.a), channel_id=1, source_target_pairs={{0,128},{8,136},{16,144},{24,152},{32,160},{40,168},{48,176},{56,1... | collective-permute-start | bytes 73736 | tf_op jit(solution)/shard_map/ppermute | solution.py:43
  50.9 1.8 %collective-permute-start.16 = (f32[24,256]{1,0:T(8,128)S(1)}, f32[24,256]{1,0:T(8,128)S(1)}, u32[]{:S(2)}, u32[]{:S(2)}) collective-permute-start(f32[24,256]{1,0:T(8,128)S(1)} %get-tuple-element.35.a), channel_id=1, source_target_pairs={{0,192},{8,200},{16,208},{24,216},{32,224},{40,232},{48,240},{56,2... | collective-permute-start | bytes 73736 | tf_op jit(solution)/shard_map/ppermute | solution.py:43
  52.9 2.6 %collective-permute-done.16.d = f32[24,256]{1,0:T(8,128)S(1)} collective-permute-done((f32[24,256]{1,0:T(8,128)S(1)}, f32[24,256]{1,0:T(8,128)S(1)}, u32[]{:S(2)}, u32[]{:S(2)}) %collective-permute-start.16) | collective-permute-done | bytes 24608 | tf_op jit(solution)/shard_map/ppermute | solution.py:43
  55.9 1.9 %collective-permute-start.18 = (bf16[16,1024]{1,0:T(8,128)(2,1)S(1)}, bf16[16,1024]{1,0:T(8,128)(2,1)S(1)}, u32[]{:S(2)}, u32[]{:S(2)}) collective-permute-start(bf16[16,1024]{1,0:T(8,128)(2,1)S(1)} %get-tuple-element.40), channel_id=1, source_target_pairs={{0,32},{8,40},{16,48},{24,56},{32,0},{40,8},{48,16},{56,24},{64,96... | collective-permute-start | bytes 98312 | tf_op jit(solution)/shard_map/ppermute | solution.py:43
  57.8 2.0 %collective-permute-start.19 = (bf16[16,1024]{1,0:T(8,128)(2,1)S(1)}, bf16[16,1024]{1,0:T(8,128)(2,1)S(1)}, u32[]{:S(2)}, u32[]{:S(2)}) collective-permute-start(bf16[16,1024]{1,0:T(8,128)(2,1)S(1)} %get-tuple-element.41), channel_id=1, source_target_pairs={{0,48},{8,56},{16,32},{24,40},{32,16},{40,24},{48,0},{56,8},{64,11... | collective-permute-start | bytes 98312 | tf_op jit(solution)/shard_map/ppermute | solution.py:43
  63.5 5.0 %all-to-all-start = ((f32[16,8,512]{2,1,0:T(8,128)}), f32[16,8,512]{2,1,0:T(8,128)S(1)}, u32[]{:S(2)}, u32[]{:S(2)}) async-start(f32[16,8,512]{2,1,0:T(8,128)} %shard_map.56), calls=%async_computation | async-start | bytes 524288 | tf_op jit(solution)/shard_map/all_to_all | solution.py:245
  68.5 8.8 %all-to-all-done.x_ref = f32[16,8,512]{2,1,0:T(8,128)S(1)} async-done(((f32[16,8,512]{2,1,0:T(8,128)}), f32[16,8,512]{2,1,0:T(8,128)S(1)}, u32[]{:S(2)}, u32[]{:S(2)}) %all-to-all-start) | async-done | bytes 262176 | tf_op jit(solution)/shard_map/all_to_all | solution.py:245
  77.4 12.0 %all_to_all.10.x_ref = f32[16,8,640]{2,1,0:T(8,128)S(1)} all-to-all(f32[16,8,640]{2,1,0:T(8,128)S(1)} %shard_map.57), channel_id=1, replica_groups={{0,16,32,48,64,80,96,112,128,144,160,176,192,208,224,240},{8,24,40,56,7..., dimensions={0} | all-to-all | bytes 655360 | tf_op jit(solution)/shard_map/all_to_all | solution.py:245
  89.4 2.4 %collective-permute-start.25 = (bf16[64,1024]{1,0:T(8,128)(2,1)S(1)}, bf16[64,1024]{1,0:T(8,128)(2,1)S(1)}, u32[]{:S(2)}, u32[]{:S(2)}) collective-permute-start(bf16[64,1024]{1,0:T(8,128)(2,1)S(1)} %get-tuple-element.44), channel_id=1, source_target_pairs={{0,193},{1,192},{2,195},{3,194},{4,197},{5,196},{6,199},{7,198},{8... | collective-permute-start | bytes 393224 | tf_op jit(solution)/shard_map/ppermute | solution.py:233
  92.8 2.3 %collective-permute-start.21 = (bf16[64,1024]{1,0:T(8,128)(2,1)S(1)}, bf16[64,1024]{1,0:T(8,128)(2,1)S(1)}, u32[]{:S(2)}, u32[]{:S(2)}) collective-permute-start(bf16[64,1024]{1,0:T(8,128)(2,1)S(1)} %get-tuple-element.44), channel_id=1, source_target_pairs={{0,2},{1,3},{2,0},{3,1},{4,6},{5,7},{6,4},{7,5},{8,10},{9,11},{10,... | collective-permute-start | bytes 393224 | tf_op jit(solution)/shard_map/ppermute | solution.py:220
  99.3 12.7 %collective-permute-start.24 = (bf16[4,64,1024]{2,1,0:T(8,128)(2,1)S(1)}, bf16[4,64,1024]{2,1,0:T(8,128)(2,1)S(1)}, u32[]{:S(2)}, u32[]{:S(2)}) collective-permute-start(bf16[4,64,1024]{2,1,0:T(8,128)(2,1)S(1)} %pad_maximum_fusion.c0), channel_id=1, source_target_pairs={{0,8},{8,0},{16,24},{24,16},{32,40},{40,32},{48,56},{56,48},{64,72... | collective-permute-start | bytes 1572872 | tf_op jit(solution)/shard_map/ppermute | solution.py:43
  112.0 4.2 %collective-permute-start.29 = (bf16[4,64,1024]{2,1,0:T(8,128)(2,1)S(1)}, bf16[4,64,1024]{2,1,0:T(8,128)(2,1)S(1)}, u32[]{:S(2)}, u32[]{:S(2)}) collective-permute-start(bf16[4,64,1024]{2,1,0:T(8,128)(2,1)S(1)} %pad_maximum_fusion.1.c2), channel_id=1, source_target_pairs={{0,8},{8,0},{16,24},{24,16},{32,40},{40,32},{48,56},{56,48},{64,72... | collective-permute-start | bytes 1572872 | tf_op jit(solution)/shard_map/ppermute | solution.py:43
  118.3 14.1 %shard_map.59 = (f32[32,128]{1,0:T(8,128)}, f32[8,16,256]{2,1,0:T(8,128)}) custom-call(s32[3]{0:T(128)S(1)} %pad_add_fusion.place_ref, bf16[4,64,1024]{2,1,0:T(8,128)(2,1)S(1)} %pad_maximum_fusion.c0, bf16[4,64,1024]{2,1,0:T(8,128)(2,1)S(1)} %collective-permute-done.24.c1, bf16[4,64,1024]{2,1,0:T(8,128)(2,1)S(1)} %pad_maximum_fusion.1.c2, ...), custom_call_target="tpu_custom_call" | custom-call | tf_op jit(solution)/shard_map/pallas_call | solution.py:305
  (60 shorter events, 26.8 us)
Async XLA Ops:
  0.6 11.7 %collective-permute-start = (bf16[512,128]{1,0:T(8,128)(2,1)}, bf16[512,128]{1,0:T(8,128)(2,1)S(1)}, u32[]{:S(2)}, u32[]{:S(2)}) collective-permute-start(bf16[512,128]{1,0:T(8,128)(2,1)} %e_ref.1), channel_id=1, source_target_pairs={{0,1},{1,0},{2,3},{3,2},{4,5},{5,4},{6,7},{7,6},{8,9},{9,8},{10,11... | collective-permute-start | bytes 393224 | tf_op jit(solution)/shard_map/ppermute | solution.py:220
  8.5 7.8 %collective-permute-start.1 = (bf16[512,128]{1,0:T(8,128)(2,1)}, bf16[512,128]{1,0:T(8,128)(2,1)S(1)}, u32[]{:S(2)}, u32[]{:S(2)}) collective-permute-start(bf16[512,128]{1,0:T(8,128)(2,1)} %e_ref.1), channel_id=1, source_target_pairs={{0,2},{1,3},{2,0},{3,1},{4,6},{5,7},{6,4},{7,5},{8,10},{9,11},{10,... | collective-permute-start | bytes 393224 | tf_op jit(solution)/shard_map/ppermute | solution.py:220
  9.8 9.4 %collective-permute-start.3 = (bf16[512,128]{1,0:T(8,128)(2,1)}, bf16[512,128]{1,0:T(8,128)(2,1)S(1)}, u32[]{:S(2)}, u32[]{:S(2)}) collective-permute-start(bf16[512,128]{1,0:T(8,128)(2,1)} %e_ref.1), channel_id=1, source_target_pairs={{0,4},{1,5},{2,6},{3,7},{4,0},{5,1},{6,2},{7,3},{8,12},{9,13},{10,... | collective-permute-start | bytes 393224 | tf_op jit(solution)/shard_map/ppermute | solution.py:220
  12.4 7.4 %collective-permute-start.5 = (bf16[512,128]{1,0:T(8,128)(2,1)}, bf16[512,128]{1,0:T(8,128)(2,1)S(1)}, u32[]{:S(2)}, u32[]{:S(2)}) collective-permute-start(bf16[512,128]{1,0:T(8,128)(2,1)} %e_ref.1), channel_id=1, source_target_pairs={{0,6},{1,7},{2,4},{3,5},{4,2},{5,3},{6,0},{7,1},{8,14},{9,15},{10,... | collective-permute-start | bytes 393224 | tf_op jit(solution)/shard_map/ppermute | solution.py:220
  12.4 7.4 %collective-permute-start.2 = (bf16[512,128]{1,0:T(8,128)(2,1)S(1)}, bf16[512,128]{1,0:T(8,128)(2,1)S(1)}, u32[]{:S(2)}, u32[]{:S(2)}) collective-permute-start(bf16[512,128]{1,0:T(8,128)(2,1)S(1)} %collective-permute-done.refs_1_), channel_id=1, source_target_pairs={{0,2},{1,3},{2,0},{3,1},{4,6},{5,7},{6,4},{7,5},{8,10},{9,11},{10,... | collective-permute-start | bytes 393224 | tf_op jit(solution)/shard_map/ppermute | solution.py:220
  13.2 10.1 %collective-permute-start.4 = (bf16[512,128]{1,0:T(8,128)(2,1)S(1)}, bf16[512,128]{1,0:T(8,128)(2,1)S(1)}, u32[]{:S(2)}, u32[]{:S(2)}) collective-permute-start(bf16[512,128]{1,0:T(8,128)(2,1)S(1)} %collective-permute-done.refs_1_), channel_id=1, source_target_pairs={{0,4},{1,5},{2,6},{3,7},{4,0},{5,1},{6,2},{7,3},{8,12},{9,13},{10,... | collective-permute-start | bytes 393224 | tf_op jit(solution)/shard_map/ppermute | solution.py:220
  16.2 10.0 %collective-permute-start.6 = (bf16[512,128]{1,0:T(8,128)(2,1)S(1)}, bf16[512,128]{1,0:T(8,128)(2,1)S(1)}, u32[]{:S(2)}, u32[]{:S(2)}) collective-permute-start(bf16[512,128]{1,0:T(8,128)(2,1)S(1)} %collective-permute-done.refs_1_), channel_id=1, source_target_pairs={{0,6},{1,7},{2,4},{3,5},{4,2},{5,3},{6,0},{7,1},{8,14},{9,15},{10,... | collective-permute-start | bytes 393224 | tf_op jit(solution)/shard_map/ppermute | solution.py:220
  29.5 32.2 %collective-permute-start.20 = (bf16[512,1024]{1,0:T(8,128)(2,1)S(1)}, bf16[512,1024]{1,0:T(8,128)(2,1)S(1)}, u32[]{:S(2)}, u32[]{:S(2)}) collective-permute-start(bf16[512,1024]{1,0:T(8,128)(2,1)S(1)} %get-tuple-element.42.own_ref), channel_id=1, source_target_pairs={{0,8},{8,0},{16,24},{24,16},{32,40},{40,32},{48,56},{56,48},{64,72... | collective-permute-start | bytes 3145736 | tf_op jit(solution)/shard_map/ppermute | solution.py:43
  31.2 4.5 %collective-permute-start.9 = (bf16[16,1024]{1,0:T(8,128)(2,1)S(1)}, bf16[16,1024]{1,0:T(8,128)(2,1)S(1)}, u32[]{:S(2)}, u32[]{:S(2)}) collective-permute-start(bf16[16,1024]{1,0:T(8,128)(2,1)S(1)} %get-tuple-element.32), channel_id=1, source_target_pairs={{0,32},{8,40},{16,48},{24,56},{32,0},{40,8},{48,16},{56,24},{64,96... | collective-permute-start | bytes 98312 | tf_op jit(solution)/shard_map/ppermute | solution.py:43
  33.7 4.0 %collective-permute-start.10 = (bf16[16,1024]{1,0:T(8,128)(2,1)S(1)}, bf16[16,1024]{1,0:T(8,128)(2,1)S(1)}, u32[]{:S(2)}, u32[]{:S(2)}) collective-permute-start(bf16[16,1024]{1,0:T(8,128)(2,1)S(1)} %get-tuple-element.33), channel_id=1, source_target_pairs={{0,48},{8,56},{16,32},{24,40},{32,16},{40,24},{48,0},{56,8},{64,11... | collective-permute-start | bytes 98312 | tf_op jit(solution)/shard_map/ppermute | solution.py:43
  42.0 4.6 %collective-permute-start.13 = (f32[24,256]{1,0:T(8,128)S(1)}, f32[24,256]{1,0:T(8,128)S(1)}, u32[]{:S(2)}, u32[]{:S(2)}) collective-permute-start(f32[24,256]{1,0:T(8,128)S(1)} %shard_map.53.a), channel_id=1, source_target_pairs={{0,192},{8,200},{16,208},{24,216},{32,224},{40,232},{48,240},{56,2... | collective-permute-start | bytes 73736 | tf_op jit(solution)/shard_map/ppermute | solution.py:43
  50.9 4.5 %collective-permute-start.16 = (f32[24,256]{1,0:T(8,128)S(1)}, f32[24,256]{1,0:T(8,128)S(1)}, u32[]{:S(2)}, u32[]{:S(2)}) collective-permute-start(f32[24,256]{1,0:T(8,128)S(1)} %get-tuple-element.35.a), channel_id=1, source_target_pairs={{0,192},{8,200},{16,208},{24,216},{32,224},{40,232},{48,240},{56,2... | collective-permute-start | bytes 73736 | tf_op jit(solution)/shard_map/ppermute | solution.py:43
  55.9 4.4 %collective-permute-start.18 = (bf16[16,1024]{1,0:T(8,128)(2,1)S(1)}, bf16[16,1024]{1,0:T(8,128)(2,1)S(1)}, u32[]{:S(2)}, u32[]{:S(2)}) collective-permute-start(bf16[16,1024]{1,0:T(8,128)(2,1)S(1)} %get-tuple-element.40), channel_id=1, source_target_pairs={{0,32},{8,40},{16,48},{24,56},{32,0},{40,8},{48,16},{56,24},{64,96... | collective-permute-start | bytes 98312 | tf_op jit(solution)/shard_map/ppermute | solution.py:43
  57.8 4.0 %collective-permute-start.19 = (bf16[16,1024]{1,0:T(8,128)(2,1)S(1)}, bf16[16,1024]{1,0:T(8,128)(2,1)S(1)}, u32[]{:S(2)}, u32[]{:S(2)}) collective-permute-start(bf16[16,1024]{1,0:T(8,128)(2,1)S(1)} %get-tuple-element.41), channel_id=1, source_target_pairs={{0,48},{8,56},{16,32},{24,40},{32,16},{40,24},{48,0},{56,8},{64,11... | collective-permute-start | bytes 98312 | tf_op jit(solution)/shard_map/ppermute | solution.py:43
  63.5 13.9 %all-to-all-start = ((f32[16,8,512]{2,1,0:T(8,128)}), f32[16,8,512]{2,1,0:T(8,128)S(1)}, u32[]{:S(2)}, u32[]{:S(2)}) async-start(f32[16,8,512]{2,1,0:T(8,128)} %shard_map.56), calls=%async_computation | async-start | bytes 524288 | tf_op jit(solution)/shard_map/all_to_all | solution.py:245
  89.4 6.5 %collective-permute-start.25 = (bf16[64,1024]{1,0:T(8,128)(2,1)S(1)}, bf16[64,1024]{1,0:T(8,128)(2,1)S(1)}, u32[]{:S(2)}, u32[]{:S(2)}) collective-permute-start(bf16[64,1024]{1,0:T(8,128)(2,1)S(1)} %get-tuple-element.44), channel_id=1, source_target_pairs={{0,193},{1,192},{2,195},{3,194},{4,197},{5,196},{6,199},{7,198},{8... | collective-permute-start | bytes 393224 | tf_op jit(solution)/shard_map/ppermute | solution.py:233
  91.8 6.7 %collective-permute-start.23 = (bf16[64,1024]{1,0:T(8,128)(2,1)S(1)}, bf16[64,1024]{1,0:T(8,128)(2,1)S(1)}, u32[]{:S(2)}, u32[]{:S(2)}) collective-permute-start(bf16[64,1024]{1,0:T(8,128)(2,1)S(1)} %get-tuple-element.44), channel_id=1, source_target_pairs={{0,6},{1,7},{2,4},{3,5},{4,2},{5,3},{6,0},{7,1},{8,14},{9,15},{10,... | collective-permute-start | bytes 393224 | tf_op jit(solution)/shard_map/ppermute | solution.py:220
  92.2 7.0 %collective-permute-start.22 = (bf16[64,1024]{1,0:T(8,128)(2,1)S(1)}, bf16[64,1024]{1,0:T(8,128)(2,1)S(1)}, u32[]{:S(2)}, u32[]{:S(2)}) collective-permute-start(bf16[64,1024]{1,0:T(8,128)(2,1)S(1)} %get-tuple-element.44), channel_id=1, source_target_pairs={{0,4},{1,5},{2,6},{3,7},{4,0},{5,1},{6,2},{7,3},{8,12},{9,13},{10,... | collective-permute-start | bytes 393224 | tf_op jit(solution)/shard_map/ppermute | solution.py:220
  92.8 6.4 %collective-permute-start.21 = (bf16[64,1024]{1,0:T(8,128)(2,1)S(1)}, bf16[64,1024]{1,0:T(8,128)(2,1)S(1)}, u32[]{:S(2)}, u32[]{:S(2)}) collective-permute-start(bf16[64,1024]{1,0:T(8,128)(2,1)S(1)} %get-tuple-element.44), channel_id=1, source_target_pairs={{0,2},{1,3},{2,0},{3,1},{4,6},{5,7},{6,4},{7,5},{8,10},{9,11},{10,... | collective-permute-start | bytes 393224 | tf_op jit(solution)/shard_map/ppermute | solution.py:220
  95.9 16.0 %collective-permute-start.28 = (bf16[64,1024]{1,0:T(8,128)(2,1)S(1)}, bf16[64,1024]{1,0:T(8,128)(2,1)S(1)}, u32[]{:S(2)}, u32[]{:S(2)}) collective-permute-start(bf16[64,1024]{1,0:T(8,128)(2,1)S(1)} %collective-permute-done.25), channel_id=1, source_target_pairs={{0,6},{1,7},{2,4},{3,5},{4,2},{5,3},{6,0},{7,1},{8,14},{9,15},{10,... | collective-permute-start | bytes 393224 | tf_op jit(solution)/shard_map/ppermute | solution.py:220
  96.4 15.5 %collective-permute-start.27 = (bf16[64,1024]{1,0:T(8,128)(2,1)S(1)}, bf16[64,1024]{1,0:T(8,128)(2,1)S(1)}, u32[]{:S(2)}, u32[]{:S(2)}) collective-permute-start(bf16[64,1024]{1,0:T(8,128)(2,1)S(1)} %collective-permute-done.25), channel_id=1, source_target_pairs={{0,4},{1,5},{2,6},{3,7},{4,0},{5,1},{6,2},{7,3},{8,12},{9,13},{10,... | collective-permute-start | bytes 393224 | tf_op jit(solution)/shard_map/ppermute | solution.py:220
  98.5 13.4 %collective-permute-start.26 = (bf16[64,1024]{1,0:T(8,128)(2,1)S(1)}, bf16[64,1024]{1,0:T(8,128)(2,1)S(1)}, u32[]{:S(2)}, u32[]{:S(2)}) collective-permute-start(bf16[64,1024]{1,0:T(8,128)(2,1)S(1)} %collective-permute-done.25), channel_id=1, source_target_pairs={{0,2},{1,3},{2,0},{3,1},{4,6},{5,7},{6,4},{7,5},{8,10},{9,11},{10,... | collective-permute-start | bytes 393224 | tf_op jit(solution)/shard_map/ppermute | solution.py:220
  99.3 19.0 %collective-permute-start.24 = (bf16[4,64,1024]{2,1,0:T(8,128)(2,1)S(1)}, bf16[4,64,1024]{2,1,0:T(8,128)(2,1)S(1)}, u32[]{:S(2)}, u32[]{:S(2)}) collective-permute-start(bf16[4,64,1024]{2,1,0:T(8,128)(2,1)S(1)} %pad_maximum_fusion.c0), channel_id=1, source_target_pairs={{0,8},{8,0},{16,24},{24,16},{32,40},{40,32},{48,56},{56,48},{64,72... | collective-permute-start | bytes 1572872 | tf_op jit(solution)/shard_map/ppermute | solution.py:43
  112.0 6.3 %collective-permute-start.29 = (bf16[4,64,1024]{2,1,0:T(8,128)(2,1)S(1)}, bf16[4,64,1024]{2,1,0:T(8,128)(2,1)S(1)}, u32[]{:S(2)}, u32[]{:S(2)}) collective-permute-start(bf16[4,64,1024]{2,1,0:T(8,128)(2,1)S(1)} %pad_maximum_fusion.1.c2), channel_id=1, source_target_pairs={{0,8},{8,0},{16,24},{24,16},{32,40},{40,32},{48,56},{56,48},{64,72... | collective-permute-start | bytes 1572872 | tf_op jit(solution)/shard_map/ppermute | solution.py:43
  (11 other events, 29.3 us)

commit v3 on v2

v3 whole, which is shorter than its diff:
```python
import jax
import jax.numpy as jnp
from jax import lax
from jax.experimental import pallas as pl
from jax.experimental.pallas import tpu as pltpu
from jax.sharding import PartitionSpec as P

SUB_DIM = 16
CODES = 256
SOFTNESS = 4.0
PRIOR = 8.0
Q1, Q3, Q5 = 3.4445, -4.775, 2.0315

ROW_DEVS = 32
SUB_DEVS = 8

f32 = jnp.float32
bf16 = jnp.bfloat16
VMEM_LIMIT = 48 * 1024 * 1024


def call(kernel, out_shape, n_scalars, n_arrays, scratch=()):
    return pl.pallas_call(
        kernel,
        out_shape=out_shape,
        in_specs=[pl.BlockSpec(memory_space=pltpu.SMEM)] * n_scalars
        + [pl.BlockSpec(memory_space=pltpu.VMEM)] * n_arrays,
        scratch_shapes=list(scratch),
        compiler_params=pltpu.CompilerParams(vmem_limit_bytes=VMEM_LIMIT),
    )


def shape(dims, dtype):
    return jax.ShapeDtypeStruct(dims, dtype)


def dot(a, b, dims=((1,), (0,)), precision=None):
    return lax.dot_general(a, b, (dims, ((), ())), precision=precision, preferred_element_type=f32)


def permute_rows(x, to):
    return lax.ppermute(x, "rows", [(i, to(i)) for i in range(ROW_DEVS)])


def other_core(x):
    return permute_rows(x, lambda i: i ^ 1)


def load_kernel(place_ref, r_ref, e_ref, book_ref, r_out, e_out, book_out):
    n = e_ref.shape[1]
    for k in range(SUB_DEVS):
        r_out[n * k : n * (k + 1)] = r_ref[pl.ds(pl.multiple_of((place_ref[3] ^ k) * n, n), n)]
    e_out[...] = e_ref[...]
    book_out[...] = book_ref[...]


def rotate_kernel(place_ref, *refs):
    e_refs, r_ref, keep_ref, send_ref, feats_ref, rot_ref = refs[:SUB_DEVS], *refs[SUB_DEVS:]
    n = e_refs[0].shape[1]
    for k in range(SUB_DEVS):
        feats_ref[:, n * k : n * (k + 1)] = e_refs[k][...]
    rot = dot(feats_ref[...], r_ref[...]).T.astype(bf16)
    for m in range(rot_ref.shape[0]):
        rot_ref[m] = rot[SUB_DIM * m : SUB_DIM * (m + 1)]
    core, x = place_ref[0], place_ref[1]
    for d in range(4):
        keep_ref[d] = rot_ref[4 * core + (x ^ d)]
        send_ref[d] = rot_ref[4 * (1 - core) + (x ^ d)]


def join_kernel(keep_ref, recv_ref, *outs):
    n = keep_ref.shape[2]
    for d, out in enumerate(outs):
        out[:, :n] = keep_ref[d + 1]
        out[:, n:] = recv_ref[d + 1]


def score_matrix(book):
    sq = 0.25 * jnp.sum(book * book, axis=0, keepdims=True)
    sq_a = sq.astype(bf16).astype(f32)
    sq_b = (sq - sq_a).astype(bf16).astype(f32)
    sq_c = (sq - sq_a) - sq_b
    low = book.astype(bf16).astype(f32)
    pad = jnp.zeros((SUB_DIM - 3, book.shape[1]), f32)
    return jnp.concatenate([0.5 * low, -sq_a, -sq_b, -sq_c, pad], axis=0).T.astype(bf16)


def assign(lhs, feats):
    rhs = jnp.concatenate([feats, jnp.ones_like(feats)], axis=0)
    logits = dot(lhs, rhs)
    e = jnp.exp(logits - jnp.max(logits, axis=0, keepdims=True))
    w = (e * (1.0 / jnp.sum(e, axis=0, keepdims=True))).astype(bf16)
    return w, dot(rhs, w, ((1,), (1,)))


def assign_all(book, f_refs, stats_ref, w_ref=None):
    keep_ref, recv_ref = f_refs[:2]
    n = keep_ref.shape[2]
    lhs = score_matrix(book)
    total = None
    for d in range(4):
        for h in range(2):
            at = slice(n * h, n * (h + 1))
            feats = f_refs[d + 1][:, at] if d else f_refs[h][0]
            w, stats = assign(lhs, feats)
            total = stats if total is None else total + stats
            if w_ref is not None:
                w_ref[d, :, at] = w
    stats_ref[...] = total[: stats_ref.shape[0]]


def first_kernel(place_ref, k, r, f1, f2, f3, book_ref, stats_ref):
    assign_all(book_ref[4 * place_ref[0] + place_ref[1]], (k, r, f1, f2, f3), stats_ref)


def new_book(a, b, c, d, book):
    stats = (a[...] + b[...]) + (c[...] + d[...])
    return (stats[:SUB_DIM] + PRIOR * book) / (stats[SUB_DIM : SUB_DIM + 1] + PRIOR)


def second_kernel(place_ref, k, r, f1, f2, f3, book_ref, a, b, c, d, book_out, w_ref, stats_ref):
    book = new_book(a, b, c, d, book_ref[4 * place_ref[0] + place_ref[1]])
    book_out[...] = book
    assign_all(book, (k, r, f1, f2, f3), stats_ref, w_ref)


def rebuild_kernel(a, b, c, d, book_ref, w_ref, book_out, *outs):
    book = new_book(a, b, c, d, book_ref[...])
    book_out[...] = book
    low = book.astype(bf16)
    for i, out in enumerate(outs):
        out[...] = dot(low, w_ref[i]).astype(bf16)


def cross_kernel(x0, x1, x2, x3, own_ref, oth_ref, *outs):
    rebuilt = jnp.concatenate([x0[...], x1[...], x2[...], x3[...]], axis=0)
    n = own_ref.shape[0]
    part = dot(rebuilt[:, :n], own_ref[...]) + dot(rebuilt[:, n:], oth_ref[...])
    for i, out in enumerate(outs):
        out[...] = part[SUB_DIM * i : SUB_DIM * (i + 1)]


def sum_kernel(a, b, c, d, book_ref, out_ref):
    n = a.shape[1]
    out_ref[:, :n] = (a[...] + b[...]) + (c[...] + d[...])
    out_ref[:, n:] = book_ref[...]


def columns_kernel(place_ref, x0, x1, x2, x3, v_ref, low_ref):
    width = low_ref.shape[1]
    n = width // SUB_DEVS
    for d, x in enumerate((x0, x1, x2, x3)):
        rows = pl.ds(pl.multiple_of((place_ref[1] ^ d) * SUB_DIM, SUB_DIM), SUB_DIM)
        for k in range(SUB_DEVS):
            at = pl.ds(pl.multiple_of((place_ref[3] ^ k) * n, n), n)
            block = x[:, n * k : n * (k + 1)]
            v_ref[rows, at] = block
            low_ref[rows, at] = block.astype(bf16)
        v_ref[rows, width:] = x[:, width:]


def polar_kernel(
    place_ref, c0, c1, c2, c3, v_ref, book_ref, keep_ref, send_ref, book_out, hi_ref, lo_ref, all_ref, block_ref
):
    rows, width = all_ref.shape
    core = place_ref[0]
    n = block_ref.shape[0]
    for x in range(4):
        at = slice(SUB_DIM * x, SUB_DIM * (x + 1))
        book_out[4 * core + x] = v_ref[at, width:]
        book_out[4 * (1 - core) + x] = book_ref[at]
    cols = jnp.concatenate([c[...].reshape(-1, width) for c in (c0, c1, c2, c3)], axis=0)
    gram = dot(cols, cols, ((0,), (0,)))
    eye = lax.broadcasted_iota(jnp.int32, (n, n), 0) == lax.broadcasted_iota(jnp.int32, (n, n), 1)
    diag = jnp.zeros((n, n), f32)
    for i in range(0, width, n):
        diag = diag + jnp.where(eye, gram[i : i + n, i : i + n], 0.0)
    square = jnp.sum(jnp.sum(diag, axis=0, keepdims=True), axis=1, keepdims=True) + 1e-06
    gram = gram * (1.0 / square)
    hi = gram.astype(bf16)
    hi_ref[...] = hi
    lo_ref[...] = (gram - hi.astype(f32)).astype(bf16)

    def times_gram(v):
        v_hi = v.astype(bf16)
        v_lo = (v - v_hi.astype(f32)).astype(bf16)
        n = v.shape[0]
        both = dot(jnp.concatenate([v_hi, v_lo], axis=0), hi_ref[...])
        return both[:n] + (both[n:] + dot(v_hi, lo_ref[...]))

    def quintic(v):
        image = times_gram(v)
        return Q1 * v + Q3 * image + Q5 * times_gram(image)

    def times_next_gram(v):
        return quintic(times_gram(quintic(v)))

    polar = v_ref[:, :width] * (1.0 / jnp.sqrt(square))
    polar = quintic(polar)
    image = times_next_gram(polar)
    second = times_next_gram(image)
    all_ref[...] = Q1 * polar + Q3 * image + Q5 * second
    n_out = keep_ref.shape[0]
    per_block = n // n_out
    block_ref[...] = all_ref[:, pl.ds(pl.multiple_of(place_ref[2] // per_block * n, n), n)].T
    at = place_ref[2] % per_block
    keep_ref[...] = block_ref[pl.ds(pl.multiple_of(at * n_out, n_out), n_out)]
    send_ref[...] = block_ref[pl.ds(pl.multiple_of((at ^ 1) * n_out, n_out), n_out)]


def over_sub(x, k):
    return lax.ppermute(x, "sub", [(i, i ^ k) for i in range(SUB_DEVS)])


def over_y(x):
    return [over_sub(x, 2 * d) for d in (1, 2, 3)]


def over_sub_mirrored(x, k):
    pairs = []
    for z in range(4):
        for j in range(8):
            for s in range(SUB_DEVS):
                pairs.append(((8 * z + j) * SUB_DEVS + s, (8 * (3 - z) + j) * SUB_DEVS + (s ^ k)))
    return lax.ppermute(x, ("rows", "sub"), pairs)


def others_over_sub(x, across):
    partner = across(x, 1)
    y = over_y(x)
    far = across(x, 5)
    return [partner, y[0], over_sub(partner, 2), y[1], far, y[2], over_sub(partner, 6)]


def over_z(x):
    return [x] + [permute_rows(x, lambda i, d=d: i ^ (8 * d)) for d in (1, 2, 3)]


def over_x(xs):
    return [permute_rows(x, lambda i, d=d: i ^ (2 * d)) for d, x in zip((1, 2, 3), xs)]


def per_device(embeddings, rotation, codebooks):
    n, n_feat = embeddings.shape
    width = rotation.shape[0]
    subs, _, codes = codebooks.shape
    half = subs * SUB_DIM // 2
    row_index = lax.axis_index("rows").astype(jnp.int32)
    sub = lax.axis_index("sub").astype(jnp.int32)
    core = row_index % 2
    place = jnp.stack([core, (row_index // 2) % 4, row_index, sub])

    others = others_over_sub(embeddings, over_sub)
    mats, mine, books = call(
        load_kernel, tuple(shape(v.shape, v.dtype) for v in (rotation, embeddings, codebooks)), 1, 3
    )(place, rotation, embeddings, codebooks)
    part = shape((4, SUB_DIM, n), bf16)
    keep, send, e_own = call(
        rotate_kernel,
        (part, part, shape((n, width), bf16)),
        1,
        SUB_DEVS + 1,
        (pltpu.VMEM((subs, SUB_DIM, n), bf16),),
    )(place, mine, *others, mats)
    recv = other_core(send)
    e_own, recv = lax.optimization_barrier((e_own, recv))
    e_oth = other_core(e_own)
    piece = shape((SUB_DIM, 2 * n), bf16)
    feats = (keep, recv, *over_x(call(join_kernel, (piece,) * 3, 0, 2)(keep, recv)))

    stats_shape = shape((SUB_DIM + 8, codes), f32)
    stats = call(first_kernel, stats_shape, 1, 6)(place, *feats, books)
    book, weights, stats = call(
        second_kernel, (shape((SUB_DIM, codes), f32), shape((4, codes, 2 * n), bf16), stats_shape), 1, 10
    )(place, *feats, books, *over_z(stats))
    book, *rebuilt = call(rebuild_kernel, (shape((SUB_DIM, codes), f32),) + (piece,) * 4, 0, 6)(
        *over_z(stats), book, weights
    )
    chunk = shape((SUB_DIM, width), f32)
    cross = call(cross_kernel, (chunk,) * 4, 0, 6)(rebuilt[0], *over_x(rebuilt[1:]), e_own, e_oth)
    got = over_x(cross[1:])
    mine = (cross[0] + got[0]) + (got[1] + got[2])
    mine = call(sum_kernel, shape((SUB_DIM, width + codes), f32), 0, 5)(*over_z(mine), book)
    v_own, low = call(
        columns_kernel, (shape((half, width + codes), f32), shape((half, width), bf16)), 1, 4
    )(place, mine, *over_x([mine] * 3))
    book_oth = other_core(v_own[:, width:])
    partner = over_sub_mirrored(low, 1)
    c_own = jnp.stack([low] + over_y(low))
    c_oth = other_core(c_own)
    z_own = jnp.stack([partner] + over_y(partner))
    z_oth = other_core(z_own)
    piece = shape((width // ROW_DEVS, half), f32)
    keep, send, new_codebooks = call(
        polar_kernel,
        (piece, piece, shape(codebooks.shape, f32)),
        1,
        6,
        (
            pltpu.VMEM((width, width), bf16),
            pltpu.VMEM((width, width), bf16),
            pltpu.VMEM((half, width), f32),
            pltpu.VMEM((128, half), f32),
        ),
    )(place, c_own, c_oth, z_own, z_oth, v_own, book_oth)
    recv = other_core(send)
    new_rotation = jnp.where(core == 0, jnp.concatenate([keep, recv], 1), jnp.concatenate([recv, keep], 1))
    return (new_codebooks, new_rotation)


def solution(mesh):
    return jax.shard_map(
        per_device,
        mesh=mesh,
        in_specs=(P("rows", "sub"), P(None, "sub"), P("sub", None, None)),
        out_specs=(P("sub", None, None), P("rows", "sub")),
        check_vma=False,
    )
```

time: 133 us -> 128 us (0.962)
  blocking collectives: 12 us -> 0 us
  starting transfers between devices: 62 us -> 68 us
  waiting for transfers between devices: 32.4 us -> 35 us
  Pallas kernels: 22.3 us -> 20.1 us
    all_to_all x1 -> x0, blocking collectives: 12 us -> none  [exchange(): return lax.all_to_all(x, 'rows', 0, 0, tiled=True, axis_index_groups=groups)]
    ppermute x17 -> x27, starting transfers between devices: 33.9 us -> 44.7 us  [permute_rows(): return lax.ppermute(x, 'rows', [(i, to(i)) for i in range(ROW_DEVS)])]
    ppermute x17 -> x27, waiting for transfers between devices: 14.1 us -> 24.7 us  [permute_rows(): return lax.ppermute(x, 'rows', [(i, to(i)) for i in range(ROW_DEVS)])]
    all_to_all x1 -> x0, waiting for transfers between devices: 8.82 us -> none  [exchange(): return lax.all_to_all(x, 'rows', 0, 0, tiled=True, axis_index_groups=groups)]
    all_to_all x1 -> x0, starting transfers between devices: 5.02 us -> none  [exchange(): return lax.all_to_all(x, 'rows', 0, 0, tiled=True, axis_index_groups=groups)]
    pallas_call x5, Pallas kernels: 16.2 us -> 13.8 us  [the longest x1 12.3 us: per_device(): call(polar_kernel, (piece, piece, shape(codebooks.shape, f32)), 1, 6, (pl...]
    ppermute x13, waiting for transfers between devices: 8.59 us -> 9.96 us  [over_sub(): return lax.ppermute(x, 'sub', [(i, i ^ k) for i in range(SUB_DEVS)])]
  transfers between devices with their start and end apart: 32 -> 41, of which waited for: 16 -> 23; matrix products, arithmetic and copies ran while one was open for 0% -> 0% of each run, Pallas kernels for 4% -> 4%
where the time goes in v3:
time: 128 us
  starting transfers between devices  68 us (53%)
  waiting for transfers between devices  35 us (27%)
  Pallas kernels  20.1 us (16%)
  local copies, waits for them, and re-layouts  2.76 us (2%)
    ppermute x27, starting transfers between devices, permute_rows(): return lax.ppermute(x, 'rows', [(i, to(i)) for i in range(ROW_DEVS)])  44.7 us
    ppermute x27, waiting for transfers between devices, permute_rows(): return lax.ppermute(x, 'rows', [(i, to(i)) for i in range(ROW_DEVS)])  24.7 us
    ppermute x13, starting transfers between devices, over_sub(): return lax.ppermute(x, 'sub', [(i, i ^ k) for i in range(SUB_DEVS)])  21.3 us
    pallas_call x1, Pallas kernels, per_device(): call(polar_kernel, (piece, piece, shape(codebooks.shape, f32)), 1, 6, (pl...  12.3 us
    ppermute x13, waiting for transfers between devices, over_sub(): return lax.ppermute(x, 'sub', [(i, i ^ k) for i in range(SUB_DEVS)])  9.96 us
    unnamed x6, local copies, waits for them, and re-layouts  2.76 us
  transfers between devices with their start and end apart: 41, of which 23 were waited for; matrix products, arithmetic and copies ran while one was open for 0% of the time, Pallas kernels for 4%

profile of v3, /device:TPU:1, one launch (start us, length us, event | category | flops | bytes accessed | tf_op | source)
XLA Modules:
  0.0 127.5 jit_solution(6466421192251499306)
XLA Ops:
  0.6 7.8 %collective-permute-start = (bf16[512,128]{1,0:T(8,128)(2,1)}, bf16[512,128]{1,0:T(8,128)(2,1)S(1)}, u32[]{:S(2)}, u32[]{:S(2)}) collective-permute-start(bf16[512,128]{1,0:T(8,128)(2,1)} %e_ref.1), channel_id=1, source_target_pairs={{0,1},{1,0},{2,3},{3,2},{4,5},{5,4},{6,7},{7,6},{8,9},{9,8},{10,11... | collective-permute-start | bytes 393224 | tf_op jit(solution)/shard_map/ppermute | solution.py:212
  9.8 2.6 %collective-permute-start.3 = (bf16[512,128]{1,0:T(8,128)(2,1)}, bf16[512,128]{1,0:T(8,128)(2,1)S(1)}, u32[]{:S(2)}, u32[]{:S(2)}) collective-permute-start(bf16[512,128]{1,0:T(8,128)(2,1)} %e_ref.1), channel_id=1, source_target_pairs={{0,4},{1,5},{2,6},{3,7},{4,0},{5,1},{6,2},{7,3},{8,12},{9,13},{10,... | collective-permute-start | bytes 393224 | tf_op jit(solution)/shard_map/ppermute | solution.py:212
  12.5 1.9 %collective-permute-start.5 = (bf16[512,128]{1,0:T(8,128)(2,1)}, bf16[512,128]{1,0:T(8,128)(2,1)S(1)}, u32[]{:S(2)}, u32[]{:S(2)}) collective-permute-start(bf16[512,128]{1,0:T(8,128)(2,1)} %e_ref.1), channel_id=1, source_target_pairs={{0,6},{1,7},{2,4},{3,5},{4,2},{5,3},{6,0},{7,1},{8,14},{9,15},{10,... | collective-permute-start | bytes 393224 | tf_op jit(solution)/shard_map/ppermute | solution.py:212
  18.9 5.4 %collective-permute-done.4.refs_5_ = bf16[512,128]{1,0:T(8,128)(2,1)S(1)} collective-permute-done((bf16[512,128]{1,0:T(8,128)(2,1)}, bf16[512,128]{1,0:T(8,128)(2,1)S(1)}, u32[]{:S(2)}, u32[]{:S(2)}) %collective-permute-start.4) | collective-permute-done | bytes 131104 | tf_op jit(solution)/shard_map/ppermute | solution.py:212
  24.3 1.7 %collective-permute-done.6.refs_7_ = bf16[512,128]{1,0:T(8,128)(2,1)S(1)} collective-permute-done((bf16[512,128]{1,0:T(8,128)(2,1)S(1)}, bf16[512,128]{1,0:T(8,128)(2,1)S(1)}, u32[]{:S(2)}, u32[]{:S(2)}) %collective-permute-start.6) | collective-permute-done | bytes 131104 | tf_op jit(solution)/shard_map/ppermute | solution.py:212
  30.0 2.6 %collective-permute-start.10 = (bf16[16,1024]{1,0:T(8,128)(2,1)S(1)}, bf16[16,1024]{1,0:T(8,128)(2,1)S(1)}, u32[]{:S(2)}, u32[]{:S(2)}) collective-permute-start(bf16[16,1024]{1,0:T(8,128)(2,1)S(1)} %get-tuple-element.38), channel_id=1, source_target_pairs={{0,48},{8,56},{16,32},{24,40},{32,16},{40,24},{48,0},{56,8},{64,11... | collective-permute-start | bytes 98312 | tf_op jit(solution)/shard_map/ppermute | solution.py:42
  36.8 2.2 %shard_map.53.a = f32[24,256]{1,0:T(8,128)S(1)} custom-call(s32[4]{0:T(128)S(1)} %pad_add_fusion.place_ref, bf16[4,16,512]{2,1,0:T(8,128)(2,1)S(1)} %get-tuple-element.32.keep_ref.k, bf16[4,16,512]{2,1,0:T(8,128)(2,1)S(1)} %collective-permute-done.7.recv_ref.r, bf16[16,1024]{1,0:T(8,128)(2,1)S(1)} %collective-permute-done.8.f1, ...), custom_call_target="tpu_custom_call" | custom-call | tf_op jit(solution)/shard_map/pallas_call | solution.py:272
  44.2 2.6 %collective-permute-done.13.d = f32[24,256]{1,0:T(8,128)S(1)} collective-permute-done((f32[24,256]{1,0:T(8,128)S(1)}, f32[24,256]{1,0:T(8,128)S(1)}, u32[]{:S(2)}, u32[]{:S(2)}) %collective-permute-start.13) | collective-permute-done | bytes 24608 | tf_op jit(solution)/shard_map/ppermute | solution.py:42
  46.8 2.3 %shard_map.54 = (f32[16,256]{1,0:T(8,128)S(1)}, bf16[4,256,1024]{2,1,0:T(8,128)(2,1)S(1)}, f32[24,256]{1,0:T(8,128)S(1)}) custom-call(s32[4]{0:T(128)S(1)} %pad_add_fusion.place_ref, bf16[4,16,512]{2,1,0:T(8,128)(2,1)S(1)} %get-tuple-element.32.keep_ref.k, bf16[4,16,512]{2,1,0:T(8,128)(2,1)S(1)} %collective-permute-done.7.recv_ref.r, ...), custom_call_target="tpu_custom_call" | custom-call | tf_op jit(solution)/shard_map/pallas_call | solution.py:273
  50.1 2.8 %collective-permute-start.16 = (f32[24,256]{1,0:T(8,128)S(1)}, f32[24,256]{1,0:T(8,128)S(1)}, u32[]{:S(2)}, u32[]{:S(2)}) collective-permute-start(f32[24,256]{1,0:T(8,128)S(1)} %get-tuple-element.40.a), channel_id=1, source_target_pairs={{0,192},{8,200},{16,208},{24,216},{32,224},{40,232},{48,240},{56,2... | collective-permute-start | bytes 73736 | tf_op jit(solution)/shard_map/ppermute | solution.py:42
  53.0 1.8 %collective-permute-done.16.d = f32[24,256]{1,0:T(8,128)S(1)} collective-permute-done((f32[24,256]{1,0:T(8,128)S(1)}, f32[24,256]{1,0:T(8,128)S(1)}, u32[]{:S(2)}, u32[]{:S(2)}) %collective-permute-start.16) | collective-permute-done | bytes 24608 | tf_op jit(solution)/shard_map/ppermute | solution.py:42
  57.4 1.8 %collective-permute-start.19 = (bf16[16,1024]{1,0:T(8,128)(2,1)S(1)}, bf16[16,1024]{1,0:T(8,128)(2,1)S(1)}, u32[]{:S(2)}, u32[]{:S(2)}) collective-permute-start(bf16[16,1024]{1,0:T(8,128)(2,1)S(1)} %get-tuple-element.46), channel_id=1, source_target_pairs={{0,48},{8,56},{16,32},{24,40},{32,16},{40,24},{48,0},{56,8},{64,11... | collective-permute-start | bytes 98312 | tf_op jit(solution)/shard_map/ppermute | solution.py:42
  59.2 1.8 %collective-permute-done.18.x2 = bf16[16,1024]{1,0:T(8,128)(2,1)S(1)} collective-permute-done((bf16[16,1024]{1,0:T(8,128)(2,1)S(1)}, bf16[16,1024]{1,0:T(8,128)(2,1)S(1)}, u32[]{:S(2)}, u32[]{:S(2)}) %collective-permute-start.18) | collective-permute-done | bytes 32800 | tf_op jit(solution)/shard_map/ppermute | solution.py:42
  62.0 2.9 %collective-permute-start.22 = (f32[16,1024]{1,0:T(8,128)S(1)}, f32[16,1024]{1,0:T(8,128)S(1)}, u32[]{:S(2)}, u32[]{:S(2)}) collective-permute-start(f32[16,1024]{1,0:T(8,128)S(1)} %get-tuple-element.50), channel_id=1, source_target_pairs={{0,32},{8,40},{16,48},{24,56},{32,0},{40,8},{48,16},{56,24},{64,96... | collective-permute-start | bytes 196616 | tf_op jit(solution)/shard_map/ppermute | solution.py:42
  65.9 1.9 %collective-permute-done.22 = f32[16,1024]{1,0:T(8,128)S(1)} collective-permute-done((f32[16,1024]{1,0:T(8,128)S(1)}, f32[16,1024]{1,0:T(8,128)S(1)}, u32[]{:S(2)}, u32[]{:S(2)}) %collective-permute-start.22) | collective-permute-done | bytes 65568 | tf_op jit(solution)/shard_map/ppermute | solution.py:42
  69.4 2.9 %collective-permute-start.25 = (f32[16,1024]{1,0:T(8,128)S(1)}, f32[16,1024]{1,0:T(8,128)S(1)}, u32[]{:S(2)}, u32[]{:S(2)}) collective-permute-start(f32[16,1024]{1,0:T(8,128)S(1)} %add_add_fusion.a), channel_id=1, source_target_pairs={{0,128},{8,136},{16,144},{24,152},{32,160},{40,168},{48,176},{56,1... | collective-permute-start | bytes 196616 | tf_op jit(solution)/shard_map/ppermute | solution.py:42
  74.2 3.0 %collective-permute-done.26.d = f32[16,1024]{1,0:T(8,128)S(1)} collective-permute-done((f32[16,1024]{1,0:T(8,128)S(1)}, f32[16,1024]{1,0:T(8,128)S(1)}, u32[]{:S(2)}, u32[]{:S(2)}) %collective-permute-start.26) | collective-permute-done | bytes 65568 | tf_op jit(solution)/shard_map/ppermute | solution.py:42
  77.3 2.0 %collective-permute-start.28 = (f32[16,1280]{1,0:T(8,128)S(1)}, f32[16,1280]{1,0:T(8,128)S(1)}, u32[]{:S(2)}, u32[]{:S(2)}) collective-permute-start(f32[16,1280]{1,0:T(8,128)S(1)} %shard_map.57.x0), channel_id=1, source_target_pairs={{0,32},{8,40},{16,48},{24,56},{32,0},{40,8},{48,16},{56,24},{64,96... | collective-permute-start | bytes 245768 | tf_op jit(solution)/shard_map/ppermute | solution.py:42
  79.3 1.8 %collective-permute-start.29 = (f32[16,1280]{1,0:T(8,128)S(1)}, f32[16,1280]{1,0:T(8,128)S(1)}, u32[]{:S(2)}, u32[]{:S(2)}) collective-permute-start(f32[16,1280]{1,0:T(8,128)S(1)} %shard_map.57.x0), channel_id=1, source_target_pairs={{0,48},{8,56},{16,32},{24,40},{32,16},{40,24},{48,0},{56,8},{64,11... | collective-permute-start | bytes 245768 | tf_op jit(solution)/shard_map/ppermute | solution.py:42
  84.5 1.9 %collective-permute-start.34 = (bf16[64,1024]{1,0:T(8,128)(2,1)S(1)}, bf16[64,1024]{1,0:T(8,128)(2,1)S(1)}, u32[]{:S(2)}, u32[]{:S(2)}) collective-permute-start(bf16[64,1024]{1,0:T(8,128)(2,1)S(1)} %get-tuple-element.53), channel_id=1, source_target_pairs={{0,193},{1,192},{2,195},{3,194},{4,197},{5,196},{6,199},{7,198},{8... | collective-permute-start | bytes 393224 | tf_op jit(solution)/shard_map/ppermute | solution.py:225
  86.4 3.1 %collective-permute-start.31 = (bf16[64,1024]{1,0:T(8,128)(2,1)S(1)}, bf16[64,1024]{1,0:T(8,128)(2,1)S(1)}, u32[]{:S(2)}, u32[]{:S(2)}) collective-permute-start(bf16[64,1024]{1,0:T(8,128)(2,1)S(1)} %get-tuple-element.53), channel_id=1, source_target_pairs={{0,4},{1,5},{2,6},{3,7},{4,0},{5,1},{6,2},{7,3},{8,12},{9,13},{10,... | collective-permute-start | bytes 393224 | tf_op jit(solution)/shard_map/ppermute | solution.py:212
  93.5 2.6 %collective-permute-done.32 = bf16[64,1024]{1,0:T(8,128)(2,1)S(1)} collective-permute-done((bf16[64,1024]{1,0:T(8,128)(2,1)S(1)}, bf16[64,1024]{1,0:T(8,128)(2,1)S(1)}, u32[]{:S(2)}, u32[]{:S(2)}) %collective-permute-start.32) | collective-permute-done | bytes 131104 | tf_op jit(solution)/shard_map/ppermute | solution.py:212
  96.1 14.1 %collective-permute-start.33 = (bf16[4,64,1024]{2,1,0:T(8,128)(2,1)S(1)}, bf16[4,64,1024]{2,1,0:T(8,128)(2,1)S(1)}, u32[]{:S(2)}, u32[]{:S(2)}) collective-permute-start(bf16[4,64,1024]{2,1,0:T(8,128)(2,1)S(1)} %pad_maximum_fusion.c0), channel_id=1, source_target_pairs={{0,8},{8,0},{16,24},{24,16},{32,40},{40,32},{48,56},{56,48},{64,72... | collective-permute-start | bytes 1572872 | tf_op jit(solution)/shard_map/ppermute | solution.py:42
  113.3 12.3 %shard_map.59 = (f32[32,64]{1,0:T(8,128)S(1)}, f32[32,64]{1,0:T(8,128)S(1)}, f32[8,16,256]{2,1,0:T(8,128)}) custom-call(s32[4]{0:T(128)S(1)} %pad_add_fusion.place_ref, bf16[4,64,1024]{2,1,0:T(8,128)(2,1)S(1)} %pad_maximum_fusion.c0, bf16[4,64,1024]{2,1,0:T(8,128)(2,1)S(1)} %collective-permute-done.33.c1, bf16[4,64,1024]{2,1,0:T(8,128)(2,1)S(1)} %pad_maximum_fusion.1.c2, ...), custom_call_target="tpu_custom_call" | custom-call | tf_op jit(solution)/shard_map/pallas_call | solution.py:294
  (80 shorter events, 40.9 us)
Async XLA Ops:
  0.6 13.8 %collective-permute-start = (bf16[512,128]{1,0:T(8,128)(2,1)}, bf16[512,128]{1,0:T(8,128)(2,1)S(1)}, u32[]{:S(2)}, u32[]{:S(2)}) collective-permute-start(bf16[512,128]{1,0:T(8,128)(2,1)} %e_ref.1), channel_id=1, source_target_pairs={{0,1},{1,0},{2,3},{3,2},{4,5},{5,4},{6,7},{7,6},{8,9},{9,8},{10,11... | collective-permute-start | bytes 393224 | tf_op jit(solution)/shard_map/ppermute | solution.py:212
  8.5 6.4 %collective-permute-start.1 = (bf16[512,128]{1,0:T(8,128)(2,1)}, bf16[512,128]{1,0:T(8,128)(2,1)S(1)}, u32[]{:S(2)}, u32[]{:S(2)}) collective-permute-start(bf16[512,128]{1,0:T(8,128)(2,1)} %e_ref.1), channel_id=1, source_target_pairs={{0,2},{1,3},{2,0},{3,1},{4,6},{5,7},{6,4},{7,5},{8,10},{9,11},{10,... | collective-permute-start | bytes 393224 | tf_op jit(solution)/shard_map/ppermute | solution.py:212
  9.8 9.1 %collective-permute-start.3 = (bf16[512,128]{1,0:T(8,128)(2,1)}, bf16[512,128]{1,0:T(8,128)(2,1)S(1)}, u32[]{:S(2)}, u32[]{:S(2)}) collective-permute-start(bf16[512,128]{1,0:T(8,128)(2,1)} %e_ref.1), channel_id=1, source_target_pairs={{0,4},{1,5},{2,6},{3,7},{4,0},{5,1},{6,2},{7,3},{8,12},{9,13},{10,... | collective-permute-start | bytes 393224 | tf_op jit(solution)/shard_map/ppermute | solution.py:212
  12.4 12.0 %collective-permute-start.4 = (bf16[512,128]{1,0:T(8,128)(2,1)}, bf16[512,128]{1,0:T(8,128)(2,1)S(1)}, u32[]{:S(2)}, u32[]{:S(2)}) collective-permute-start(bf16[512,128]{1,0:T(8,128)(2,1)} %e_ref.1), channel_id=1, source_target_pairs={{0,5},{1,4},{2,7},{3,6},{4,1},{5,0},{6,3},{7,2},{8,13},{9,12},{10,... | collective-permute-start | bytes 393224 | tf_op jit(solution)/shard_map/ppermute | solution.py:212
  12.5 11.8 %collective-permute-start.5 = (bf16[512,128]{1,0:T(8,128)(2,1)}, bf16[512,128]{1,0:T(8,128)(2,1)S(1)}, u32[]{:S(2)}, u32[]{:S(2)}) collective-permute-start(bf16[512,128]{1,0:T(8,128)(2,1)} %e_ref.1), channel_id=1, source_target_pairs={{0,6},{1,7},{2,4},{3,5},{4,2},{5,3},{6,0},{7,1},{8,14},{9,15},{10,... | collective-permute-start | bytes 393224 | tf_op jit(solution)/shard_map/ppermute | solution.py:212
  14.4 9.9 %collective-permute-start.2 = (bf16[512,128]{1,0:T(8,128)(2,1)S(1)}, bf16[512,128]{1,0:T(8,128)(2,1)S(1)}, u32[]{:S(2)}, u32[]{:S(2)}) collective-permute-start(bf16[512,128]{1,0:T(8,128)(2,1)S(1)} %collective-permute-done.refs_1_), channel_id=1, source_target_pairs={{0,2},{1,3},{2,0},{3,1},{4,6},{5,7},{6,4},{7,5},{8,10},{9,11},{10,... | collective-permute-start | bytes 393224 | tf_op jit(solution)/shard_map/ppermute | solution.py:212
  14.8 11.2 %collective-permute-start.6 = (bf16[512,128]{1,0:T(8,128)(2,1)S(1)}, bf16[512,128]{1,0:T(8,128)(2,1)S(1)}, u32[]{:S(2)}, u32[]{:S(2)}) collective-permute-start(bf16[512,128]{1,0:T(8,128)(2,1)S(1)} %collective-permute-done.refs_1_), channel_id=1, source_target_pairs={{0,6},{1,7},{2,4},{3,5},{4,2},{5,3},{6,0},{7,1},{8,14},{9,15},{10,... | collective-permute-start | bytes 393224 | tf_op jit(solution)/shard_map/ppermute | solution.py:212
  29.6 31.8 %collective-permute-start.20 = (bf16[512,1024]{1,0:T(8,128)(2,1)S(1)}, bf16[512,1024]{1,0:T(8,128)(2,1)S(1)}, u32[]{:S(2)}, u32[]{:S(2)}) collective-permute-start(bf16[512,1024]{1,0:T(8,128)(2,1)S(1)} %get-tuple-element.47.own_ref), channel_id=1, source_target_pairs={{0,8},{8,0},{16,24},{24,16},{32,40},{40,32},{48,56},{56,48},{64,72... | collective-permute-start | bytes 3145736 | tf_op jit(solution)/shard_map/ppermute | solution.py:42
  41.9 4.8 %collective-permute-start.13 = (f32[24,256]{1,0:T(8,128)S(1)}, f32[24,256]{1,0:T(8,128)S(1)}, u32[]{:S(2)}, u32[]{:S(2)}) collective-permute-start(f32[24,256]{1,0:T(8,128)S(1)} %shard_map.53.a), channel_id=1, source_target_pairs={{0,192},{8,200},{16,208},{24,216},{32,224},{40,232},{48,240},{56,2... | collective-permute-start | bytes 73736 | tf_op jit(solution)/shard_map/ppermute | solution.py:42
  50.1 4.7 %collective-permute-start.16 = (f32[24,256]{1,0:T(8,128)S(1)}, f32[24,256]{1,0:T(8,128)S(1)}, u32[]{:S(2)}, u32[]{:S(2)}) collective-permute-start(f32[24,256]{1,0:T(8,128)S(1)} %get-tuple-element.40.a), channel_id=1, source_target_pairs={{0,192},{8,200},{16,208},{24,216},{32,224},{40,232},{48,240},{56,2... | collective-permute-start | bytes 73736 | tf_op jit(solution)/shard_map/ppermute | solution.py:42
  62.0 5.7 %collective-permute-start.22 = (f32[16,1024]{1,0:T(8,128)S(1)}, f32[16,1024]{1,0:T(8,128)S(1)}, u32[]{:S(2)}, u32[]{:S(2)}) collective-permute-start(f32[16,1024]{1,0:T(8,128)S(1)} %get-tuple-element.50), channel_id=1, source_target_pairs={{0,32},{8,40},{16,48},{24,56},{32,0},{40,8},{48,16},{56,24},{64,96... | collective-permute-start | bytes 196616 | tf_op jit(solution)/shard_map/ppermute | solution.py:42
  64.9 4.3 %collective-permute-start.23 = (f32[16,1024]{1,0:T(8,128)S(1)}, f32[16,1024]{1,0:T(8,128)S(1)}, u32[]{:S(2)}, u32[]{:S(2)}) collective-permute-start(f32[16,1024]{1,0:T(8,128)S(1)} %get-tuple-element.51), channel_id=1, source_target_pairs={{0,48},{8,56},{16,32},{24,40},{32,16},{40,24},{48,0},{56,8},{64,11... | collective-permute-start | bytes 196616 | tf_op jit(solution)/shard_map/ppermute | solution.py:42
  69.4 4.8 %collective-permute-start.25 = (f32[16,1024]{1,0:T(8,128)S(1)}, f32[16,1024]{1,0:T(8,128)S(1)}, u32[]{:S(2)}, u32[]{:S(2)}) collective-permute-start(f32[16,1024]{1,0:T(8,128)S(1)} %add_add_fusion.a), channel_id=1, source_target_pairs={{0,128},{8,136},{16,144},{24,152},{32,160},{40,168},{48,176},{56,1... | collective-permute-start | bytes 196616 | tf_op jit(solution)/shard_map/ppermute | solution.py:42
  72.3 4.9 %collective-permute-start.26 = (f32[16,1024]{1,0:T(8,128)S(1)}, f32[16,1024]{1,0:T(8,128)S(1)}, u32[]{:S(2)}, u32[]{:S(2)}) collective-permute-start(f32[16,1024]{1,0:T(8,128)S(1)} %add_add_fusion.a), channel_id=1, source_target_pairs={{0,192},{8,200},{16,208},{24,216},{32,224},{40,232},{48,240},{56,2... | collective-permute-start | bytes 196616 | tf_op jit(solution)/shard_map/ppermute | solution.py:42
  77.3 4.9 %collective-permute-start.28 = (f32[16,1280]{1,0:T(8,128)S(1)}, f32[16,1280]{1,0:T(8,128)S(1)}, u32[]{:S(2)}, u32[]{:S(2)}) collective-permute-start(f32[16,1280]{1,0:T(8,128)S(1)} %shard_map.57.x0), channel_id=1, source_target_pairs={{0,32},{8,40},{16,48},{24,56},{32,0},{40,8},{48,16},{56,24},{64,96... | collective-permute-start | bytes 245768 | tf_op jit(solution)/shard_map/ppermute | solution.py:42
  79.3 4.5 %collective-permute-start.29 = (f32[16,1280]{1,0:T(8,128)S(1)}, f32[16,1280]{1,0:T(8,128)S(1)}, u32[]{:S(2)}, u32[]{:S(2)}) collective-permute-start(f32[16,1280]{1,0:T(8,128)S(1)} %shard_map.57.x0), channel_id=1, source_target_pairs={{0,48},{8,56},{16,32},{24,40},{32,16},{40,24},{48,0},{56,8},{64,11... | collective-permute-start | bytes 245768 | tf_op jit(solution)/shard_map/ppermute | solution.py:42
  84.5 6.1 %collective-permute-start.34 = (bf16[64,1024]{1,0:T(8,128)(2,1)S(1)}, bf16[64,1024]{1,0:T(8,128)(2,1)S(1)}, u32[]{:S(2)}, u32[]{:S(2)}) collective-permute-start(bf16[64,1024]{1,0:T(8,128)(2,1)S(1)} %get-tuple-element.53), channel_id=1, source_target_pairs={{0,193},{1,192},{2,195},{3,194},{4,197},{5,196},{6,199},{7,198},{8... | collective-permute-start | bytes 393224 | tf_op jit(solution)/shard_map/ppermute | solution.py:225
  86.4 6.4 %collective-permute-start.30 = (bf16[64,1024]{1,0:T(8,128)(2,1)S(1)}, bf16[64,1024]{1,0:T(8,128)(2,1)S(1)}, u32[]{:S(2)}, u32[]{:S(2)}) collective-permute-start(bf16[64,1024]{1,0:T(8,128)(2,1)S(1)} %get-tuple-element.53), channel_id=1, source_target_pairs={{0,2},{1,3},{2,0},{3,1},{4,6},{5,7},{6,4},{7,5},{8,10},{9,11},{10,... | collective-permute-start | bytes 393224 | tf_op jit(solution)/shard_map/ppermute | solution.py:212
  86.4 7.0 %collective-permute-start.31 = (bf16[64,1024]{1,0:T(8,128)(2,1)S(1)}, bf16[64,1024]{1,0:T(8,128)(2,1)S(1)}, u32[]{:S(2)}, u32[]{:S(2)}) collective-permute-start(bf16[64,1024]{1,0:T(8,128)(2,1)S(1)} %get-tuple-element.53), channel_id=1, source_target_pairs={{0,4},{1,5},{2,6},{3,7},{4,0},{5,1},{6,2},{7,3},{8,12},{9,13},{10,... | collective-permute-start | bytes 393224 | tf_op jit(solution)/shard_map/ppermute | solution.py:212
  89.5 6.6 %collective-permute-start.32 = (bf16[64,1024]{1,0:T(8,128)(2,1)S(1)}, bf16[64,1024]{1,0:T(8,128)(2,1)S(1)}, u32[]{:S(2)}, u32[]{:S(2)}) collective-permute-start(bf16[64,1024]{1,0:T(8,128)(2,1)S(1)} %get-tuple-element.53), channel_id=1, source_target_pairs={{0,6},{1,7},{2,4},{3,5},{4,2},{5,3},{6,0},{7,1},{8,14},{9,15},{10,... | collective-permute-start | bytes 393224 | tf_op jit(solution)/shard_map/ppermute | solution.py:212
  90.6 19.7 %collective-permute-start.36 = (bf16[64,1024]{1,0:T(8,128)(2,1)S(1)}, bf16[64,1024]{1,0:T(8,128)(2,1)S(1)}, u32[]{:S(2)}, u32[]{:S(2)}) collective-permute-start(bf16[64,1024]{1,0:T(8,128)(2,1)S(1)} %collective-permute-done.34), channel_id=1, source_target_pairs={{0,4},{1,5},{2,6},{3,7},{4,0},{5,1},{6,2},{7,3},{8,12},{9,13},{10,... | collective-permute-start | bytes 393224 | tf_op jit(solution)/shard_map/ppermute | solution.py:212
  91.3 18.9 %collective-permute-start.37 = (bf16[64,1024]{1,0:T(8,128)(2,1)S(1)}, bf16[64,1024]{1,0:T(8,128)(2,1)S(1)}, u32[]{:S(2)}, u32[]{:S(2)}) collective-permute-start(bf16[64,1024]{1,0:T(8,128)(2,1)S(1)} %collective-permute-done.34), channel_id=1, source_target_pairs={{0,6},{1,7},{2,4},{3,5},{4,2},{5,3},{6,0},{7,1},{8,14},{9,15},{10,... | collective-permute-start | bytes 393224 | tf_op jit(solution)/shard_map/ppermute | solution.py:212
  92.8 17.5 %collective-permute-start.35 = (bf16[64,1024]{1,0:T(8,128)(2,1)S(1)}, bf16[64,1024]{1,0:T(8,128)(2,1)S(1)}, u32[]{:S(2)}, u32[]{:S(2)}) collective-permute-start(bf16[64,1024]{1,0:T(8,128)(2,1)S(1)} %collective-permute-done.34), channel_id=1, source_target_pairs={{0,2},{1,3},{2,0},{3,1},{4,6},{5,7},{6,4},{7,5},{8,10},{9,11},{10,... | collective-permute-start | bytes 393224 | tf_op jit(solution)/shard_map/ppermute | solution.py:212
  96.1 17.2 %collective-permute-start.33 = (bf16[4,64,1024]{2,1,0:T(8,128)(2,1)S(1)}, bf16[4,64,1024]{2,1,0:T(8,128)(2,1)S(1)}, u32[]{:S(2)}, u32[]{:S(2)}) collective-permute-start(bf16[4,64,1024]{2,1,0:T(8,128)(2,1)S(1)} %pad_maximum_fusion.c0), channel_id=1, source_target_pairs={{0,8},{8,0},{16,24},{24,16},{32,40},{40,32},{48,56},{56,48},{64,72... | collective-permute-start | bytes 1572872 | tf_op jit(solution)/shard_map/ppermute | solution.py:42
  (20 other events, 60.9 us)

commit v4 on v3

--- a/solution.py
+++ b/solution.py
@@ -13,6 +13,8 @@
 
 ROW_DEVS = 32
 SUB_DEVS = 8
+ORDER = (0, 2, 3, 1)
+BLOCKS = (0, 1, 4, 5, 6, 7, 2, 3)
 
 f32 = jnp.float32
 bf16 = jnp.bfloat16
@@ -49,7 +51,7 @@
 def load_kernel(place_ref, r_ref, e_ref, book_ref, r_out, e_out, book_out):
     n = e_ref.shape[1]
     for k in range(SUB_DEVS):
-        r_out[n * k : n * (k + 1)] = r_ref[pl.ds(pl.multiple_of((place_ref[3] ^ k) * n, n), n)]
+        r_out[n * k : n * (k + 1)] = r_ref[pl.ds(pl.multiple_of((place_ref[3] ^ BLOCKS[k]) * n, n), n)]
     e_out[...] = e_ref[...]
     book_out[...] = book_ref[...]
 
@@ -63,9 +65,9 @@
     for m in range(rot_ref.shape[0]):
         rot_ref[m] = rot[SUB_DIM * m : SUB_DIM * (m + 1)]
     core, x = place_ref[0], place_ref[1]
-    for d in range(4):
-        keep_ref[d] = rot_ref[4 * core + (x ^ d)]
-        send_ref[d] = rot_ref[4 * (1 - core) + (x ^ d)]
+    for j in range(4):
+        keep_ref[j] = rot_ref[4 * core + (x ^ ORDER[j])]
+        send_ref[j] = rot_ref[4 * (1 - core) + (x ^ ORDER[j])]
 
 
 def join_kernel(keep_ref, recv_ref, *outs):
@@ -150,17 +152,26 @@
     width = low_ref.shape[1]
     n = width // SUB_DEVS
     for d, x in enumerate((x0, x1, x2, x3)):
-        rows = pl.ds(pl.multiple_of((place_ref[1] ^ d) * SUB_DIM, SUB_DIM), SUB_DIM)
+        rows = pl.ds(pl.multiple_of((place_ref[1] ^ ORDER[d]) * SUB_DIM, SUB_DIM), SUB_DIM)
         for k in range(SUB_DEVS):
-            at = pl.ds(pl.multiple_of((place_ref[3] ^ k) * n, n), n)
+            at = pl.ds(pl.multiple_of((place_ref[3] ^ BLOCKS[k]) * n, n), n)
             block = x[:, n * k : n * (k + 1)]
             v_ref[rows, at] = block
             low_ref[rows, at] = block.astype(bf16)
         v_ref[rows, width:] = x[:, width:]
 
 
+def pack_kernel(*refs):
+    for i, ref in enumerate(refs[:-1]):
+        refs[-1][i] = ref[...]
+
+
+def pack(xs):
+    return call(pack_kernel, shape((len(xs),) + xs[0].shape, xs[0].dtype), 0, len(xs))(*xs)
+
+
 def polar_kernel(
-    place_ref, c0, c1, c2, c3, v_ref, book_ref, keep_ref, send_ref, book_out, hi_ref, lo_ref, all_ref, block_ref
+    place_ref, c0, c1, c2, c3, v_ref, book_ref, keep_ref, send_ref, book_out, parts_ref, all_ref, block_ref
 ):
     rows, width = all_ref.shape
     core = place_ref[0]
@@ -170,7 +181,7 @@
         book_out[4 * core + x] = v_ref[at, width:]
         book_out[4 * (1 - core) + x] = book_ref[at]
     cols = jnp.concatenate([c[...].reshape(-1, width) for c in (c0, c1, c2, c3)], axis=0)
-    gram = dot(cols, cols, ((0,), (0,)))
+    gram = dot(cols.T, cols)
     eye = lax.broadcasted_iota(jnp.int32, (n, n), 0) == lax.broadcasted_iota(jnp.int32, (n, n), 1)
     diag = jnp.zeros((n, n), f32)
     for i in range(0, width, n):
@@ -178,15 +189,15 @@
     square = jnp.sum(jnp.sum(diag, axis=0, keepdims=True), axis=1, keepdims=True) + 1e-06
     gram = gram * (1.0 / square)
     hi = gram.astype(bf16)
-    hi_ref[...] = hi
-    lo_ref[...] = (gram - hi.astype(f32)).astype(bf16)
+    parts_ref[:, :width] = hi
+    parts_ref[:, width:] = (gram - hi.astype(f32)).astype(bf16)
 
     def times_gram(v):
         v_hi = v.astype(bf16)
         v_lo = (v - v_hi.astype(f32)).astype(bf16)
-        n = v.shape[0]
-        both = dot(jnp.concatenate([v_hi, v_lo], axis=0), hi_ref[...])
-        return both[:n] + (both[n:] + dot(v_hi, lo_ref[...]))
+        m = v.shape[0]
+        out = dot(jnp.concatenate([v_hi, v_lo], axis=0), parts_ref[...])
+        return out[:m, :width] + (out[m:, :width] + out[:m, width:])
 
     def quintic(v):
         image = times_gram(v)
@@ -213,7 +224,7 @@
 
 
 def over_y(x):
-    return [over_sub(x, 2 * d) for d in (1, 2, 3)]
+    return [over_sub(x, 2 * d) for d in ORDER[1:]]
 
 
 def over_sub_mirrored(x, k):
@@ -229,15 +240,15 @@
     partner = across(x, 1)
     y = over_y(x)
     far = across(x, 5)
-    return [partner, y[0], over_sub(partner, 2), y[1], far, y[2], over_sub(partner, 6)]
+    return [partner, y[0], far, y[1], over_sub(partner, 6), y[2], over_sub(partner, 2)]
 
 
 def over_z(x):
-    return [x] + [permute_rows(x, lambda i, d=d: i ^ (8 * d)) for d in (1, 2, 3)]
+    return [x] + [permute_rows(x, lambda i, d=d: i ^ (8 * d)) for d in ORDER[1:]]
 
 
 def over_x(xs):
-    return [permute_rows(x, lambda i, d=d: i ^ (2 * d)) for d, x in zip((1, 2, 3), xs)]
+    return [permute_rows(x, lambda i, d=d: i ^ (2 * d)) for d, x in zip(ORDER[1:], xs)]
 
 
 def per_device(embeddings, rotation, codebooks):
@@ -286,9 +297,9 @@
     )(place, mine, *over_x([mine] * 3))
     book_oth = other_core(v_own[:, width:])
     partner = over_sub_mirrored(low, 1)
-    c_own = jnp.stack([low] + over_y(low))
+    c_own = pack([low] + over_y(low))
     c_oth = other_core(c_own)
-    z_own = jnp.stack([partner] + over_y(partner))
+    z_own = pack([partner] + over_y(partner))
     z_oth = other_core(z_own)
     piece = shape((width // ROW_DEVS, half), f32)
     keep, send, new_codebooks = call(
@@ -297,8 +308,7 @@
         1,
         6,
         (
-            pltpu.VMEM((width, width), bf16),
-            pltpu.VMEM((width, width), bf16),
+            pltpu.VMEM((width, 2 * width), bf16),
             pltpu.VMEM((half, width), f32),
             pltpu.VMEM((128, half), f32),
         ),

time: 128 us -> 123 us (0.961)
  starting transfers between devices: 68 us -> 64.8 us
    ppermute x27, starting transfers between devices: 44.7 us -> 40.9 us  [permute_rows(): return lax.ppermute(x, 'rows', [(i, to(i)) for i in range(ROW_DEVS)])]
    ppermute x1, starting transfers between devices: 1.93 us -> 3.68 us  [over_sub_mirrored(): return lax.ppermute(x, ('rows', 'sub'), pairs)]
  transfers between devices with their start and end apart: 41 -> 41, of which waited for: 23 -> 22; matrix products, arithmetic and copies ran while one was open for 0% -> 0% of each run, Pallas kernels for 4% -> 5%
where the time goes in v4:
time: 123 us; the launch traced here: 122 us
  starting transfers between devices  64.8 us (53%)
  waiting for transfers between devices  34.1 us (28%)
  Pallas kernels  19.3 us (16%)
  local copies, waits for them, and re-layouts  2.76 us (2%)
    ppermute x27, starting transfers between devices, permute_rows(): return lax.ppermute(x, 'rows', [(i, to(i)) for i in range(ROW_DEVS)])  40.9 us
    ppermute x27, waiting for transfers between devices, permute_rows(): return lax.ppermute(x, 'rows', [(i, to(i)) for i in range(ROW_DEVS)])  23.8 us
    ppermute x13, starting transfers between devices, over_sub(): return lax.ppermute(x, 'sub', [(i, i ^ k) for i in range(SUB_DEVS)])  20.2 us
    pallas_call x1, Pallas kernels, per_device(): call(polar_kernel, (piece, piece, shape(codebooks.shape, f32)), 1, 6, (pl...  11.5 us
    ppermute x13, waiting for transfers between devices, over_sub(): return lax.ppermute(x, 'sub', [(i, i ^ k) for i in range(SUB_DEVS)])  8.88 us
    ppermute x1, starting transfers between devices, over_sub_mirrored(): return lax.ppermute(x, ('rows', 'sub'), pairs)  3.68 us
    unnamed x6, local copies, waits for them, and re-layouts  2.76 us
  transfers between devices with their start and end apart: 41, of which 22 were waited for; matrix products, arithmetic and copies ran while one was open for 0% of the time, Pallas kernels for 5%

profile of v4, /device:TPU:1, one launch (start us, length us, event | category | flops | bytes accessed | tf_op | source)
XLA Modules:
  0.0 122.4 jit_solution(12580629986586602688)
XLA Ops:
  0.6 7.8 %collective-permute-start = (bf16[512,128]{1,0:T(8,128)(2,1)}, bf16[512,128]{1,0:T(8,128)(2,1)S(1)}, u32[]{:S(2)}, u32[]{:S(2)}) collective-permute-start(bf16[512,128]{1,0:T(8,128)(2,1)} %e_ref.1), channel_id=1, source_target_pairs={{0,1},{1,0},{2,3},{3,2},{4,5},{5,4},{6,7},{7,6},{8,9},{9,8},{10,11... | collective-permute-start | bytes 393224 | tf_op jit(solution)/shard_map/ppermute | solution.py:223
  8.5 2.9 %collective-permute-start.1 = (bf16[512,128]{1,0:T(8,128)(2,1)}, bf16[512,128]{1,0:T(8,128)(2,1)S(1)}, u32[]{:S(2)}, u32[]{:S(2)}) collective-permute-start(bf16[512,128]{1,0:T(8,128)(2,1)} %e_ref.1), channel_id=1, source_target_pairs={{0,4},{1,5},{2,6},{3,7},{4,0},{5,1},{6,2},{7,3},{8,12},{9,13},{10,... | collective-permute-start | bytes 393224 | tf_op jit(solution)/shard_map/ppermute | solution.py:223
  11.4 2.6 %collective-permute-start.3 = (bf16[512,128]{1,0:T(8,128)(2,1)}, bf16[512,128]{1,0:T(8,128)(2,1)S(1)}, u32[]{:S(2)}, u32[]{:S(2)}) collective-permute-start(bf16[512,128]{1,0:T(8,128)(2,1)} %e_ref.1), channel_id=1, source_target_pairs={{0,6},{1,7},{2,4},{3,5},{4,2},{5,3},{6,0},{7,1},{8,14},{9,15},{10,... | collective-permute-start | bytes 393224 | tf_op jit(solution)/shard_map/ppermute | solution.py:223
  19.0 8.8 %collective-permute-done.2.refs_3_ = bf16[512,128]{1,0:T(8,128)(2,1)S(1)} collective-permute-done((bf16[512,128]{1,0:T(8,128)(2,1)}, bf16[512,128]{1,0:T(8,128)(2,1)S(1)}, u32[]{:S(2)}, u32[]{:S(2)}) %collective-permute-start.2) | collective-permute-done | bytes 131104 | tf_op jit(solution)/shard_map/ppermute | solution.py:223
  32.1 2.5 %collective-permute-start.8 = (bf16[16,1024]{1,0:T(8,128)(2,1)S(1)}, bf16[16,1024]{1,0:T(8,128)(2,1)S(1)}, u32[]{:S(2)}, u32[]{:S(2)}) collective-permute-start(bf16[16,1024]{1,0:T(8,128)(2,1)S(1)} %get-tuple-element.36), channel_id=1, source_target_pairs={{0,32},{8,40},{16,48},{24,56},{32,0},{40,8},{48,16},{56,24},{64,96... | collective-permute-start | bytes 98312 | tf_op jit(solution)/shard_map/ppermute | solution.py:44
  34.8 1.9 %collective-permute-done.8.f1 = bf16[16,1024]{1,0:T(8,128)(2,1)S(1)} collective-permute-done((bf16[16,1024]{1,0:T(8,128)(2,1)S(1)}, bf16[16,1024]{1,0:T(8,128)(2,1)S(1)}, u32[]{:S(2)}, u32[]{:S(2)}) %collective-permute-start.8) | collective-permute-done | bytes 32800 | tf_op jit(solution)/shard_map/ppermute | solution.py:44
  36.6 1.9 %collective-permute-done.9.f2 = bf16[16,1024]{1,0:T(8,128)(2,1)S(1)} collective-permute-done((bf16[16,1024]{1,0:T(8,128)(2,1)S(1)}, bf16[16,1024]{1,0:T(8,128)(2,1)S(1)}, u32[]{:S(2)}, u32[]{:S(2)}) %collective-permute-start.9) | collective-permute-done | bytes 32800 | tf_op jit(solution)/shard_map/ppermute | solution.py:44
  38.5 2.2 %shard_map.53.a = f32[24,256]{1,0:T(8,128)S(1)} custom-call(s32[4]{0:T(128)S(1)} %pad_add_fusion.place_ref, bf16[4,16,512]{2,1,0:T(8,128)(2,1)S(1)} %get-tuple-element.32.keep_ref.k, bf16[4,16,512]{2,1,0:T(8,128)(2,1)S(1)} %collective-permute-done.7.recv_ref.r, bf16[16,1024]{1,0:T(8,128)(2,1)S(1)} %collective-permute-done.8.f1, ...), custom_call_target="tpu_custom_call" | custom-call | tf_op jit(solution)/shard_map/pallas_call | solution.py:283
  45.5 2.4 %shard_map.54 = (f32[16,256]{1,0:T(8,128)S(1)}, bf16[4,256,1024]{2,1,0:T(8,128)(2,1)S(1)}, f32[24,256]{1,0:T(8,128)S(1)}) custom-call(s32[4]{0:T(128)S(1)} %pad_add_fusion.place_ref, bf16[4,16,512]{2,1,0:T(8,128)(2,1)S(1)} %get-tuple-element.32.keep_ref.k, bf16[4,16,512]{2,1,0:T(8,128)(2,1)S(1)} %collective-permute-done.7.recv_ref.r, ...), custom_call_target="tpu_custom_call" | custom-call | tf_op jit(solution)/shard_map/pallas_call | solution.py:284
  49.0 2.0 %collective-permute-start.15 = (f32[24,256]{1,0:T(8,128)S(1)}, f32[24,256]{1,0:T(8,128)S(1)}, u32[]{:S(2)}, u32[]{:S(2)}) collective-permute-start(f32[24,256]{1,0:T(8,128)S(1)} %get-tuple-element.40.a), channel_id=1, source_target_pairs={{0,192},{8,200},{16,208},{24,216},{32,224},{40,232},{48,240},{56,2... | collective-permute-start | bytes 73736 | tf_op jit(solution)/shard_map/ppermute | solution.py:44
  51.6 1.9 %collective-permute-done.15.c = f32[24,256]{1,0:T(8,128)S(1)} collective-permute-done((f32[24,256]{1,0:T(8,128)S(1)}, f32[24,256]{1,0:T(8,128)S(1)}, u32[]{:S(2)}, u32[]{:S(2)}) %collective-permute-start.15) | collective-permute-done | bytes 24608 | tf_op jit(solution)/shard_map/ppermute | solution.py:44
  56.8 1.7 %collective-permute-done.17.x1 = bf16[16,1024]{1,0:T(8,128)(2,1)S(1)} collective-permute-done((bf16[16,1024]{1,0:T(8,128)(2,1)S(1)}, bf16[16,1024]{1,0:T(8,128)(2,1)S(1)}, u32[]{:S(2)}, u32[]{:S(2)}) %collective-permute-start.17) | collective-permute-done | bytes 32800 | tf_op jit(solution)/shard_map/ppermute | solution.py:44
  60.5 2.1 %collective-permute-start.22 = (f32[16,1024]{1,0:T(8,128)S(1)}, f32[16,1024]{1,0:T(8,128)S(1)}, u32[]{:S(2)}, u32[]{:S(2)}) collective-permute-start(f32[16,1024]{1,0:T(8,128)S(1)} %get-tuple-element.50), channel_id=1, source_target_pairs={{0,48},{8,56},{16,32},{24,40},{32,16},{40,24},{48,0},{56,8},{64,11... | collective-permute-start | bytes 196616 | tf_op jit(solution)/shard_map/ppermute | solution.py:44
  62.6 1.9 %collective-permute-done.21 = f32[16,1024]{1,0:T(8,128)S(1)} collective-permute-done((f32[16,1024]{1,0:T(8,128)S(1)}, f32[16,1024]{1,0:T(8,128)S(1)}, u32[]{:S(2)}, u32[]{:S(2)}) %collective-permute-start.21) | collective-permute-done | bytes 65568 | tf_op jit(solution)/shard_map/ppermute | solution.py:44
  66.1 2.0 %collective-permute-start.25 = (f32[16,1024]{1,0:T(8,128)S(1)}, f32[16,1024]{1,0:T(8,128)S(1)}, u32[]{:S(2)}, u32[]{:S(2)}) collective-permute-start(f32[16,1024]{1,0:T(8,128)S(1)} %add_add_fusion.a), channel_id=1, source_target_pairs={{0,192},{8,200},{16,208},{24,216},{32,224},{40,232},{48,240},{56,2... | collective-permute-start | bytes 196616 | tf_op jit(solution)/shard_map/ppermute | solution.py:44
  68.4 3.0 %collective-permute-done.24.b = f32[16,1024]{1,0:T(8,128)S(1)} collective-permute-done((f32[16,1024]{1,0:T(8,128)S(1)}, f32[16,1024]{1,0:T(8,128)S(1)}, u32[]{:S(2)}, u32[]{:S(2)}) %collective-permute-start.24) | collective-permute-done | bytes 65568 | tf_op jit(solution)/shard_map/ppermute | solution.py:44
  73.0 2.0 %collective-permute-start.28 = (f32[16,1280]{1,0:T(8,128)S(1)}, f32[16,1280]{1,0:T(8,128)S(1)}, u32[]{:S(2)}, u32[]{:S(2)}) collective-permute-start(f32[16,1280]{1,0:T(8,128)S(1)} %shard_map.57.x0), channel_id=1, source_target_pairs={{0,48},{8,56},{16,32},{24,40},{32,16},{40,24},{48,0},{56,8},{64,11... | collective-permute-start | bytes 245768 | tf_op jit(solution)/shard_map/ppermute | solution.py:44
  75.0 2.1 %collective-permute-done.27.x1 = f32[16,1280]{1,0:T(8,128)S(1)} collective-permute-done((f32[16,1280]{1,0:T(8,128)S(1)}, f32[16,1280]{1,0:T(8,128)S(1)}, u32[]{:S(2)}, u32[]{:S(2)}) %collective-permute-start.27) | collective-permute-done | bytes 81952 | tf_op jit(solution)/shard_map/ppermute | solution.py:44
  78.9 3.7 %collective-permute-start.34 = (bf16[64,1024]{1,0:T(8,128)(2,1)S(1)}, bf16[64,1024]{1,0:T(8,128)(2,1)S(1)}, u32[]{:S(2)}, u32[]{:S(2)}) collective-permute-start(bf16[64,1024]{1,0:T(8,128)(2,1)S(1)} %get-tuple-element.53.refs_0_), channel_id=1, source_target_pairs={{0,193},{1,192},{2,195},{3,194},{4,197},{5,196},{6,199},{7,198},{8... | collective-permute-start | bytes 393224 | tf_op jit(solution)/shard_map/ppermute | solution.py:236
  82.9 2.3 %collective-permute-start.31 = (bf16[64,1024]{1,0:T(8,128)(2,1)S(1)}, bf16[64,1024]{1,0:T(8,128)(2,1)S(1)}, u32[]{:S(2)}, u32[]{:S(2)}) collective-permute-start(bf16[64,1024]{1,0:T(8,128)(2,1)S(1)} %get-tuple-element.53.refs_0_), channel_id=1, source_target_pairs={{0,6},{1,7},{2,4},{3,5},{4,2},{5,3},{6,0},{7,1},{8,14},{9,15},{10,... | collective-permute-start | bytes 393224 | tf_op jit(solution)/shard_map/ppermute | solution.py:223
  86.8 2.4 %collective-permute-start.36 = (bf16[64,1024]{1,0:T(8,128)(2,1)S(1)}, bf16[64,1024]{1,0:T(8,128)(2,1)S(1)}, u32[]{:S(2)}, u32[]{:S(2)}) collective-permute-start(bf16[64,1024]{1,0:T(8,128)(2,1)S(1)} %collective-permute-done.34.refs_0_), channel_id=1, source_target_pairs={{0,6},{1,7},{2,4},{3,5},{4,2},{5,3},{6,0},{7,1},{8,14},{9,15},{10,... | collective-permute-start | bytes 393224 | tf_op jit(solution)/shard_map/ppermute | solution.py:223
  89.3 13.4 %collective-permute-start.33 = (bf16[4,64,1024]{2,1,0:T(8,128)(2,1)S(1)}, bf16[4,64,1024]{2,1,0:T(8,128)(2,1)S(1)}, u32[]{:S(2)}, u32[]{:S(2)}) collective-permute-start(bf16[4,64,1024]{2,1,0:T(8,128)(2,1)S(1)} %shard_map.59.c0), channel_id=1, source_target_pairs={{0,8},{8,0},{16,24},{24,16},{32,40},{40,32},{48,56},{56,48},{64,72... | collective-permute-start | bytes 1572872 | tf_op jit(solution)/shard_map/ppermute | solution.py:44
  102.8 4.7 %collective-permute-start.38 = (bf16[4,64,1024]{2,1,0:T(8,128)(2,1)S(1)}, bf16[4,64,1024]{2,1,0:T(8,128)(2,1)S(1)}, u32[]{:S(2)}, u32[]{:S(2)}) collective-permute-start(bf16[4,64,1024]{2,1,0:T(8,128)(2,1)S(1)} %shard_map.60.c2), channel_id=1, source_target_pairs={{0,8},{8,0},{16,24},{24,16},{32,40},{40,32},{48,56},{56,48},{64,72... | collective-permute-start | bytes 1572872 | tf_op jit(solution)/shard_map/ppermute | solution.py:44
  109.1 11.5 %shard_map.61 = (f32[32,64]{1,0:T(8,128)S(1)}, f32[32,64]{1,0:T(8,128)S(1)}, f32[8,16,256]{2,1,0:T(8,128)}) custom-call(s32[4]{0:T(128)S(1)} %pad_add_fusion.place_ref, bf16[4,64,1024]{2,1,0:T(8,128)(2,1)S(1)} %shard_map.59.c0, bf16[4,64,1024]{2,1,0:T(8,128)(2,1)S(1)} %collective-permute-done.33.c1, bf16[4,64,1024]{2,1,0:T(8,128)(2,1)S(1)} %shard_map.60.c2, ...), custom_call_target="tpu_custom_call" | custom-call | tf_op jit(solution)/shard_map/pallas_call | solution.py:305
  (80 shorter events, 32.1 us)
Async XLA Ops:
  0.6 13.4 %collective-permute-start = (bf16[512,128]{1,0:T(8,128)(2,1)}, bf16[512,128]{1,0:T(8,128)(2,1)S(1)}, u32[]{:S(2)}, u32[]{:S(2)}) collective-permute-start(bf16[512,128]{1,0:T(8,128)(2,1)} %e_ref.1), channel_id=1, source_target_pairs={{0,1},{1,0},{2,3},{3,2},{4,5},{5,4},{6,7},{7,6},{8,9},{9,8},{10,11... | collective-permute-start | bytes 393224 | tf_op jit(solution)/shard_map/ppermute | solution.py:223
  8.5 6.2 %collective-permute-start.1 = (bf16[512,128]{1,0:T(8,128)(2,1)}, bf16[512,128]{1,0:T(8,128)(2,1)S(1)}, u32[]{:S(2)}, u32[]{:S(2)}) collective-permute-start(bf16[512,128]{1,0:T(8,128)(2,1)} %e_ref.1), channel_id=1, source_target_pairs={{0,4},{1,5},{2,6},{3,7},{4,0},{5,1},{6,2},{7,3},{8,12},{9,13},{10,... | collective-permute-start | bytes 393224 | tf_op jit(solution)/shard_map/ppermute | solution.py:223
  11.4 16.4 %collective-permute-start.2 = (bf16[512,128]{1,0:T(8,128)(2,1)}, bf16[512,128]{1,0:T(8,128)(2,1)S(1)}, u32[]{:S(2)}, u32[]{:S(2)}) collective-permute-start(bf16[512,128]{1,0:T(8,128)(2,1)} %e_ref.1), channel_id=1, source_target_pairs={{0,5},{1,4},{2,7},{3,6},{4,1},{5,0},{6,3},{7,2},{8,13},{9,12},{10,... | collective-permute-start | bytes 393224 | tf_op jit(solution)/shard_map/ppermute | solution.py:223
  11.4 16.4 %collective-permute-start.3 = (bf16[512,128]{1,0:T(8,128)(2,1)}, bf16[512,128]{1,0:T(8,128)(2,1)S(1)}, u32[]{:S(2)}, u32[]{:S(2)}) collective-permute-start(bf16[512,128]{1,0:T(8,128)(2,1)} %e_ref.1), channel_id=1, source_target_pairs={{0,6},{1,7},{2,4},{3,5},{4,2},{5,3},{6,0},{7,1},{8,14},{9,15},{10,... | collective-permute-start | bytes 393224 | tf_op jit(solution)/shard_map/ppermute | solution.py:223
  14.0 13.8 %collective-permute-start.5 = (bf16[512,128]{1,0:T(8,128)(2,1)}, bf16[512,128]{1,0:T(8,128)(2,1)S(1)}, u32[]{:S(2)}, u32[]{:S(2)}) collective-permute-start(bf16[512,128]{1,0:T(8,128)(2,1)} %e_ref.1), channel_id=1, source_target_pairs={{0,2},{1,3},{2,0},{3,1},{4,6},{5,7},{6,4},{7,5},{8,10},{9,11},{10,... | collective-permute-start | bytes 393224 | tf_op jit(solution)/shard_map/ppermute | solution.py:223
  14.0 13.8 %collective-permute-start.4 = (bf16[512,128]{1,0:T(8,128)(2,1)S(1)}, bf16[512,128]{1,0:T(8,128)(2,1)S(1)}, u32[]{:S(2)}, u32[]{:S(2)}) collective-permute-start(bf16[512,128]{1,0:T(8,128)(2,1)S(1)} %collective-permute-done.refs_1_), channel_id=1, source_target_pairs={{0,6},{1,7},{2,4},{3,5},{4,2},{5,3},{6,0},{7,1},{8,14},{9,15},{10,... | collective-permute-start | bytes 393224 | tf_op jit(solution)/shard_map/ppermute | solution.py:223
  14.6 13.2 %collective-permute-start.6 = (bf16[512,128]{1,0:T(8,128)(2,1)S(1)}, bf16[512,128]{1,0:T(8,128)(2,1)S(1)}, u32[]{:S(2)}, u32[]{:S(2)}) collective-permute-start(bf16[512,128]{1,0:T(8,128)(2,1)S(1)} %collective-permute-done.refs_1_), channel_id=1, source_target_pairs={{0,2},{1,3},{2,0},{3,1},{4,6},{5,7},{6,4},{7,5},{8,10},{9,11},{10,... | collective-permute-start | bytes 393224 | tf_op jit(solution)/shard_map/ppermute | solution.py:223
  30.5 28.3 %collective-permute-start.20 = (bf16[512,1024]{1,0:T(8,128)(2,1)S(1)}, bf16[512,1024]{1,0:T(8,128)(2,1)S(1)}, u32[]{:S(2)}, u32[]{:S(2)}) collective-permute-start(bf16[512,1024]{1,0:T(8,128)(2,1)S(1)} %get-tuple-element.47.own_ref), channel_id=1, source_target_pairs={{0,8},{8,0},{16,24},{24,16},{32,40},{40,32},{48,56},{56,48},{64,72... | collective-permute-start | bytes 3145736 | tf_op jit(solution)/shard_map/ppermute | solution.py:44
  32.1 4.5 %collective-permute-start.8 = (bf16[16,1024]{1,0:T(8,128)(2,1)S(1)}, bf16[16,1024]{1,0:T(8,128)(2,1)S(1)}, u32[]{:S(2)}, u32[]{:S(2)}) collective-permute-start(bf16[16,1024]{1,0:T(8,128)(2,1)S(1)} %get-tuple-element.36), channel_id=1, source_target_pairs={{0,32},{8,40},{16,48},{24,56},{32,0},{40,8},{48,16},{56,24},{64,96... | collective-permute-start | bytes 98312 | tf_op jit(solution)/shard_map/ppermute | solution.py:44
  40.8 4.7 %collective-permute-start.12 = (f32[24,256]{1,0:T(8,128)S(1)}, f32[24,256]{1,0:T(8,128)S(1)}, u32[]{:S(2)}, u32[]{:S(2)}) collective-permute-start(f32[24,256]{1,0:T(8,128)S(1)} %shard_map.53.a), channel_id=1, source_target_pairs={{0,192},{8,200},{16,208},{24,216},{32,224},{40,232},{48,240},{56,2... | collective-permute-start | bytes 73736 | tf_op jit(solution)/shard_map/ppermute | solution.py:44
  59.2 5.3 %collective-permute-start.21 = (f32[16,1024]{1,0:T(8,128)S(1)}, f32[16,1024]{1,0:T(8,128)S(1)}, u32[]{:S(2)}, u32[]{:S(2)}) collective-permute-start(f32[16,1024]{1,0:T(8,128)S(1)} %get-tuple-element.49), channel_id=1, source_target_pairs={{0,32},{8,40},{16,48},{24,56},{32,0},{40,8},{48,16},{56,24},{64,96... | collective-permute-start | bytes 196616 | tf_op jit(solution)/shard_map/ppermute | solution.py:44
  60.5 4.9 %collective-permute-start.22 = (f32[16,1024]{1,0:T(8,128)S(1)}, f32[16,1024]{1,0:T(8,128)S(1)}, u32[]{:S(2)}, u32[]{:S(2)}) collective-permute-start(f32[16,1024]{1,0:T(8,128)S(1)} %get-tuple-element.50), channel_id=1, source_target_pairs={{0,48},{8,56},{16,32},{24,40},{32,16},{40,24},{48,0},{56,8},{64,11... | collective-permute-start | bytes 196616 | tf_op jit(solution)/shard_map/ppermute | solution.py:44
  65.7 5.7 %collective-permute-start.24 = (f32[16,1024]{1,0:T(8,128)S(1)}, f32[16,1024]{1,0:T(8,128)S(1)}, u32[]{:S(2)}, u32[]{:S(2)}) collective-permute-start(f32[16,1024]{1,0:T(8,128)S(1)} %add_add_fusion.a), channel_id=1, source_target_pairs={{0,128},{8,136},{16,144},{24,152},{32,160},{40,168},{48,176},{56,1... | collective-permute-start | bytes 196616 | tf_op jit(solution)/shard_map/ppermute | solution.py:44
  66.1 5.3 %collective-permute-start.25 = (f32[16,1024]{1,0:T(8,128)S(1)}, f32[16,1024]{1,0:T(8,128)S(1)}, u32[]{:S(2)}, u32[]{:S(2)}) collective-permute-start(f32[16,1024]{1,0:T(8,128)S(1)} %add_add_fusion.a), channel_id=1, source_target_pairs={{0,192},{8,200},{16,208},{24,216},{32,224},{40,232},{48,240},{56,2... | collective-permute-start | bytes 196616 | tf_op jit(solution)/shard_map/ppermute | solution.py:44
  72.1 4.9 %collective-permute-start.27 = (f32[16,1280]{1,0:T(8,128)S(1)}, f32[16,1280]{1,0:T(8,128)S(1)}, u32[]{:S(2)}, u32[]{:S(2)}) collective-permute-start(f32[16,1280]{1,0:T(8,128)S(1)} %shard_map.57.x0), channel_id=1, source_target_pairs={{0,32},{8,40},{16,48},{24,56},{32,0},{40,8},{48,16},{56,24},{64,96... | collective-permute-start | bytes 245768 | tf_op jit(solution)/shard_map/ppermute | solution.py:44
  73.0 4.9 %collective-permute-start.28 = (f32[16,1280]{1,0:T(8,128)S(1)}, f32[16,1280]{1,0:T(8,128)S(1)}, u32[]{:S(2)}, u32[]{:S(2)}) collective-permute-start(f32[16,1280]{1,0:T(8,128)S(1)} %shard_map.57.x0), channel_id=1, source_target_pairs={{0,48},{8,56},{16,32},{24,40},{32,16},{40,24},{48,0},{56,8},{64,11... | collective-permute-start | bytes 245768 | tf_op jit(solution)/shard_map/ppermute | solution.py:44
  78.9 7.7 %collective-permute-start.34 = (bf16[64,1024]{1,0:T(8,128)(2,1)S(1)}, bf16[64,1024]{1,0:T(8,128)(2,1)S(1)}, u32[]{:S(2)}, u32[]{:S(2)}) collective-permute-start(bf16[64,1024]{1,0:T(8,128)(2,1)S(1)} %get-tuple-element.53.refs_0_), channel_id=1, source_target_pairs={{0,193},{1,192},{2,195},{3,194},{4,197},{5,196},{6,199},{7,198},{8... | collective-permute-start | bytes 393224 | tf_op jit(solution)/shard_map/ppermute | solution.py:236
  82.6 6.7 %collective-permute-start.30 = (bf16[64,1024]{1,0:T(8,128)(2,1)S(1)}, bf16[64,1024]{1,0:T(8,128)(2,1)S(1)}, u32[]{:S(2)}, u32[]{:S(2)}) collective-permute-start(bf16[64,1024]{1,0:T(8,128)(2,1)S(1)} %get-tuple-element.53.refs_0_), channel_id=1, source_target_pairs={{0,4},{1,5},{2,6},{3,7},{4,0},{5,1},{6,2},{7,3},{8,12},{9,13},{10,... | collective-permute-start | bytes 393224 | tf_op jit(solution)/shard_map/ppermute | solution.py:223
  82.9 6.3 %collective-permute-start.31 = (bf16[64,1024]{1,0:T(8,128)(2,1)S(1)}, bf16[64,1024]{1,0:T(8,128)(2,1)S(1)}, u32[]{:S(2)}, u32[]{:S(2)}) collective-permute-start(bf16[64,1024]{1,0:T(8,128)(2,1)S(1)} %get-tuple-element.53.refs_0_), channel_id=1, source_target_pairs={{0,6},{1,7},{2,4},{3,5},{4,2},{5,3},{6,0},{7,1},{8,14},{9,15},{10,... | collective-permute-start | bytes 393224 | tf_op jit(solution)/shard_map/ppermute | solution.py:223
  86.6 16.1 %collective-permute-start.35 = (bf16[64,1024]{1,0:T(8,128)(2,1)S(1)}, bf16[64,1024]{1,0:T(8,128)(2,1)S(1)}, u32[]{:S(2)}, u32[]{:S(2)}) collective-permute-start(bf16[64,1024]{1,0:T(8,128)(2,1)S(1)} %collective-permute-done.34.refs_0_), channel_id=1, source_target_pairs={{0,4},{1,5},{2,6},{3,7},{4,0},{5,1},{6,2},{7,3},{8,12},{9,13},{10,... | collective-permute-start | bytes 393224 | tf_op jit(solution)/shard_map/ppermute | solution.py:223
  86.8 15.9 %collective-permute-start.36 = (bf16[64,1024]{1,0:T(8,128)(2,1)S(1)}, bf16[64,1024]{1,0:T(8,128)(2,1)S(1)}, u32[]{:S(2)}, u32[]{:S(2)}) collective-permute-start(bf16[64,1024]{1,0:T(8,128)(2,1)S(1)} %collective-permute-done.34.refs_0_), channel_id=1, source_target_pairs={{0,6},{1,7},{2,4},{3,5},{4,2},{5,3},{6,0},{7,1},{8,14},{9,15},{10,... | collective-permute-start | bytes 393224 | tf_op jit(solution)/shard_map/ppermute | solution.py:223
  89.3 13.5 %collective-permute-start.37 = (bf16[64,1024]{1,0:T(8,128)(2,1)S(1)}, bf16[64,1024]{1,0:T(8,128)(2,1)S(1)}, u32[]{:S(2)}, u32[]{:S(2)}) collective-permute-start(bf16[64,1024]{1,0:T(8,128)(2,1)S(1)} %collective-permute-done.34.refs_0_), channel_id=1, source_target_pairs={{0,2},{1,3},{2,0},{3,1},{4,6},{5,7},{6,4},{7,5},{8,10},{9,11},{10,... | collective-permute-start | bytes 393224 | tf_op jit(solution)/shard_map/ppermute | solution.py:223
  89.3 19.8 %collective-permute-start.33 = (bf16[4,64,1024]{2,1,0:T(8,128)(2,1)S(1)}, bf16[4,64,1024]{2,1,0:T(8,128)(2,1)S(1)}, u32[]{:S(2)}, u32[]{:S(2)}) collective-permute-start(bf16[4,64,1024]{2,1,0:T(8,128)(2,1)S(1)} %shard_map.59.c0), channel_id=1, source_target_pairs={{0,8},{8,0},{16,24},{24,16},{32,40},{40,32},{48,56},{56,48},{64,72... | collective-permute-start | bytes 1572872 | tf_op jit(solution)/shard_map/ppermute | solution.py:44
  102.8 6.3 %collective-permute-start.38 = (bf16[4,64,1024]{2,1,0:T(8,128)(2,1)S(1)}, bf16[4,64,1024]{2,1,0:T(8,128)(2,1)S(1)}, u32[]{:S(2)}, u32[]{:S(2)}) collective-permute-start(bf16[4,64,1024]{2,1,0:T(8,128)(2,1)S(1)} %shard_map.60.c2), channel_id=1, source_target_pairs={{0,8},{8,0},{16,24},{24,16},{32,40},{40,32},{48,56},{56,48},{64,72... | collective-permute-start | bytes 1572872 | tf_op jit(solution)/shard_map/ppermute | solution.py:44
  (20 other events, 59.6 us)

commit v5 on v4

--- a/solution.py
+++ b/solution.py
@@ -48,12 +48,14 @@
     return permute_rows(x, lambda i: i ^ 1)
 
 
-def load_kernel(place_ref, r_ref, e_ref, book_ref, r_out, e_out, book_out):
+def load_kernel(place_ref, r_ref, e_ref, book_ref, r_out, e_out, book_out, scores_out):
     n = e_ref.shape[1]
     for k in range(SUB_DEVS):
         r_out[n * k : n * (k + 1)] = r_ref[pl.ds(pl.multiple_of((place_ref[3] ^ BLOCKS[k]) * n, n), n)]
     e_out[...] = e_ref[...]
-    book_out[...] = book_ref[...]
+    book = book_ref[4 * place_ref[0] + place_ref[1]]
+    book_out[...] = book
+    scores_out[...] = score_matrix(book)
 
 
 def rotate_kernel(place_ref, *refs):
@@ -95,10 +97,9 @@
     return w, dot(rhs, w, ((1,), (1,)))
 
 
-def assign_all(book, f_refs, stats_ref, w_ref=None):
+def assign_all(lhs, f_refs, stats_ref, w_ref=None):
     keep_ref, recv_ref = f_refs[:2]
     n = keep_ref.shape[2]
-    lhs = score_matrix(book)
     total = None
     for d in range(4):
         for h in range(2):
@@ -111,8 +112,8 @@
     stats_ref[...] = total[: stats_ref.shape[0]]
 
 
-def first_kernel(place_ref, k, r, f1, f2, f3, book_ref, stats_ref):
-    assign_all(book_ref[4 * place_ref[0] + place_ref[1]], (k, r, f1, f2, f3), stats_ref)
+def first_kernel(k, r, f1, f2, f3, scores_ref, stats_ref):
+    assign_all(scores_ref[...], (k, r, f1, f2, f3), stats_ref)
 
 
 def new_book(a, b, c, d, book):
@@ -120,10 +121,10 @@
     return (stats[:SUB_DIM] + PRIOR * book) / (stats[SUB_DIM : SUB_DIM + 1] + PRIOR)
 
 
-def second_kernel(place_ref, k, r, f1, f2, f3, book_ref, a, b, c, d, book_out, w_ref, stats_ref):
-    book = new_book(a, b, c, d, book_ref[4 * place_ref[0] + place_ref[1]])
+def second_kernel(k, r, f1, f2, f3, book_ref, a, b, c, d, book_out, w_ref, stats_ref):
+    book = new_book(a, b, c, d, book_ref[...])
     book_out[...] = book
-    assign_all(book, (k, r, f1, f2, f3), stats_ref, w_ref)
+    assign_all(score_matrix(book), (k, r, f1, f2, f3), stats_ref, w_ref)
 
 
 def rebuild_kernel(a, b, c, d, book_ref, w_ref, book_out, *outs):
@@ -236,13 +237,6 @@
     return lax.ppermute(x, ("rows", "sub"), pairs)
 
 
-def others_over_sub(x, across):
-    partner = across(x, 1)
-    y = over_y(x)
-    far = across(x, 5)
-    return [partner, y[0], far, y[1], over_sub(partner, 6), y[2], over_sub(partner, 2)]
-
-
 def over_z(x):
     return [x] + [permute_rows(x, lambda i, d=d: i ^ (8 * d)) for d in ORDER[1:]]
 
@@ -261,9 +255,22 @@
     core = row_index % 2
     place = jnp.stack([core, (row_index // 2) % 4, row_index, sub])
 
-    others = others_over_sub(embeddings, over_sub)
-    mats, mine, books = call(
-        load_kernel, tuple(shape(v.shape, v.dtype) for v in (rotation, embeddings, codebooks)), 1, 3
+    partner = over_sub(embeddings, 1)
+    own_y = over_y(embeddings)
+    partner_y = over_y(partner)
+    others = [partner]
+    for pair in zip(own_y, partner_y):
+        others += pair
+    mats, mine, book, scores = call(
+        load_kernel,
+        (
+            shape(rotation.shape, bf16),
+            shape(embeddings.shape, bf16),
+            shape((SUB_DIM, codes), f32),
+            shape((codes, 2 * SUB_DIM), bf16),
+        ),
+        1,
+        3,
     )(place, rotation, embeddings, codebooks)
     part = shape((4, SUB_DIM, n), bf16)
     keep, send, e_own = call(
@@ -280,10 +287,10 @@
     feats = (keep, recv, *over_x(call(join_kernel, (piece,) * 3, 0, 2)(keep, recv)))
 
     stats_shape = shape((SUB_DIM + 8, codes), f32)
-    stats = call(first_kernel, stats_shape, 1, 6)(place, *feats, books)
+    stats = call(first_kernel, stats_shape, 0, 6)(*feats, scores)
     book, weights, stats = call(
-        second_kernel, (shape((SUB_DIM, codes), f32), shape((4, codes, 2 * n), bf16), stats_shape), 1, 10
-    )(place, *feats, books, *over_z(stats))
+        second_kernel, (shape((SUB_DIM, codes), f32), shape((4, codes, 2 * n), bf16), stats_shape), 0, 10
+    )(*feats, book, *over_z(stats))
     book, *rebuilt = call(rebuild_kernel, (shape((SUB_DIM, codes), f32),) + (piece,) * 4, 0, 6)(
         *over_z(stats), book, weights
     )

time: 123 us -> 120 us (0.976)
  waiting for transfers between devices: 34.1 us -> 30 us
  starting transfers between devices: 64.8 us -> 67.3 us
    ppermute x13, waiting for transfers between devices: 8.88 us -> 3.89 us  [over_sub(): return lax.ppermute(x, 'sub', [(i, i ^ k) for i in range(SUB_DEVS)])]
    ppermute x27, waiting for transfers between devices: 23.8 us -> 25.1 us  [permute_rows(): return lax.ppermute(x, 'rows', [(i, to(i)) for i in range(ROW_DEVS)])]
    ppermute x13, starting transfers between devices: 20.2 us -> 21.5 us  [over_sub(): return lax.ppermute(x, 'sub', [(i, i ^ k) for i in range(SUB_DEVS)])]
  transfers between devices with their start and end apart: 41 -> 41, of which waited for: 22 -> 23; matrix products, arithmetic and copies ran while one was open for 0% -> 0% of each run, Pallas kernels for 5% -> 4%
where the time goes in v5:
time: 120 us
  starting transfers between devices  67.3 us (56%)
  waiting for transfers between devices  30 us (25%)
  Pallas kernels  18.2 us (15%)
  local copies, waits for them, and re-layouts  2.77 us (2%)
    ppermute x27, starting transfers between devices, permute_rows(): return lax.ppermute(x, 'rows', [(i, to(i)) for i in range(ROW_DEVS)])  42 us
    ppermute x27, waiting for transfers between devices, permute_rows(): return lax.ppermute(x, 'rows', [(i, to(i)) for i in range(ROW_DEVS)])  25.1 us
    ppermute x13, starting transfers between devices, over_sub(): return lax.ppermute(x, 'sub', [(i, i ^ k) for i in range(SUB_DEVS)])  21.5 us
    pallas_call x1, Pallas kernels, per_device(): call(polar_kernel, (piece, piece, shape(codebooks.shape, f32)), 1, 6, (pl...  11.5 us
    ppermute x13, waiting for transfers between devices, over_sub(): return lax.ppermute(x, 'sub', [(i, i ^ k) for i in range(SUB_DEVS)])  3.89 us
    ppermute x1, starting transfers between devices, over_sub_mirrored(): return lax.ppermute(x, ('rows', 'sub'), pairs)  3.84 us
    unnamed x6, local copies, waits for them, and re-layouts  2.76 us
  transfers between devices with their start and end apart: 41, of which 23 were waited for; matrix products, arithmetic and copies ran while one was open for 0% of the time, Pallas kernels for 4%

profile of v5, /device:TPU:1, one launch (start us, length us, event | category | flops | bytes accessed | tf_op | source)
XLA Modules:
  0.0 119.8 jit_solution(5550164128779635745)
XLA Ops:
  0.6 7.8 %collective-permute-start = (bf16[512,128]{1,0:T(8,128)(2,1)}, bf16[512,128]{1,0:T(8,128)(2,1)S(1)}, u32[]{:S(2)}, u32[]{:S(2)}) collective-permute-start(bf16[512,128]{1,0:T(8,128)(2,1)} %e_ref.1), channel_id=1, source_target_pairs={{0,1},{1,0},{2,3},{3,2},{4,5},{5,4},{6,7},{7,6},{8,9},{9,8},{10,11... | collective-permute-start | bytes 393224 | tf_op jit(solution)/shard_map/ppermute | solution.py:224
  8.5 2.9 %collective-permute-start.1 = (bf16[512,128]{1,0:T(8,128)(2,1)}, bf16[512,128]{1,0:T(8,128)(2,1)S(1)}, u32[]{:S(2)}, u32[]{:S(2)}) collective-permute-start(bf16[512,128]{1,0:T(8,128)(2,1)} %e_ref.1), channel_id=1, source_target_pairs={{0,4},{1,5},{2,6},{3,7},{4,0},{5,1},{6,2},{7,3},{8,12},{9,13},{10,... | collective-permute-start | bytes 393224 | tf_op jit(solution)/shard_map/ppermute | solution.py:224
  12.2 3.1 %collective-permute-start.2 = (bf16[512,128]{1,0:T(8,128)(2,1)S(1)}, bf16[512,128]{1,0:T(8,128)(2,1)S(1)}, u32[]{:S(2)}, u32[]{:S(2)}) collective-permute-start(bf16[512,128]{1,0:T(8,128)(2,1)S(1)} %collective-permute-done.refs_1_), channel_id=1, source_target_pairs={{0,4},{1,5},{2,6},{3,7},{4,0},{5,1},{6,2},{7,3},{8,12},{9,13},{10,... | collective-permute-start | bytes 393224 | tf_op jit(solution)/shard_map/ppermute | solution.py:224
  20.0 3.2 %collective-permute-done.4.refs_5_ = bf16[512,128]{1,0:T(8,128)(2,1)S(1)} collective-permute-done((bf16[512,128]{1,0:T(8,128)(2,1)S(1)}, bf16[512,128]{1,0:T(8,128)(2,1)S(1)}, u32[]{:S(2)}, u32[]{:S(2)}) %collective-permute-start.4) | collective-permute-done | bytes 131104 | tf_op jit(solution)/shard_map/ppermute | solution.py:224
  24.5 1.5 %collective-permute-start.7 = (bf16[4,16,512]{2,1,0:T(8,128)(2,1)S(1)}, bf16[4,16,512]{2,1,0:T(8,128)(2,1)S(1)}, u32[]{:S(2)}, u32[]{:S(2)}) collective-permute-start(bf16[4,16,512]{2,1,0:T(8,128)(2,1)S(1)} %get-tuple-element.35), channel_id=1, source_target_pairs={{0,8},{8,0},{16,24},{24,16},{32,40},{40,32},{48,56},{56,48},{64,72... | collective-permute-start | bytes 196616 | tf_op jit(solution)/shard_map/ppermute | solution.py:44
  28.6 2.5 %collective-permute-start.8 = (bf16[16,1024]{1,0:T(8,128)(2,1)S(1)}, bf16[16,1024]{1,0:T(8,128)(2,1)S(1)}, u32[]{:S(2)}, u32[]{:S(2)}) collective-permute-start(bf16[16,1024]{1,0:T(8,128)(2,1)S(1)} %get-tuple-element.37), channel_id=1, source_target_pairs={{0,32},{8,40},{16,48},{24,56},{32,0},{40,8},{48,16},{56,24},{64,96... | collective-permute-start | bytes 98312 | tf_op jit(solution)/shard_map/ppermute | solution.py:44
  31.2 1.9 %collective-permute-done.8.f1 = bf16[16,1024]{1,0:T(8,128)(2,1)S(1)} collective-permute-done((bf16[16,1024]{1,0:T(8,128)(2,1)S(1)}, bf16[16,1024]{1,0:T(8,128)(2,1)S(1)}, u32[]{:S(2)}, u32[]{:S(2)}) %collective-permute-start.8) | collective-permute-done | bytes 32800 | tf_op jit(solution)/shard_map/ppermute | solution.py:44
  33.1 1.9 %collective-permute-done.9.f2 = bf16[16,1024]{1,0:T(8,128)(2,1)S(1)} collective-permute-done((bf16[16,1024]{1,0:T(8,128)(2,1)S(1)}, bf16[16,1024]{1,0:T(8,128)(2,1)S(1)}, u32[]{:S(2)}, u32[]{:S(2)}) %collective-permute-start.9) | collective-permute-done | bytes 32800 | tf_op jit(solution)/shard_map/ppermute | solution.py:44
  35.0 1.6 %shard_map.53.a = f32[24,256]{1,0:T(8,128)S(1)} custom-call(bf16[4,16,512]{2,1,0:T(8,128)(2,1)S(1)} %get-tuple-element.33.keep_ref.k, bf16[4,16,512]{2,1,0:T(8,128)(2,1)S(1)} %collective-permute-done.7.recv_ref.r, bf16[16,1024]{1,0:T(8,128)(2,1)S(1)} %collective-permute-done.8.f1, bf16[16,1024]{1,0:T(8,128)(2,1)S(1)} %collective-permute-done.9.f2, ...), custom_call_target="tpu_custom_call" | custom-call | tf_op jit(solution)/shard_map/pallas_call | solution.py:290
  36.6 2.4 %collective-permute-start.11 = (f32[24,256]{1,0:T(8,128)S(1)}, f32[24,256]{1,0:T(8,128)S(1)}, u32[]{:S(2)}, u32[]{:S(2)}) collective-permute-start(f32[24,256]{1,0:T(8,128)S(1)} %shard_map.53.a), channel_id=1, source_target_pairs={{0,128},{8,136},{16,144},{24,152},{32,160},{40,168},{48,176},{56,1... | collective-permute-start | bytes 73736 | tf_op jit(solution)/shard_map/ppermute | solution.py:44
  40.3 3.5 %collective-permute-done.12.c = f32[24,256]{1,0:T(8,128)S(1)} collective-permute-done((f32[24,256]{1,0:T(8,128)S(1)}, f32[24,256]{1,0:T(8,128)S(1)}, u32[]{:S(2)}, u32[]{:S(2)}) %collective-permute-start.12) | collective-permute-done | bytes 24608 | tf_op jit(solution)/shard_map/ppermute | solution.py:44
  43.8 1.8 %shard_map.54 = (f32[16,256]{1,0:T(8,128)S(1)}, bf16[4,256,1024]{2,1,0:T(8,128)(2,1)S(1)}, f32[24,256]{1,0:T(8,128)S(1)}) custom-call(bf16[4,16,512]{2,1,0:T(8,128)(2,1)S(1)} %get-tuple-element.33.keep_ref.k, bf16[4,16,512]{2,1,0:T(8,128)(2,1)S(1)} %collective-permute-done.7.recv_ref.r, bf16[16,1024]{1,0:T(8,128)(2,1)S(1)} %collective-permute-done.8.f1, ...), custom_call_target="tpu_custom_call" | custom-call | tf_op jit(solution)/shard_map/pallas_call | solution.py:291
  49.3 1.8 %collective-permute-done.15.c = f32[24,256]{1,0:T(8,128)S(1)} collective-permute-done((f32[24,256]{1,0:T(8,128)S(1)}, f32[24,256]{1,0:T(8,128)S(1)}, u32[]{:S(2)}, u32[]{:S(2)}) %collective-permute-start.15) | collective-permute-done | bytes 24608 | tf_op jit(solution)/shard_map/ppermute | solution.py:44
  54.2 1.7 %collective-permute-done.17.x1 = bf16[16,1024]{1,0:T(8,128)(2,1)S(1)} collective-permute-done((bf16[16,1024]{1,0:T(8,128)(2,1)S(1)}, bf16[16,1024]{1,0:T(8,128)(2,1)S(1)}, u32[]{:S(2)}, u32[]{:S(2)}) %collective-permute-start.17) | collective-permute-done | bytes 32800 | tf_op jit(solution)/shard_map/ppermute | solution.py:44
  57.8 2.1 %collective-permute-start.22 = (f32[16,1024]{1,0:T(8,128)S(1)}, f32[16,1024]{1,0:T(8,128)S(1)}, u32[]{:S(2)}, u32[]{:S(2)}) collective-permute-start(f32[16,1024]{1,0:T(8,128)S(1)} %get-tuple-element.52), channel_id=1, source_target_pairs={{0,48},{8,56},{16,32},{24,40},{32,16},{40,24},{48,0},{56,8},{64,11... | collective-permute-start | bytes 196616 | tf_op jit(solution)/shard_map/ppermute | solution.py:44
  65.8 2.1 %collective-permute-done.24.b = f32[16,1024]{1,0:T(8,128)S(1)} collective-permute-done((f32[16,1024]{1,0:T(8,128)S(1)}, f32[16,1024]{1,0:T(8,128)S(1)}, u32[]{:S(2)}, u32[]{:S(2)}) %collective-permute-start.24) | collective-permute-done | bytes 65568 | tf_op jit(solution)/shard_map/ppermute | solution.py:44
  70.2 2.0 %collective-permute-start.28 = (f32[16,1280]{1,0:T(8,128)S(1)}, f32[16,1280]{1,0:T(8,128)S(1)}, u32[]{:S(2)}, u32[]{:S(2)}) collective-permute-start(f32[16,1280]{1,0:T(8,128)S(1)} %shard_map.57.x0), channel_id=1, source_target_pairs={{0,48},{8,56},{16,32},{24,40},{32,16},{40,24},{48,0},{56,8},{64,11... | collective-permute-start | bytes 245768 | tf_op jit(solution)/shard_map/ppermute | solution.py:44
  72.2 2.1 %collective-permute-done.27.x1 = f32[16,1280]{1,0:T(8,128)S(1)} collective-permute-done((f32[16,1280]{1,0:T(8,128)S(1)}, f32[16,1280]{1,0:T(8,128)S(1)}, u32[]{:S(2)}, u32[]{:S(2)}) %collective-permute-start.27) | collective-permute-done | bytes 81952 | tf_op jit(solution)/shard_map/ppermute | solution.py:44
  76.2 3.8 %collective-permute-start.34 = (bf16[64,1024]{1,0:T(8,128)(2,1)S(1)}, bf16[64,1024]{1,0:T(8,128)(2,1)S(1)}, u32[]{:S(2)}, u32[]{:S(2)}) collective-permute-start(bf16[64,1024]{1,0:T(8,128)(2,1)S(1)} %get-tuple-element.55.refs_0_), channel_id=1, source_target_pairs={{0,193},{1,192},{2,195},{3,194},{4,197},{5,196},{6,199},{7,198},{8... | collective-permute-start | bytes 393224 | tf_op jit(solution)/shard_map/ppermute | solution.py:237
  81.3 1.8 %collective-permute-start.31 = (bf16[64,1024]{1,0:T(8,128)(2,1)S(1)}, bf16[64,1024]{1,0:T(8,128)(2,1)S(1)}, u32[]{:S(2)}, u32[]{:S(2)}) collective-permute-start(bf16[64,1024]{1,0:T(8,128)(2,1)S(1)} %get-tuple-element.55.refs_0_), channel_id=1, source_target_pairs={{0,6},{1,7},{2,4},{3,5},{4,2},{5,3},{6,0},{7,1},{8,14},{9,15},{10,... | collective-permute-start | bytes 393224 | tf_op jit(solution)/shard_map/ppermute | solution.py:224
  85.1 2.0 %collective-permute-start.36 = (bf16[64,1024]{1,0:T(8,128)(2,1)S(1)}, bf16[64,1024]{1,0:T(8,128)(2,1)S(1)}, u32[]{:S(2)}, u32[]{:S(2)}) collective-permute-start(bf16[64,1024]{1,0:T(8,128)(2,1)S(1)} %collective-permute-done.34.refs_0_), channel_id=1, source_target_pairs={{0,6},{1,7},{2,4},{3,5},{4,2},{5,3},{6,0},{7,1},{8,14},{9,15},{10,... | collective-permute-start | bytes 393224 | tf_op jit(solution)/shard_map/ppermute | solution.py:224
  87.2 12.9 %collective-permute-start.33 = (bf16[4,64,1024]{2,1,0:T(8,128)(2,1)S(1)}, bf16[4,64,1024]{2,1,0:T(8,128)(2,1)S(1)}, u32[]{:S(2)}, u32[]{:S(2)}) collective-permute-start(bf16[4,64,1024]{2,1,0:T(8,128)(2,1)S(1)} %shard_map.59.c0), channel_id=1, source_target_pairs={{0,8},{8,0},{16,24},{24,16},{32,40},{40,32},{48,56},{56,48},{64,72... | collective-permute-start | bytes 1572872 | tf_op jit(solution)/shard_map/ppermute | solution.py:44
  100.1 4.7 %collective-permute-start.38 = (bf16[4,64,1024]{2,1,0:T(8,128)(2,1)S(1)}, bf16[4,64,1024]{2,1,0:T(8,128)(2,1)S(1)}, u32[]{:S(2)}, u32[]{:S(2)}) collective-permute-start(bf16[4,64,1024]{2,1,0:T(8,128)(2,1)S(1)} %shard_map.60.c2), channel_id=1, source_target_pairs={{0,8},{8,0},{16,24},{24,16},{32,40},{40,32},{48,56},{56,48},{64,72... | collective-permute-start | bytes 1572872 | tf_op jit(solution)/shard_map/ppermute | solution.py:44
  106.4 11.5 %shard_map.61 = (f32[32,64]{1,0:T(8,128)S(1)}, f32[32,64]{1,0:T(8,128)S(1)}, f32[8,16,256]{2,1,0:T(8,128)}) custom-call(s32[4]{0:T(128)S(1)} %pad_add_fusion.place_ref, bf16[4,64,1024]{2,1,0:T(8,128)(2,1)S(1)} %shard_map.59.c0, bf16[4,64,1024]{2,1,0:T(8,128)(2,1)S(1)} %collective-permute-done.33.c1, bf16[4,64,1024]{2,1,0:T(8,128)(2,1)S(1)} %shard_map.60.c2, ...), custom_call_target="tpu_custom_call" | custom-call | tf_op jit(solution)/shard_map/pallas_call | solution.py:312
  (80 shorter events, 36.6 us)
Async XLA Ops:
  0.6 11.5 %collective-permute-start = (bf16[512,128]{1,0:T(8,128)(2,1)}, bf16[512,128]{1,0:T(8,128)(2,1)S(1)}, u32[]{:S(2)}, u32[]{:S(2)}) collective-permute-start(bf16[512,128]{1,0:T(8,128)(2,1)} %e_ref.1), channel_id=1, source_target_pairs={{0,1},{1,0},{2,3},{3,2},{4,5},{5,4},{6,7},{7,6},{8,9},{9,8},{10,11... | collective-permute-start | bytes 393224 | tf_op jit(solution)/shard_map/ppermute | solution.py:224
  8.5 7.6 %collective-permute-start.1 = (bf16[512,128]{1,0:T(8,128)(2,1)}, bf16[512,128]{1,0:T(8,128)(2,1)S(1)}, u32[]{:S(2)}, u32[]{:S(2)}) collective-permute-start(bf16[512,128]{1,0:T(8,128)(2,1)} %e_ref.1), channel_id=1, source_target_pairs={{0,4},{1,5},{2,6},{3,7},{4,0},{5,1},{6,2},{7,3},{8,12},{9,13},{10,... | collective-permute-start | bytes 393224 | tf_op jit(solution)/shard_map/ppermute | solution.py:224
  11.4 8.2 %collective-permute-start.3 = (bf16[512,128]{1,0:T(8,128)(2,1)}, bf16[512,128]{1,0:T(8,128)(2,1)S(1)}, u32[]{:S(2)}, u32[]{:S(2)}) collective-permute-start(bf16[512,128]{1,0:T(8,128)(2,1)} %e_ref.1), channel_id=1, source_target_pairs={{0,6},{1,7},{2,4},{3,5},{4,2},{5,3},{6,0},{7,1},{8,14},{9,15},{10,... | collective-permute-start | bytes 393224 | tf_op jit(solution)/shard_map/ppermute | solution.py:224
  12.1 7.4 %collective-permute-start.5 = (bf16[512,128]{1,0:T(8,128)(2,1)}, bf16[512,128]{1,0:T(8,128)(2,1)S(1)}, u32[]{:S(2)}, u32[]{:S(2)}) collective-permute-start(bf16[512,128]{1,0:T(8,128)(2,1)} %e_ref.1), channel_id=1, source_target_pairs={{0,2},{1,3},{2,0},{3,1},{4,6},{5,7},{6,4},{7,5},{8,10},{9,11},{10,... | collective-permute-start | bytes 393224 | tf_op jit(solution)/shard_map/ppermute | solution.py:224
  12.2 7.8 %collective-permute-start.2 = (bf16[512,128]{1,0:T(8,128)(2,1)S(1)}, bf16[512,128]{1,0:T(8,128)(2,1)S(1)}, u32[]{:S(2)}, u32[]{:S(2)}) collective-permute-start(bf16[512,128]{1,0:T(8,128)(2,1)S(1)} %collective-permute-done.refs_1_), channel_id=1, source_target_pairs={{0,4},{1,5},{2,6},{3,7},{4,0},{5,1},{6,2},{7,3},{8,12},{9,13},{10,... | collective-permute-start | bytes 393224 | tf_op jit(solution)/shard_map/ppermute | solution.py:224
  15.2 7.9 %collective-permute-start.4 = (bf16[512,128]{1,0:T(8,128)(2,1)S(1)}, bf16[512,128]{1,0:T(8,128)(2,1)S(1)}, u32[]{:S(2)}, u32[]{:S(2)}) collective-permute-start(bf16[512,128]{1,0:T(8,128)(2,1)S(1)} %collective-permute-done.refs_1_), channel_id=1, source_target_pairs={{0,6},{1,7},{2,4},{3,5},{4,2},{5,3},{6,0},{7,1},{8,14},{9,15},{10,... | collective-permute-start | bytes 393224 | tf_op jit(solution)/shard_map/ppermute | solution.py:224
  16.0 7.4 %collective-permute-start.6 = (bf16[512,128]{1,0:T(8,128)(2,1)S(1)}, bf16[512,128]{1,0:T(8,128)(2,1)S(1)}, u32[]{:S(2)}, u32[]{:S(2)}) collective-permute-start(bf16[512,128]{1,0:T(8,128)(2,1)S(1)} %collective-permute-done.refs_1_), channel_id=1, source_target_pairs={{0,2},{1,3},{2,0},{3,1},{4,6},{5,7},{6,4},{7,5},{8,10},{9,11},{10,... | collective-permute-start | bytes 393224 | tf_op jit(solution)/shard_map/ppermute | solution.py:224
  26.9 29.0 %collective-permute-start.20 = (bf16[512,1024]{1,0:T(8,128)(2,1)S(1)}, bf16[512,1024]{1,0:T(8,128)(2,1)S(1)}, u32[]{:S(2)}, u32[]{:S(2)}) collective-permute-start(bf16[512,1024]{1,0:T(8,128)(2,1)S(1)} %get-tuple-element.49.own_ref), channel_id=1, source_target_pairs={{0,8},{8,0},{16,24},{24,16},{32,40},{40,32},{48,56},{56,48},{64,72... | collective-permute-start | bytes 3145736 | tf_op jit(solution)/shard_map/ppermute | solution.py:44
  28.6 4.5 %collective-permute-start.8 = (bf16[16,1024]{1,0:T(8,128)(2,1)S(1)}, bf16[16,1024]{1,0:T(8,128)(2,1)S(1)}, u32[]{:S(2)}, u32[]{:S(2)}) collective-permute-start(bf16[16,1024]{1,0:T(8,128)(2,1)S(1)} %get-tuple-element.37), channel_id=1, source_target_pairs={{0,32},{8,40},{16,48},{24,56},{32,0},{40,8},{48,16},{56,24},{64,96... | collective-permute-start | bytes 98312 | tf_op jit(solution)/shard_map/ppermute | solution.py:44
  39.1 4.7 %collective-permute-start.12 = (f32[24,256]{1,0:T(8,128)S(1)}, f32[24,256]{1,0:T(8,128)S(1)}, u32[]{:S(2)}, u32[]{:S(2)}) collective-permute-start(f32[24,256]{1,0:T(8,128)S(1)} %shard_map.53.a), channel_id=1, source_target_pairs={{0,192},{8,200},{16,208},{24,216},{32,224},{40,232},{48,240},{56,2... | collective-permute-start | bytes 73736 | tf_op jit(solution)/shard_map/ppermute | solution.py:44
  46.6 4.5 %collective-permute-start.15 = (f32[24,256]{1,0:T(8,128)S(1)}, f32[24,256]{1,0:T(8,128)S(1)}, u32[]{:S(2)}, u32[]{:S(2)}) collective-permute-start(f32[24,256]{1,0:T(8,128)S(1)} %get-tuple-element.42.a), channel_id=1, source_target_pairs={{0,192},{8,200},{16,208},{24,216},{32,224},{40,232},{48,240},{56,2... | collective-permute-start | bytes 73736 | tf_op jit(solution)/shard_map/ppermute | solution.py:44
  56.4 4.8 %collective-permute-start.21 = (f32[16,1024]{1,0:T(8,128)S(1)}, f32[16,1024]{1,0:T(8,128)S(1)}, u32[]{:S(2)}, u32[]{:S(2)}) collective-permute-start(f32[16,1024]{1,0:T(8,128)S(1)} %get-tuple-element.51), channel_id=1, source_target_pairs={{0,32},{8,40},{16,48},{24,56},{32,0},{40,8},{48,16},{56,24},{64,96... | collective-permute-start | bytes 196616 | tf_op jit(solution)/shard_map/ppermute | solution.py:44
  63.0 4.8 %collective-permute-start.24 = (f32[16,1024]{1,0:T(8,128)S(1)}, f32[16,1024]{1,0:T(8,128)S(1)}, u32[]{:S(2)}, u32[]{:S(2)}) collective-permute-start(f32[16,1024]{1,0:T(8,128)S(1)} %add_add_fusion.a), channel_id=1, source_target_pairs={{0,128},{8,136},{16,144},{24,152},{32,160},{40,168},{48,176},{56,1... | collective-permute-start | bytes 196616 | tf_op jit(solution)/shard_map/ppermute | solution.py:44
  63.7 5.1 %collective-permute-start.25 = (f32[16,1024]{1,0:T(8,128)S(1)}, f32[16,1024]{1,0:T(8,128)S(1)}, u32[]{:S(2)}, u32[]{:S(2)}) collective-permute-start(f32[16,1024]{1,0:T(8,128)S(1)} %add_add_fusion.a), channel_id=1, source_target_pairs={{0,192},{8,200},{16,208},{24,216},{32,224},{40,232},{48,240},{56,2... | collective-permute-start | bytes 196616 | tf_op jit(solution)/shard_map/ppermute | solution.py:44
  69.3 4.9 %collective-permute-start.27 = (f32[16,1280]{1,0:T(8,128)S(1)}, f32[16,1280]{1,0:T(8,128)S(1)}, u32[]{:S(2)}, u32[]{:S(2)}) collective-permute-start(f32[16,1280]{1,0:T(8,128)S(1)} %shard_map.57.x0), channel_id=1, source_target_pairs={{0,32},{8,40},{16,48},{24,56},{32,0},{40,8},{48,16},{56,24},{64,96... | collective-permute-start | bytes 245768 | tf_op jit(solution)/shard_map/ppermute | solution.py:44
  70.2 5.0 %collective-permute-start.28 = (f32[16,1280]{1,0:T(8,128)S(1)}, f32[16,1280]{1,0:T(8,128)S(1)}, u32[]{:S(2)}, u32[]{:S(2)}) collective-permute-start(f32[16,1280]{1,0:T(8,128)S(1)} %shard_map.57.x0), channel_id=1, source_target_pairs={{0,48},{8,56},{16,32},{24,40},{32,16},{40,24},{48,0},{56,8},{64,11... | collective-permute-start | bytes 245768 | tf_op jit(solution)/shard_map/ppermute | solution.py:44
  76.2 7.9 %collective-permute-start.34 = (bf16[64,1024]{1,0:T(8,128)(2,1)S(1)}, bf16[64,1024]{1,0:T(8,128)(2,1)S(1)}, u32[]{:S(2)}, u32[]{:S(2)}) collective-permute-start(bf16[64,1024]{1,0:T(8,128)(2,1)S(1)} %get-tuple-element.55.refs_0_), channel_id=1, source_target_pairs={{0,193},{1,192},{2,195},{3,194},{4,197},{5,196},{6,199},{7,198},{8... | collective-permute-start | bytes 393224 | tf_op jit(solution)/shard_map/ppermute | solution.py:237
  80.0 7.1 %collective-permute-start.30 = (bf16[64,1024]{1,0:T(8,128)(2,1)S(1)}, bf16[64,1024]{1,0:T(8,128)(2,1)S(1)}, u32[]{:S(2)}, u32[]{:S(2)}) collective-permute-start(bf16[64,1024]{1,0:T(8,128)(2,1)S(1)} %get-tuple-element.55.refs_0_), channel_id=1, source_target_pairs={{0,4},{1,5},{2,6},{3,7},{4,0},{5,1},{6,2},{7,3},{8,12},{9,13},{10,... | collective-permute-start | bytes 393224 | tf_op jit(solution)/shard_map/ppermute | solution.py:224
  81.3 5.8 %collective-permute-start.31 = (bf16[64,1024]{1,0:T(8,128)(2,1)S(1)}, bf16[64,1024]{1,0:T(8,128)(2,1)S(1)}, u32[]{:S(2)}, u32[]{:S(2)}) collective-permute-start(bf16[64,1024]{1,0:T(8,128)(2,1)S(1)} %get-tuple-element.55.refs_0_), channel_id=1, source_target_pairs={{0,6},{1,7},{2,4},{3,5},{4,2},{5,3},{6,0},{7,1},{8,14},{9,15},{10,... | collective-permute-start | bytes 393224 | tf_op jit(solution)/shard_map/ppermute | solution.py:224
  84.1 16.0 %collective-permute-start.35 = (bf16[64,1024]{1,0:T(8,128)(2,1)S(1)}, bf16[64,1024]{1,0:T(8,128)(2,1)S(1)}, u32[]{:S(2)}, u32[]{:S(2)}) collective-permute-start(bf16[64,1024]{1,0:T(8,128)(2,1)S(1)} %collective-permute-done.34.refs_0_), channel_id=1, source_target_pairs={{0,4},{1,5},{2,6},{3,7},{4,0},{5,1},{6,2},{7,3},{8,12},{9,13},{10,... | collective-permute-start | bytes 393224 | tf_op jit(solution)/shard_map/ppermute | solution.py:224
  85.1 15.0 %collective-permute-start.36 = (bf16[64,1024]{1,0:T(8,128)(2,1)S(1)}, bf16[64,1024]{1,0:T(8,128)(2,1)S(1)}, u32[]{:S(2)}, u32[]{:S(2)}) collective-permute-start(bf16[64,1024]{1,0:T(8,128)(2,1)S(1)} %collective-permute-done.34.refs_0_), channel_id=1, source_target_pairs={{0,6},{1,7},{2,4},{3,5},{4,2},{5,3},{6,0},{7,1},{8,14},{9,15},{10,... | collective-permute-start | bytes 393224 | tf_op jit(solution)/shard_map/ppermute | solution.py:224
  87.1 13.0 %collective-permute-start.37 = (bf16[64,1024]{1,0:T(8,128)(2,1)S(1)}, bf16[64,1024]{1,0:T(8,128)(2,1)S(1)}, u32[]{:S(2)}, u32[]{:S(2)}) collective-permute-start(bf16[64,1024]{1,0:T(8,128)(2,1)S(1)} %collective-permute-done.34.refs_0_), channel_id=1, source_target_pairs={{0,2},{1,3},{2,0},{3,1},{4,6},{5,7},{6,4},{7,5},{8,10},{9,11},{10,... | collective-permute-start | bytes 393224 | tf_op jit(solution)/shard_map/ppermute | solution.py:224
  87.2 19.2 %collective-permute-start.33 = (bf16[4,64,1024]{2,1,0:T(8,128)(2,1)S(1)}, bf16[4,64,1024]{2,1,0:T(8,128)(2,1)S(1)}, u32[]{:S(2)}, u32[]{:S(2)}) collective-permute-start(bf16[4,64,1024]{2,1,0:T(8,128)(2,1)S(1)} %shard_map.59.c0), channel_id=1, source_target_pairs={{0,8},{8,0},{16,24},{24,16},{32,40},{40,32},{48,56},{56,48},{64,72... | collective-permute-start | bytes 1572872 | tf_op jit(solution)/shard_map/ppermute | solution.py:44
  100.1 6.3 %collective-permute-start.38 = (bf16[4,64,1024]{2,1,0:T(8,128)(2,1)S(1)}, bf16[4,64,1024]{2,1,0:T(8,128)(2,1)S(1)}, u32[]{:S(2)}, u32[]{:S(2)}) collective-permute-start(bf16[4,64,1024]{2,1,0:T(8,128)(2,1)S(1)} %shard_map.60.c2), channel_id=1, source_target_pairs={{0,8},{8,0},{16,24},{24,16},{32,40},{40,32},{48,56},{56,48},{64,72... | collective-permute-start | bytes 1572872 | tf_op jit(solution)/shard_map/ppermute | solution.py:44
  (20 other events, 62.1 us)

commit v6 on v5

--- a/solution.py
+++ b/solution.py
@@ -238,7 +238,7 @@
 
 
 def over_z(x):
-    return [x] + [permute_rows(x, lambda i, d=d: i ^ (8 * d)) for d in ORDER[1:]]
+    return [x] + [permute_rows(x, lambda i, d=d: i ^ (8 * d)) for d in (3, 2, 1)]
 
 
 def over_x(xs):

time: 120 us -> 119 us (level)
  waiting for transfers between devices: 30 us -> 26.3 us
  starting transfers between devices: 67.3 us -> 69.8 us
    ppermute x27, waiting for transfers between devices: 25.1 us -> 22.4 us  [permute_rows(): return lax.ppermute(x, 'rows', [(i, to(i)) for i in range(ROW_DEVS)])]
    ppermute x27, starting transfers between devices: 42 us -> 44.2 us  [permute_rows(): return lax.ppermute(x, 'rows', [(i, to(i)) for i in range(ROW_DEVS)])]
where the time goes in v6:
time: 119 us
  starting transfers between devices  69.8 us (59%)
  waiting for transfers between devices  26.3 us (22%)
  Pallas kernels  18.2 us (15%)
  local copies, waits for them, and re-layouts  2.77 us (2%)
    ppermute x27, starting transfers between devices, permute_rows(): return lax.ppermute(x, 'rows', [(i, to(i)) for i in range(ROW_DEVS)])  44.2 us
    ppermute x27, waiting for transfers between devices, permute_rows(): return lax.ppermute(x, 'rows', [(i, to(i)) for i in range(ROW_DEVS)])  22.4 us
    ppermute x13, starting transfers between devices, over_sub(): return lax.ppermute(x, 'sub', [(i, i ^ k) for i in range(SUB_DEVS)])  22.3 us
    pallas_call x1, Pallas kernels, per_device(): call(polar_kernel, (piece, piece, shape(codebooks.shape, f32)), 1, 6, (pl...  11.5 us
    ppermute x13, waiting for transfers between devices, over_sub(): return lax.ppermute(x, 'sub', [(i, i ^ k) for i in range(SUB_DEVS)])  3.89 us
    ppermute x1, starting transfers between devices, over_sub_mirrored(): return lax.ppermute(x, ('rows', 'sub'), pairs)  3.34 us
    unnamed x6, local copies, waits for them, and re-layouts  2.76 us
  transfers between devices with their start and end apart: 41, of which 23 were waited for; matrix products, arithmetic and copies ran while one was open for 0% of the time, Pallas kernels for 4%

profile of v6, /device:TPU:1, one launch (start us, length us, event | category | flops | bytes accessed | tf_op | source)
XLA Modules:
  0.0 118.7 jit_solution(17561195398422272378)
XLA Ops:
  0.6 7.8 %collective-permute-start = (bf16[512,128]{1,0:T(8,128)(2,1)}, bf16[512,128]{1,0:T(8,128)(2,1)S(1)}, u32[]{:S(2)}, u32[]{:S(2)}) collective-permute-start(bf16[512,128]{1,0:T(8,128)(2,1)} %e_ref.1), channel_id=1, source_target_pairs={{0,1},{1,0},{2,3},{3,2},{4,5},{5,4},{6,7},{7,6},{8,9},{9,8},{10,11... | collective-permute-start | bytes 393224 | tf_op jit(solution)/shard_map/ppermute | solution.py:224
  8.5 2.9 %collective-permute-start.1 = (bf16[512,128]{1,0:T(8,128)(2,1)}, bf16[512,128]{1,0:T(8,128)(2,1)S(1)}, u32[]{:S(2)}, u32[]{:S(2)}) collective-permute-start(bf16[512,128]{1,0:T(8,128)(2,1)} %e_ref.1), channel_id=1, source_target_pairs={{0,4},{1,5},{2,6},{3,7},{4,0},{5,1},{6,2},{7,3},{8,12},{9,13},{10,... | collective-permute-start | bytes 393224 | tf_op jit(solution)/shard_map/ppermute | solution.py:224
  12.2 3.1 %collective-permute-start.2 = (bf16[512,128]{1,0:T(8,128)(2,1)S(1)}, bf16[512,128]{1,0:T(8,128)(2,1)S(1)}, u32[]{:S(2)}, u32[]{:S(2)}) collective-permute-start(bf16[512,128]{1,0:T(8,128)(2,1)S(1)} %collective-permute-done.refs_1_), channel_id=1, source_target_pairs={{0,4},{1,5},{2,6},{3,7},{4,0},{5,1},{6,2},{7,3},{8,12},{9,13},{10,... | collective-permute-start | bytes 393224 | tf_op jit(solution)/shard_map/ppermute | solution.py:224
  20.0 3.2 %collective-permute-done.4.refs_5_ = bf16[512,128]{1,0:T(8,128)(2,1)S(1)} collective-permute-done((bf16[512,128]{1,0:T(8,128)(2,1)S(1)}, bf16[512,128]{1,0:T(8,128)(2,1)S(1)}, u32[]{:S(2)}, u32[]{:S(2)}) %collective-permute-start.4) | collective-permute-done | bytes 131104 | tf_op jit(solution)/shard_map/ppermute | solution.py:224
  28.6 2.5 %collective-permute-start.8 = (bf16[16,1024]{1,0:T(8,128)(2,1)S(1)}, bf16[16,1024]{1,0:T(8,128)(2,1)S(1)}, u32[]{:S(2)}, u32[]{:S(2)}) collective-permute-start(bf16[16,1024]{1,0:T(8,128)(2,1)S(1)} %get-tuple-element.37), channel_id=1, source_target_pairs={{0,32},{8,40},{16,48},{24,56},{32,0},{40,8},{48,16},{56,24},{64,96... | collective-permute-start | bytes 98312 | tf_op jit(solution)/shard_map/ppermute | solution.py:44
  31.2 1.9 %collective-permute-done.8.f1 = bf16[16,1024]{1,0:T(8,128)(2,1)S(1)} collective-permute-done((bf16[16,1024]{1,0:T(8,128)(2,1)S(1)}, bf16[16,1024]{1,0:T(8,128)(2,1)S(1)}, u32[]{:S(2)}, u32[]{:S(2)}) %collective-permute-start.8) | collective-permute-done | bytes 32800 | tf_op jit(solution)/shard_map/ppermute | solution.py:44
  33.1 1.9 %collective-permute-done.9.f2 = bf16[16,1024]{1,0:T(8,128)(2,1)S(1)} collective-permute-done((bf16[16,1024]{1,0:T(8,128)(2,1)S(1)}, bf16[16,1024]{1,0:T(8,128)(2,1)S(1)}, u32[]{:S(2)}, u32[]{:S(2)}) %collective-permute-start.9) | collective-permute-done | bytes 32800 | tf_op jit(solution)/shard_map/ppermute | solution.py:44
  35.0 1.6 %shard_map.53.a = f32[24,256]{1,0:T(8,128)S(1)} custom-call(bf16[4,16,512]{2,1,0:T(8,128)(2,1)S(1)} %get-tuple-element.33.keep_ref.k, bf16[4,16,512]{2,1,0:T(8,128)(2,1)S(1)} %collective-permute-done.7.recv_ref.r, bf16[16,1024]{1,0:T(8,128)(2,1)S(1)} %collective-permute-done.8.f1, bf16[16,1024]{1,0:T(8,128)(2,1)S(1)} %collective-permute-done.9.f2, ...), custom_call_target="tpu_custom_call" | custom-call | tf_op jit(solution)/shard_map/pallas_call | solution.py:290
  36.6 1.7 %collective-permute-start.11 = (f32[24,256]{1,0:T(8,128)S(1)}, f32[24,256]{1,0:T(8,128)S(1)}, u32[]{:S(2)}, u32[]{:S(2)}) collective-permute-start(f32[24,256]{1,0:T(8,128)S(1)} %shard_map.53.a), channel_id=1, source_target_pairs={{0,192},{8,200},{16,208},{24,216},{32,224},{40,232},{48,240},{56,2... | collective-permute-start | bytes 73736 | tf_op jit(solution)/shard_map/ppermute | solution.py:44
  42.2 1.8 %shard_map.54 = (f32[16,256]{1,0:T(8,128)S(1)}, bf16[4,256,1024]{2,1,0:T(8,128)(2,1)S(1)}, f32[24,256]{1,0:T(8,128)S(1)}) custom-call(bf16[4,16,512]{2,1,0:T(8,128)(2,1)S(1)} %get-tuple-element.33.keep_ref.k, bf16[4,16,512]{2,1,0:T(8,128)(2,1)S(1)} %collective-permute-done.7.recv_ref.r, bf16[16,1024]{1,0:T(8,128)(2,1)S(1)} %collective-permute-done.8.f1, ...), custom_call_target="tpu_custom_call" | custom-call | tf_op jit(solution)/shard_map/pallas_call | solution.py:291
  44.0 2.2 %collective-permute-start.14 = (f32[24,256]{1,0:T(8,128)S(1)}, f32[24,256]{1,0:T(8,128)S(1)}, u32[]{:S(2)}, u32[]{:S(2)}) collective-permute-start(f32[24,256]{1,0:T(8,128)S(1)} %get-tuple-element.42.a), channel_id=1, source_target_pairs={{0,192},{8,200},{16,208},{24,216},{32,224},{40,232},{48,240},{56,2... | collective-permute-start | bytes 73736 | tf_op jit(solution)/shard_map/ppermute | solution.py:44
  52.8 1.6 %collective-permute-done.17.x1 = bf16[16,1024]{1,0:T(8,128)(2,1)S(1)} collective-permute-done((bf16[16,1024]{1,0:T(8,128)(2,1)S(1)}, bf16[16,1024]{1,0:T(8,128)(2,1)S(1)}, u32[]{:S(2)}, u32[]{:S(2)}) %collective-permute-start.17) | collective-permute-done | bytes 32800 | tf_op jit(solution)/shard_map/ppermute | solution.py:44
  56.6 1.9 %collective-permute-start.22 = (f32[16,1024]{1,0:T(8,128)S(1)}, f32[16,1024]{1,0:T(8,128)S(1)}, u32[]{:S(2)}, u32[]{:S(2)}) collective-permute-start(f32[16,1024]{1,0:T(8,128)S(1)} %get-tuple-element.52), channel_id=1, source_target_pairs={{0,48},{8,56},{16,32},{24,40},{32,16},{40,24},{48,0},{56,8},{64,11... | collective-permute-start | bytes 196616 | tf_op jit(solution)/shard_map/ppermute | solution.py:44
  58.5 2.0 %collective-permute-done.21 = f32[16,1024]{1,0:T(8,128)S(1)} collective-permute-done((f32[16,1024]{1,0:T(8,128)S(1)}, f32[16,1024]{1,0:T(8,128)S(1)}, u32[]{:S(2)}, u32[]{:S(2)}) %collective-permute-start.21) | collective-permute-done | bytes 65568 | tf_op jit(solution)/shard_map/ppermute | solution.py:44
  63.6 1.7 %collective-permute-start.26 = (f32[16,1024]{1,0:T(8,128)S(1)}, f32[16,1024]{1,0:T(8,128)S(1)}, u32[]{:S(2)}, u32[]{:S(2)}) collective-permute-start(f32[16,1024]{1,0:T(8,128)S(1)} %add_add_fusion.a), channel_id=1, source_target_pairs={{0,64},{8,72},{16,80},{24,88},{32,96},{40,104},{48,112},{56,120},{... | collective-permute-start | bytes 196616 | tf_op jit(solution)/shard_map/ppermute | solution.py:44
  65.3 1.7 %collective-permute-done.24.b = f32[16,1024]{1,0:T(8,128)S(1)} collective-permute-done((f32[16,1024]{1,0:T(8,128)S(1)}, f32[16,1024]{1,0:T(8,128)S(1)}, u32[]{:S(2)}, u32[]{:S(2)}) %collective-permute-start.24) | collective-permute-done | bytes 65568 | tf_op jit(solution)/shard_map/ppermute | solution.py:44
  68.9 2.2 %collective-permute-start.28 = (f32[16,1280]{1,0:T(8,128)S(1)}, f32[16,1280]{1,0:T(8,128)S(1)}, u32[]{:S(2)}, u32[]{:S(2)}) collective-permute-start(f32[16,1280]{1,0:T(8,128)S(1)} %shard_map.57.x0), channel_id=1, source_target_pairs={{0,48},{8,56},{16,32},{24,40},{32,16},{40,24},{48,0},{56,8},{64,11... | collective-permute-start | bytes 245768 | tf_op jit(solution)/shard_map/ppermute | solution.py:44
  71.2 2.2 %collective-permute-done.27.x1 = f32[16,1280]{1,0:T(8,128)S(1)} collective-permute-done((f32[16,1280]{1,0:T(8,128)S(1)}, f32[16,1280]{1,0:T(8,128)S(1)}, u32[]{:S(2)}, u32[]{:S(2)}) %collective-permute-start.27) | collective-permute-done | bytes 81952 | tf_op jit(solution)/shard_map/ppermute | solution.py:44
  75.1 3.3 %collective-permute-start.34 = (bf16[64,1024]{1,0:T(8,128)(2,1)S(1)}, bf16[64,1024]{1,0:T(8,128)(2,1)S(1)}, u32[]{:S(2)}, u32[]{:S(2)}) collective-permute-start(bf16[64,1024]{1,0:T(8,128)(2,1)S(1)} %get-tuple-element.55.refs_0_), channel_id=1, source_target_pairs={{0,193},{1,192},{2,195},{3,194},{4,197},{5,196},{6,199},{7,198},{8... | collective-permute-start | bytes 393224 | tf_op jit(solution)/shard_map/ppermute | solution.py:237
  78.4 1.8 %collective-permute-start.30 = (bf16[64,1024]{1,0:T(8,128)(2,1)S(1)}, bf16[64,1024]{1,0:T(8,128)(2,1)S(1)}, u32[]{:S(2)}, u32[]{:S(2)}) collective-permute-start(bf16[64,1024]{1,0:T(8,128)(2,1)S(1)} %get-tuple-element.55.refs_0_), channel_id=1, source_target_pairs={{0,4},{1,5},{2,6},{3,7},{4,0},{5,1},{6,2},{7,3},{8,12},{9,13},{10,... | collective-permute-start | bytes 393224 | tf_op jit(solution)/shard_map/ppermute | solution.py:224
  81.5 2.6 %collective-permute-start.35 = (bf16[64,1024]{1,0:T(8,128)(2,1)S(1)}, bf16[64,1024]{1,0:T(8,128)(2,1)S(1)}, u32[]{:S(2)}, u32[]{:S(2)}) collective-permute-start(bf16[64,1024]{1,0:T(8,128)(2,1)S(1)} %collective-permute-done.34.refs_0_), channel_id=1, source_target_pairs={{0,4},{1,5},{2,6},{3,7},{4,0},{5,1},{6,2},{7,3},{8,12},{9,13},{10,... | collective-permute-start | bytes 393224 | tf_op jit(solution)/shard_map/ppermute | solution.py:224
  85.4 13.5 %collective-permute-start.33 = (bf16[4,64,1024]{2,1,0:T(8,128)(2,1)S(1)}, bf16[4,64,1024]{2,1,0:T(8,128)(2,1)S(1)}, u32[]{:S(2)}, u32[]{:S(2)}) collective-permute-start(bf16[4,64,1024]{2,1,0:T(8,128)(2,1)S(1)} %shard_map.59.c0), channel_id=1, source_target_pairs={{0,8},{8,0},{16,24},{24,16},{32,40},{40,32},{48,56},{56,48},{64,72... | collective-permute-start | bytes 1572872 | tf_op jit(solution)/shard_map/ppermute | solution.py:44
  99.0 4.7 %collective-permute-start.38 = (bf16[4,64,1024]{2,1,0:T(8,128)(2,1)S(1)}, bf16[4,64,1024]{2,1,0:T(8,128)(2,1)S(1)}, u32[]{:S(2)}, u32[]{:S(2)}) collective-permute-start(bf16[4,64,1024]{2,1,0:T(8,128)(2,1)S(1)} %shard_map.60.c2), channel_id=1, source_target_pairs={{0,8},{8,0},{16,24},{24,16},{32,40},{40,32},{48,56},{56,48},{64,72... | collective-permute-start | bytes 1572872 | tf_op jit(solution)/shard_map/ppermute | solution.py:44
  105.3 11.5 %shard_map.61 = (f32[32,64]{1,0:T(8,128)S(1)}, f32[32,64]{1,0:T(8,128)S(1)}, f32[8,16,256]{2,1,0:T(8,128)}) custom-call(s32[4]{0:T(128)S(1)} %pad_add_fusion.place_ref, bf16[4,64,1024]{2,1,0:T(8,128)(2,1)S(1)} %shard_map.59.c0, bf16[4,64,1024]{2,1,0:T(8,128)(2,1)S(1)} %collective-permute-done.33.c1, bf16[4,64,1024]{2,1,0:T(8,128)(2,1)S(1)} %shard_map.60.c2, ...), custom_call_target="tpu_custom_call" | custom-call | tf_op jit(solution)/shard_map/pallas_call | solution.py:312
  (80 shorter events, 36.8 us)
Async XLA Ops:
  0.6 11.5 %collective-permute-start = (bf16[512,128]{1,0:T(8,128)(2,1)}, bf16[512,128]{1,0:T(8,128)(2,1)S(1)}, u32[]{:S(2)}, u32[]{:S(2)}) collective-permute-start(bf16[512,128]{1,0:T(8,128)(2,1)} %e_ref.1), channel_id=1, source_target_pairs={{0,1},{1,0},{2,3},{3,2},{4,5},{5,4},{6,7},{7,6},{8,9},{9,8},{10,11... | collective-permute-start | bytes 393224 | tf_op jit(solution)/shard_map/ppermute | solution.py:224
  8.5 7.6 %collective-permute-start.1 = (bf16[512,128]{1,0:T(8,128)(2,1)}, bf16[512,128]{1,0:T(8,128)(2,1)S(1)}, u32[]{:S(2)}, u32[]{:S(2)}) collective-permute-start(bf16[512,128]{1,0:T(8,128)(2,1)} %e_ref.1), channel_id=1, source_target_pairs={{0,4},{1,5},{2,6},{3,7},{4,0},{5,1},{6,2},{7,3},{8,12},{9,13},{10,... | collective-permute-start | bytes 393224 | tf_op jit(solution)/shard_map/ppermute | solution.py:224
  11.4 8.2 %collective-permute-start.3 = (bf16[512,128]{1,0:T(8,128)(2,1)}, bf16[512,128]{1,0:T(8,128)(2,1)S(1)}, u32[]{:S(2)}, u32[]{:S(2)}) collective-permute-start(bf16[512,128]{1,0:T(8,128)(2,1)} %e_ref.1), channel_id=1, source_target_pairs={{0,6},{1,7},{2,4},{3,5},{4,2},{5,3},{6,0},{7,1},{8,14},{9,15},{10,... | collective-permute-start | bytes 393224 | tf_op jit(solution)/shard_map/ppermute | solution.py:224
  12.1 7.4 %collective-permute-start.5 = (bf16[512,128]{1,0:T(8,128)(2,1)}, bf16[512,128]{1,0:T(8,128)(2,1)S(1)}, u32[]{:S(2)}, u32[]{:S(2)}) collective-permute-start(bf16[512,128]{1,0:T(8,128)(2,1)} %e_ref.1), channel_id=1, source_target_pairs={{0,2},{1,3},{2,0},{3,1},{4,6},{5,7},{6,4},{7,5},{8,10},{9,11},{10,... | collective-permute-start | bytes 393224 | tf_op jit(solution)/shard_map/ppermute | solution.py:224
  12.2 7.8 %collective-permute-start.2 = (bf16[512,128]{1,0:T(8,128)(2,1)S(1)}, bf16[512,128]{1,0:T(8,128)(2,1)S(1)}, u32[]{:S(2)}, u32[]{:S(2)}) collective-permute-start(bf16[512,128]{1,0:T(8,128)(2,1)S(1)} %collective-permute-done.refs_1_), channel_id=1, source_target_pairs={{0,4},{1,5},{2,6},{3,7},{4,0},{5,1},{6,2},{7,3},{8,12},{9,13},{10,... | collective-permute-start | bytes 393224 | tf_op jit(solution)/shard_map/ppermute | solution.py:224
  15.2 7.9 %collective-permute-start.4 = (bf16[512,128]{1,0:T(8,128)(2,1)S(1)}, bf16[512,128]{1,0:T(8,128)(2,1)S(1)}, u32[]{:S(2)}, u32[]{:S(2)}) collective-permute-start(bf16[512,128]{1,0:T(8,128)(2,1)S(1)} %collective-permute-done.refs_1_), channel_id=1, source_target_pairs={{0,6},{1,7},{2,4},{3,5},{4,2},{5,3},{6,0},{7,1},{8,14},{9,15},{10,... | collective-permute-start | bytes 393224 | tf_op jit(solution)/shard_map/ppermute | solution.py:224
  16.0 7.4 %collective-permute-start.6 = (bf16[512,128]{1,0:T(8,128)(2,1)S(1)}, bf16[512,128]{1,0:T(8,128)(2,1)S(1)}, u32[]{:S(2)}, u32[]{:S(2)}) collective-permute-start(bf16[512,128]{1,0:T(8,128)(2,1)S(1)} %collective-permute-done.refs_1_), channel_id=1, source_target_pairs={{0,2},{1,3},{2,0},{3,1},{4,6},{5,7},{6,4},{7,5},{8,10},{9,11},{10,... | collective-permute-start | bytes 393224 | tf_op jit(solution)/shard_map/ppermute | solution.py:224
  26.9 27.8 %collective-permute-start.20 = (bf16[512,1024]{1,0:T(8,128)(2,1)S(1)}, bf16[512,1024]{1,0:T(8,128)(2,1)S(1)}, u32[]{:S(2)}, u32[]{:S(2)}) collective-permute-start(bf16[512,1024]{1,0:T(8,128)(2,1)S(1)} %get-tuple-element.49.own_ref), channel_id=1, source_target_pairs={{0,8},{8,0},{16,24},{24,16},{32,40},{40,32},{48,56},{56,48},{64,72... | collective-permute-start | bytes 3145736 | tf_op jit(solution)/shard_map/ppermute | solution.py:44
  44.0 4.7 %collective-permute-start.14 = (f32[24,256]{1,0:T(8,128)S(1)}, f32[24,256]{1,0:T(8,128)S(1)}, u32[]{:S(2)}, u32[]{:S(2)}) collective-permute-start(f32[24,256]{1,0:T(8,128)S(1)} %get-tuple-element.42.a), channel_id=1, source_target_pairs={{0,192},{8,200},{16,208},{24,216},{32,224},{40,232},{48,240},{56,2... | collective-permute-start | bytes 73736 | tf_op jit(solution)/shard_map/ppermute | solution.py:44
  55.2 5.3 %collective-permute-start.21 = (f32[16,1024]{1,0:T(8,128)S(1)}, f32[16,1024]{1,0:T(8,128)S(1)}, u32[]{:S(2)}, u32[]{:S(2)}) collective-permute-start(f32[16,1024]{1,0:T(8,128)S(1)} %get-tuple-element.51), channel_id=1, source_target_pairs={{0,32},{8,40},{16,48},{24,56},{32,0},{40,8},{48,16},{56,24},{64,96... | collective-permute-start | bytes 196616 | tf_op jit(solution)/shard_map/ppermute | solution.py:44
  56.6 4.7 %collective-permute-start.22 = (f32[16,1024]{1,0:T(8,128)S(1)}, f32[16,1024]{1,0:T(8,128)S(1)}, u32[]{:S(2)}, u32[]{:S(2)}) collective-permute-start(f32[16,1024]{1,0:T(8,128)S(1)} %get-tuple-element.52), channel_id=1, source_target_pairs={{0,48},{8,56},{16,32},{24,40},{32,16},{40,24},{48,0},{56,8},{64,11... | collective-permute-start | bytes 196616 | tf_op jit(solution)/shard_map/ppermute | solution.py:44
  61.6 5.3 %collective-permute-start.24 = (f32[16,1024]{1,0:T(8,128)S(1)}, f32[16,1024]{1,0:T(8,128)S(1)}, u32[]{:S(2)}, u32[]{:S(2)}) collective-permute-start(f32[16,1024]{1,0:T(8,128)S(1)} %add_add_fusion.a), channel_id=1, source_target_pairs={{0,192},{8,200},{16,208},{24,216},{32,224},{40,232},{48,240},{56,2... | collective-permute-start | bytes 196616 | tf_op jit(solution)/shard_map/ppermute | solution.py:44
  63.2 5.2 %collective-permute-start.25 = (f32[16,1024]{1,0:T(8,128)S(1)}, f32[16,1024]{1,0:T(8,128)S(1)}, u32[]{:S(2)}, u32[]{:S(2)}) collective-permute-start(f32[16,1024]{1,0:T(8,128)S(1)} %add_add_fusion.a), channel_id=1, source_target_pairs={{0,128},{8,136},{16,144},{24,152},{32,160},{40,168},{48,176},{56,1... | collective-permute-start | bytes 196616 | tf_op jit(solution)/shard_map/ppermute | solution.py:44
  63.6 4.8 %collective-permute-start.26 = (f32[16,1024]{1,0:T(8,128)S(1)}, f32[16,1024]{1,0:T(8,128)S(1)}, u32[]{:S(2)}, u32[]{:S(2)}) collective-permute-start(f32[16,1024]{1,0:T(8,128)S(1)} %add_add_fusion.a), channel_id=1, source_target_pairs={{0,64},{8,72},{16,80},{24,88},{32,96},{40,104},{48,112},{56,120},{... | collective-permute-start | bytes 196616 | tf_op jit(solution)/shard_map/ppermute | solution.py:44
  68.4 5.0 %collective-permute-start.27 = (f32[16,1280]{1,0:T(8,128)S(1)}, f32[16,1280]{1,0:T(8,128)S(1)}, u32[]{:S(2)}, u32[]{:S(2)}) collective-permute-start(f32[16,1280]{1,0:T(8,128)S(1)} %shard_map.57.x0), channel_id=1, source_target_pairs={{0,32},{8,40},{16,48},{24,56},{32,0},{40,8},{48,16},{56,24},{64,96... | collective-permute-start | bytes 245768 | tf_op jit(solution)/shard_map/ppermute | solution.py:44
  68.9 5.2 %collective-permute-start.28 = (f32[16,1280]{1,0:T(8,128)S(1)}, f32[16,1280]{1,0:T(8,128)S(1)}, u32[]{:S(2)}, u32[]{:S(2)}) collective-permute-start(f32[16,1280]{1,0:T(8,128)S(1)} %shard_map.57.x0), channel_id=1, source_target_pairs={{0,48},{8,56},{16,32},{24,40},{32,16},{40,24},{48,0},{56,8},{64,11... | collective-permute-start | bytes 245768 | tf_op jit(solution)/shard_map/ppermute | solution.py:44
  75.1 6.4 %collective-permute-start.34 = (bf16[64,1024]{1,0:T(8,128)(2,1)S(1)}, bf16[64,1024]{1,0:T(8,128)(2,1)S(1)}, u32[]{:S(2)}, u32[]{:S(2)}) collective-permute-start(bf16[64,1024]{1,0:T(8,128)(2,1)S(1)} %get-tuple-element.55.refs_0_), channel_id=1, source_target_pairs={{0,193},{1,192},{2,195},{3,194},{4,197},{5,196},{6,199},{7,198},{8... | collective-permute-start | bytes 393224 | tf_op jit(solution)/shard_map/ppermute | solution.py:237
  78.4 6.9 %collective-permute-start.30 = (bf16[64,1024]{1,0:T(8,128)(2,1)S(1)}, bf16[64,1024]{1,0:T(8,128)(2,1)S(1)}, u32[]{:S(2)}, u32[]{:S(2)}) collective-permute-start(bf16[64,1024]{1,0:T(8,128)(2,1)S(1)} %get-tuple-element.55.refs_0_), channel_id=1, source_target_pairs={{0,4},{1,5},{2,6},{3,7},{4,0},{5,1},{6,2},{7,3},{8,12},{9,13},{10,... | collective-permute-start | bytes 393224 | tf_op jit(solution)/shard_map/ppermute | solution.py:224
  80.2 5.2 %collective-permute-start.31 = (bf16[64,1024]{1,0:T(8,128)(2,1)S(1)}, bf16[64,1024]{1,0:T(8,128)(2,1)S(1)}, u32[]{:S(2)}, u32[]{:S(2)}) collective-permute-start(bf16[64,1024]{1,0:T(8,128)(2,1)S(1)} %get-tuple-element.55.refs_0_), channel_id=1, source_target_pairs={{0,6},{1,7},{2,4},{3,5},{4,2},{5,3},{6,0},{7,1},{8,14},{9,15},{10,... | collective-permute-start | bytes 393224 | tf_op jit(solution)/shard_map/ppermute | solution.py:224
  81.5 17.5 %collective-permute-start.35 = (bf16[64,1024]{1,0:T(8,128)(2,1)S(1)}, bf16[64,1024]{1,0:T(8,128)(2,1)S(1)}, u32[]{:S(2)}, u32[]{:S(2)}) collective-permute-start(bf16[64,1024]{1,0:T(8,128)(2,1)S(1)} %collective-permute-done.34.refs_0_), channel_id=1, source_target_pairs={{0,4},{1,5},{2,6},{3,7},{4,0},{5,1},{6,2},{7,3},{8,12},{9,13},{10,... | collective-permute-start | bytes 393224 | tf_op jit(solution)/shard_map/ppermute | solution.py:224
  84.1 14.9 %collective-permute-start.36 = (bf16[64,1024]{1,0:T(8,128)(2,1)S(1)}, bf16[64,1024]{1,0:T(8,128)(2,1)S(1)}, u32[]{:S(2)}, u32[]{:S(2)}) collective-permute-start(bf16[64,1024]{1,0:T(8,128)(2,1)S(1)} %collective-permute-done.34.refs_0_), channel_id=1, source_target_pairs={{0,6},{1,7},{2,4},{3,5},{4,2},{5,3},{6,0},{7,1},{8,14},{9,15},{10,... | collective-permute-start | bytes 393224 | tf_op jit(solution)/shard_map/ppermute | solution.py:224
  85.3 13.6 %collective-permute-start.37 = (bf16[64,1024]{1,0:T(8,128)(2,1)S(1)}, bf16[64,1024]{1,0:T(8,128)(2,1)S(1)}, u32[]{:S(2)}, u32[]{:S(2)}) collective-permute-start(bf16[64,1024]{1,0:T(8,128)(2,1)S(1)} %collective-permute-done.34.refs_0_), channel_id=1, source_target_pairs={{0,2},{1,3},{2,0},{3,1},{4,6},{5,7},{6,4},{7,5},{8,10},{9,11},{10,... | collective-permute-start | bytes 393224 | tf_op jit(solution)/shard_map/ppermute | solution.py:224
  85.4 19.9 %collective-permute-start.33 = (bf16[4,64,1024]{2,1,0:T(8,128)(2,1)S(1)}, bf16[4,64,1024]{2,1,0:T(8,128)(2,1)S(1)}, u32[]{:S(2)}, u32[]{:S(2)}) collective-permute-start(bf16[4,64,1024]{2,1,0:T(8,128)(2,1)S(1)} %shard_map.59.c0), channel_id=1, source_target_pairs={{0,8},{8,0},{16,24},{24,16},{32,40},{40,32},{48,56},{56,48},{64,72... | collective-permute-start | bytes 1572872 | tf_op jit(solution)/shard_map/ppermute | solution.py:44
  99.0 6.3 %collective-permute-start.38 = (bf16[4,64,1024]{2,1,0:T(8,128)(2,1)S(1)}, bf16[4,64,1024]{2,1,0:T(8,128)(2,1)S(1)}, u32[]{:S(2)}, u32[]{:S(2)}) collective-permute-start(bf16[4,64,1024]{2,1,0:T(8,128)(2,1)S(1)} %shard_map.60.c2), channel_id=1, source_target_pairs={{0,8},{8,0},{16,24},{24,16},{32,40},{40,32},{48,56},{56,48},{64,72... | collective-permute-start | bytes 1572872 | tf_op jit(solution)/shard_map/ppermute | solution.py:44
  (20 other events, 59.9 us)
